TPU v7x, 32 devices: a whole 2x2x4 slice. The times are simulated.
32 devices in a mesh: replica: 4 (over y, x), shard: 8 (over z, core).
Axes of the slice: x: 2, y: 2, z: 4, core: 2. Of those that a mesh axis runs over, the one named last changes fastest.
Arguments:
- hidden: bfloat16 [4, 1024, 1024], P('replica', 'shard'), may hold values from -6 to 6
- encoded: bfloat16 [4, 1024, 1024], P('replica', 'shard'), may hold values from -6 to 6
- cotangent: bfloat16 [4, 1024, 1024], P('replica', 'shard'), may hold values from -6 to 6
- norm_gain: bfloat16 [1024, 3], P('shard'), may hold values from 0.5 to 1.5
- norm_bias: bfloat16 [1024, 3], P('shard'), may hold values from -2 to 2
- attn_bias: bfloat16 [1024, 4], P('shard'), may hold values from -3 to 3
- out_bias: bfloat16 [1024, 3], P('shard'), may hold values from -2 to 2
- self_qkv: bfloat16 [1024, 3072], P('shard'), may hold values from -0.1875 to 0.1875
- self_out: bfloat16 [1024, 1024], P('shard'), may hold values from -3 to 3
- cross_q: bfloat16 [1024, 1024], P('shard'), may hold values from -0.1875 to 0.1875
- cross_kv: bfloat16 [1024, 2048], P('shard'), may hold values from -0.1875 to 0.1875
- cross_out: bfloat16 [1024, 1024], P('shard'), may hold values from -3 to 3
- ffn_in: bfloat16 [1024, 4096], P('shard'), may hold values from -0.1875 to 0.1875
- ffn_in_bias: bfloat16 [4096], P('shard'), may hold values from -3 to 3
- ffn_out: bfloat16 [4096, 1024], P('shard'), may hold values from -0.09375 to 0.09375
Outputs:
- output: bfloat16 [4, 1024, 1024], P('replica', 'shard')
- hidden_grad: float32 [4, 1024, 1024], P('replica', 'shard')
- encoded_grad: float32 [4, 1024, 1024], P('replica', 'shard')
- norm_gain_grad: float32 [1024, 3], P('shard')
- norm_bias_grad: float32 [1024, 3], P('shard')
- attn_bias_grad: float32 [1024, 4], P('shard')
- out_bias_grad: float32 [1024, 3], P('shard')
- self_qkv_grad: float32 [1024, 3072], P('shard')
- self_out_grad: float32 [1024, 1024], P('shard')
- cross_q_grad: float32 [1024, 1024], P('shard')
- cross_kv_grad: float32 [1024, 2048], P('shard')
- cross_out_grad: float32 [1024, 1024], P('shard')
- ffn_in_grad: float32 [1024, 4096], P('shard')
- ffn_in_bias_grad: float32 [4096], P('shard')
- ffn_out_grad: float32 [4096, 1024], P('shard')
All inputs are finite; a program needn't handle non-finite values.
Results may differ from a plain program's by a relative error of at most 0.025.
Values may be sent and summed in bfloat16 or wider, within the bound.
No kernel may reach another device: no remote copies, remote signals or barrier semaphores. Data moves between devices by JAX's collectives and lax.ppermute only.
A program may use at most 256 MiB of HBM per device.

v0:
```python
from functools import partial

import jax
import jax.numpy as jnp
from jax import lax
from jax.sharding import PartitionSpec as P

HEADS = 16
HEAD_DIM = 64


def product(left_side, right_side):
    return jnp.dot(left_side, right_side, preferred_element_type=jnp.float32)


def outer_sum(left_side, right_side):
    return lax.dot_general(
        left_side, right_side, (((0,), (0,)), ((), ())), preferred_element_type=jnp.float32
    )


def back_product(left_side, right_side):
    return lax.dot_general(
        left_side, right_side, (((1,), (1,)), ((), ())), preferred_element_type=jnp.float32
    )


def layer_norm(values_in, norm_scale, norm_shift):
    average = jnp.mean(values_in, axis=-1, keepdims=True)
    centred = values_in - average
    variance = jnp.mean(centred * centred, axis=-1, keepdims=True)
    inverse = lax.rsqrt(variance + 1e-05)
    normed = centred * inverse
    return (normed * norm_scale + norm_shift, normed, inverse)


def norm_backward(grad_out, normed, inverse, norm_scale):
    scale_grad = jnp.sum(grad_out * normed, axis=0)
    shift_grad = jnp.sum(grad_out, axis=0)
    scaled = grad_out * norm_scale
    projected = (
        scaled
        - jnp.mean(scaled, axis=-1, keepdims=True)
        - normed * jnp.mean(scaled * normed, axis=-1, keepdims=True)
    )
    return (inverse * projected, scale_grad, shift_grad)


def head_layout():
    group_heads = min(HEADS, 4)
    return (group_heads, HEADS // group_heads, group_heads * HEAD_DIM)


def rejoin(stacked):
    return stacked.transpose(1, 0, 2).reshape(stacked.shape[1], stacked.shape[0] * stacked.shape[2])


def group_scores(query_part, key_part, query_start, causal):
    scores = jnp.einsum(
        "qhd,khd->hqk", query_part, key_part, preferred_element_type=jnp.float32
    ) * HEAD_DIM ** (-0.5)
    if causal:
        positions = query_start + jnp.arange(query_part.shape[0], dtype=jnp.int32)
        key_places = jnp.arange(key_part.shape[0], dtype=jnp.int32)
        allowed = positions[:, None] >= key_places[None, :]
        scores = jnp.where(allowed[None], scores, -1e30)
    return scores


def head_slice(values_in, column, rows):
    group_heads, group_count, group_width = head_layout()
    return lax.dynamic_slice_in_dim(values_in, column, group_width, 1).reshape(
        rows, group_heads, HEAD_DIM
    )


def attend(queries, keys_all, values_all, row_start, causal):
    local_rows = queries.shape[0]
    key_rows = keys_all.shape[0]
    group_heads, group_count, group_width = head_layout()

    def one_group(group_index):
        column = group_index * group_width
        query_part = head_slice(queries, column, local_rows)
        key_part = head_slice(keys_all, column, key_rows)
        value_part = head_slice(values_all, column, key_rows)
        scores = group_scores(query_part, key_part, row_start, causal)
        row_max = jnp.max(scores, axis=-1, keepdims=True)
        weights = jnp.exp(scores - row_max)
        totals = jnp.sum(weights, axis=-1, keepdims=True)
        probabilities = (weights / totals).astype(jnp.bfloat16)
        context = jnp.einsum(
            "hqk,khd->qhd", probabilities, value_part, preferred_element_type=jnp.float32
        )
        return (context.reshape(local_rows, group_width), row_max[..., 0] + jnp.log(totals[..., 0]))

    contexts, log_totals = lax.map(one_group, jnp.arange(group_count, dtype=jnp.int32))
    return (rejoin(contexts), log_totals)


def attend_back(queries, keys_all, values_all, grad_context, log_totals, row_start, causal):
    local_rows = queries.shape[0]
    key_rows = keys_all.shape[0]
    group_heads, group_count, group_width = head_layout()

    def one_group(group_input):
        group_index, group_totals = group_input
        column = group_index * group_width
        query_part = head_slice(queries, column, local_rows)
        key_part = head_slice(keys_all, column, key_rows)
        value_part = head_slice(values_all, column, key_rows)
        grad_part = head_slice(grad_context, column, local_rows)
        scores = group_scores(query_part, key_part, row_start, causal)
        probabilities = jnp.exp(scores - group_totals[..., None])
        prob_grad = jnp.einsum(
            "qhd,khd->hqk", grad_part, value_part, preferred_element_type=jnp.float32
        )
        row_inner = jnp.sum(prob_grad * probabilities, axis=-1, keepdims=True)
        score_grad = (probabilities * (prob_grad - row_inner)).astype(jnp.bfloat16)
        query_grad = jnp.einsum(
            "hqk,khd->qhd", score_grad, key_part, preferred_element_type=jnp.float32
        ) * HEAD_DIM ** (-0.5)
        prob_low = probabilities.astype(jnp.bfloat16)
        value_grad = jnp.einsum(
            "hqk,qhd->khd", prob_low, grad_part, preferred_element_type=jnp.float32
        )
        key_grad = jnp.einsum(
            "hqk,qhd->khd", score_grad, query_part, preferred_element_type=jnp.float32
        ) * HEAD_DIM ** (-0.5)
        return (
            query_grad.reshape(local_rows, group_width),
            key_grad.reshape(key_rows, group_width),
            value_grad.reshape(key_rows, group_width),
            row_inner[..., 0],
        )

    results = lax.map(one_group, (jnp.arange(group_count, dtype=jnp.int32), log_totals))
    return (rejoin(results[0]), rejoin(results[1]), rejoin(results[2]), results[3])


def on_device(
    hidden,
    encoded,
    cotangent,
    norm_gain,
    norm_bias,
    attn_bias,
    out_bias,
    self_qkv,
    self_out,
    cross_q,
    cross_kv,
    cross_out,
    ffn_in,
    ffn_in_bias,
    ffn_out,
):
    state_rows = hidden[0].astype(jnp.float32)
    memory = encoded[0]
    seed_grad = cotangent[0].astype(jnp.float32)
    local_rows = state_rows.shape[0]
    model_width = state_rows.shape[1]
    row_start = lax.axis_index("shard") * local_rows
    self_set = (
        lax.all_gather(self_qkv, "shard", axis=0, tiled=True),
        lax.all_gather(self_out, "shard", axis=0, tiled=True),
        lax.all_gather(norm_gain, "shard", axis=0, tiled=True),
        lax.all_gather(norm_bias, "shard", axis=0, tiled=True),
        lax.all_gather(attn_bias, "shard", axis=0, tiled=True),
        lax.all_gather(out_bias, "shard", axis=0, tiled=True),
    )
    qkv_weight = self_set[0]
    self_projection = self_set[1]
    norm_gains = self_set[2].astype(jnp.float32)
    norm_shifts = self_set[3].astype(jnp.float32)
    pair_biases = self_set[4].astype(jnp.float32)
    branch_biases = self_set[5].astype(jnp.float32)
    normed_out, normed_one, inverse_one = layer_norm(
        state_rows, norm_gains[:, 0], norm_shifts[:, 0]
    )
    input_one = normed_out.astype(jnp.bfloat16)
    joined = product(input_one, qkv_weight)
    queries_one = (joined[:, :model_width] + pair_biases[:, 0]).astype(jnp.bfloat16)
    keys_local = joined[:, model_width : 2 * model_width].astype(jnp.bfloat16)
    values_local = (joined[:, 2 * model_width :] + pair_biases[:, 1]).astype(jnp.bfloat16)
    keys_one, values_one = (
        lax.all_gather(keys_local, "shard", axis=0, tiled=True),
        lax.all_gather(values_local, "shard", axis=0, tiled=True),
    )
    context_one, totals_one = attend(queries_one, keys_one, values_one, row_start, True)
    context_low_one = context_one.astype(jnp.bfloat16)
    first = state_rows + (product(context_low_one, self_projection) + branch_biases[:, 0])
    cross_set = (
        lax.all_gather(cross_q, "shard", axis=0, tiled=True),
        lax.all_gather(cross_kv, "shard", axis=0, tiled=True),
        lax.all_gather(cross_out, "shard", axis=0, tiled=True),
    )
    cross_query_weight = cross_set[0]
    cross_pair_weight = cross_set[1]
    cross_projection = cross_set[2]
    normed_out, normed_two, inverse_two = layer_norm(first, norm_gains[:, 1], norm_shifts[:, 1])
    input_two = normed_out.astype(jnp.bfloat16)
    queries_two = (product(input_two, cross_query_weight) + pair_biases[:, 2]).astype(jnp.bfloat16)
    memory_pair = product(memory, cross_pair_weight)
    memory_keys = memory_pair[:, :model_width].astype(jnp.bfloat16)
    memory_values = (memory_pair[:, model_width:] + pair_biases[:, 3]).astype(jnp.bfloat16)
    keys_two, values_two = (
        lax.all_gather(memory_keys, "shard", axis=0, tiled=True),
        lax.all_gather(memory_values, "shard", axis=0, tiled=True),
    )
    context_two, totals_two = attend(queries_two, keys_two, values_two, row_start, False)
    context_low_two = context_two.astype(jnp.bfloat16)
    second = first + (product(context_low_two, cross_projection) + branch_biases[:, 1])
    ffn_set = (
        lax.all_gather(ffn_in, "shard", axis=0, tiled=True),
        lax.all_gather(ffn_out, "shard", axis=0, tiled=True),
        lax.all_gather(ffn_in_bias, "shard", axis=0, tiled=True),
    )
    ffn_up = ffn_set[0]
    ffn_down = ffn_set[1]
    ffn_shift = ffn_set[2].astype(jnp.float32)
    normed_out, normed_three, inverse_three = layer_norm(
        second, norm_gains[:, 2], norm_shifts[:, 2]
    )
    input_three = normed_out.astype(jnp.bfloat16)
    hidden_pre = product(input_three, ffn_up) + ffn_shift
    activated = jax.nn.gelu(hidden_pre, approximate=False).astype(jnp.bfloat16)
    output = (second + (product(activated, ffn_down) + branch_biases[:, 2])).astype(jnp.bfloat16)
    again = (
        lax.all_gather(self_qkv, "shard", axis=0, tiled=True),
        lax.all_gather(self_out, "shard", axis=0, tiled=True),
        lax.all_gather(norm_gain, "shard", axis=0, tiled=True),
        lax.all_gather(cross_q, "shard", axis=0, tiled=True),
        lax.all_gather(cross_kv, "shard", axis=0, tiled=True),
        lax.all_gather(cross_out, "shard", axis=0, tiled=True),
        lax.all_gather(ffn_in, "shard", axis=0, tiled=True),
        lax.all_gather(ffn_out, "shard", axis=0, tiled=True),
    )
    qkv_weight = again[0]
    self_projection = again[1]
    norm_gains = again[2].astype(jnp.float32)
    cross_query_weight = again[3]
    cross_pair_weight = again[4]
    cross_projection = again[5]
    ffn_up = again[6]
    ffn_down = again[7]
    grad_three = cotangent[0]
    out_shift_three = jnp.sum(seed_grad, axis=0)
    ffn_out_grad = outer_sum(activated, grad_three)
    act_grad = back_product(grad_three, ffn_down)
    _, gelu_back = jax.vjp(partial(jax.nn.gelu, approximate=False), hidden_pre)
    pre_low = gelu_back(act_grad)[0].astype(jnp.bfloat16)
    ffn_in_bias_grad = jnp.sum(pre_low.astype(jnp.float32), axis=0)
    ffn_in_grad = outer_sum(input_three, pre_low)
    lifted, scale_three, shift_three = norm_backward(
        back_product(pre_low, ffn_up), normed_three, inverse_three, norm_gains[:, 2]
    )
    grad_second = seed_grad + lifted
    grad_two_low = grad_second.astype(jnp.bfloat16)
    out_shift_two = jnp.sum(grad_two_low.astype(jnp.float32), axis=0)
    cross_out_grad = outer_sum(context_low_two, grad_two_low)
    context_grad_two = back_product(grad_two_low, cross_projection).astype(jnp.bfloat16)
    query_part_two, key_part_two, value_part_two, inner_two = attend_back(
        queries_two, keys_two, values_two, context_grad_two, totals_two, row_start, False
    )
    key_sum_two, value_sum_two = (
        lax.psum_scatter(
            key_part_two.astype(jnp.bfloat16), "shard", scatter_dimension=0, tiled=True
        ).astype(jnp.float32),
        lax.psum_scatter(
            value_part_two.astype(jnp.bfloat16), "shard", scatter_dimension=0, tiled=True
        ).astype(jnp.float32),
    )
    query_low_two = query_part_two.astype(jnp.bfloat16)
    memory_grad_low = jnp.concatenate(
        [key_sum_two.astype(jnp.bfloat16), value_sum_two.astype(jnp.bfloat16)], axis=1
    )
    query_shift_two = jnp.sum(query_low_two.astype(jnp.float32), axis=0)
    value_shift_two = jnp.sum(memory_grad_low[:, model_width:].astype(jnp.float32), axis=0)
    cross_q_grad = outer_sum(input_two, query_low_two)
    cross_kv_grad = outer_sum(memory, memory_grad_low)
    encoded_grad = back_product(memory_grad_low, cross_pair_weight)
    lifted, scale_two, shift_two = norm_backward(
        back_product(query_low_two, cross_query_weight), normed_two, inverse_two, norm_gains[:, 1]
    )
    grad_first = grad_second + lifted
    grad_one_low = grad_first.astype(jnp.bfloat16)
    out_shift_one = jnp.sum(grad_one_low.astype(jnp.float32), axis=0)
    self_out_grad = outer_sum(context_low_one, grad_one_low)
    context_grad_one = back_product(grad_one_low, self_projection).astype(jnp.bfloat16)
    query_part_one, key_part_one, value_part_one, inner_one = attend_back(
        queries_one, keys_one, values_one, context_grad_one, totals_one, row_start, True
    )
    key_sum_one, value_sum_one = (
        lax.psum_scatter(
            key_part_one.astype(jnp.bfloat16), "shard", scatter_dimension=0, tiled=True
        ).astype(jnp.float32),
        lax.psum_scatter(
            value_part_one.astype(jnp.bfloat16), "shard", scatter_dimension=0, tiled=True
        ).astype(jnp.float32),
    )
    qkv_grad_low = jnp.concatenate(
        [
            query_part_one.astype(jnp.bfloat16),
            key_sum_one.astype(jnp.bfloat16),
            value_sum_one.astype(jnp.bfloat16),
        ],
        axis=1,
    )
    query_shift_one = jnp.sum(qkv_grad_low[:, :model_width].astype(jnp.float32), axis=0)
    value_shift_one = jnp.sum(qkv_grad_low[:, 2 * model_width :].astype(jnp.float32), axis=0)
    self_qkv_grad = outer_sum(input_one, qkv_grad_low)
    lifted, scale_one, shift_one = norm_backward(
        back_product(qkv_grad_low, qkv_weight), normed_one, inverse_one, norm_gains[:, 0]
    )
    hidden_grad = grad_first + lifted
    norm_gain_grad = jnp.stack([scale_one, scale_two, scale_three], axis=1)
    norm_bias_grad = jnp.stack([shift_one, shift_two, shift_three], axis=1)
    attn_bias_grad = jnp.stack(
        [query_shift_one, value_shift_one, query_shift_two, value_shift_two], axis=1
    )
    out_bias_grad = jnp.stack([out_shift_one, out_shift_two, out_shift_three], axis=1)
    owned = (
        lax.psum_scatter(
            norm_gain_grad.astype(jnp.bfloat16), "shard", scatter_dimension=0, tiled=True
        ).astype(jnp.float32),
        lax.psum_scatter(
            norm_bias_grad.astype(jnp.bfloat16), "shard", scatter_dimension=0, tiled=True
        ).astype(jnp.float32),
        lax.psum_scatter(
            attn_bias_grad.astype(jnp.bfloat16), "shard", scatter_dimension=0, tiled=True
        ).astype(jnp.float32),
        lax.psum_scatter(
            out_bias_grad.astype(jnp.bfloat16), "shard", scatter_dimension=0, tiled=True
        ).astype(jnp.float32),
        lax.psum_scatter(
            self_qkv_grad.astype(jnp.bfloat16), "shard", scatter_dimension=0, tiled=True
        ).astype(jnp.float32),
        lax.psum_scatter(
            self_out_grad.astype(jnp.bfloat16), "shard", scatter_dimension=0, tiled=True
        ).astype(jnp.float32),
        lax.psum_scatter(
            cross_q_grad.astype(jnp.bfloat16), "shard", scatter_dimension=0, tiled=True
        ).astype(jnp.float32),
        lax.psum_scatter(
            cross_kv_grad.astype(jnp.bfloat16), "shard", scatter_dimension=0, tiled=True
        ).astype(jnp.float32),
        lax.psum_scatter(
            cross_out_grad.astype(jnp.bfloat16), "shard", scatter_dimension=0, tiled=True
        ).astype(jnp.float32),
        lax.psum_scatter(
            ffn_in_grad.astype(jnp.bfloat16), "shard", scatter_dimension=0, tiled=True
        ).astype(jnp.float32),
        lax.psum_scatter(
            ffn_in_bias_grad.astype(jnp.bfloat16), "shard", scatter_dimension=0, tiled=True
        ).astype(jnp.float32),
        lax.psum_scatter(
            ffn_out_grad.astype(jnp.bfloat16), "shard", scatter_dimension=0, tiled=True
        ).astype(jnp.float32),
    )
    summed = (
        lax.psum(owned[0].astype(jnp.bfloat16), "replica").astype(jnp.float32),
        lax.psum(owned[1].astype(jnp.bfloat16), "replica").astype(jnp.float32),
        lax.psum(owned[2].astype(jnp.bfloat16), "replica").astype(jnp.float32),
        lax.psum(owned[3].astype(jnp.bfloat16), "replica").astype(jnp.float32),
        lax.psum(owned[4].astype(jnp.bfloat16), "replica").astype(jnp.float32),
        lax.psum(owned[5].astype(jnp.bfloat16), "replica").astype(jnp.float32),
        lax.psum(owned[6].astype(jnp.bfloat16), "replica").astype(jnp.float32),
        lax.psum(owned[7].astype(jnp.bfloat16), "replica").astype(jnp.float32),
        lax.psum(owned[8].astype(jnp.bfloat16), "replica").astype(jnp.float32),
        lax.psum(owned[9].astype(jnp.bfloat16), "replica").astype(jnp.float32),
        lax.psum(owned[10].astype(jnp.bfloat16), "replica").astype(jnp.float32),
        lax.psum(owned[11].astype(jnp.bfloat16), "replica").astype(jnp.float32),
    )
    return (
        output[None],
        hidden_grad[None],
        encoded_grad[None],
        summed[0],
        summed[1],
        summed[2],
        summed[3],
        summed[4],
        summed[5],
        summed[6],
        summed[7],
        summed[8],
        summed[9],
        summed[10],
        summed[11],
    )


def solution(mesh):
    placed = (
        P("replica", "shard", None),
        P("replica", "shard", None),
        P("replica", "shard", None),
        P("shard", None),
        P("shard", None),
        P("shard", None),
        P("shard", None),
        P("shard", None),
        P("shard", None),
        P("shard", None),
        P("shard", None),
        P("shard", None),
        P("shard", None),
        P("shard"),
        P("shard", None),
    )
    return jax.shard_map(
        on_device,
        mesh=mesh,
        in_specs=placed,
        out_specs=(
            P("replica", "shard", None),
            P("replica", "shard", None),
            P("replica", "shard", None),
            P("shard", None),
            P("shard", None),
            P("shard", None),
            P("shard", None),
            P("shard", None),
            P("shard", None),
            P("shard", None),
            P("shard", None),
            P("shard", None),
            P("shard", None),
            P("shard"),
            P("shard", None),
        ),
        check_vma=False,
    )
```

profile of v0, /device:TPU:8, one launch (start us, length us, event | category | flops | bytes accessed | tf_op | source)
XLA Modules:
  0.0 1378.4 jit_solution(8366145022611689226)
XLA Ops:
  18.0 38.4 %all-gather.21.cloned.1.call-done = bf16[1024,2048]{1,0:T(8,128)(2,1)} async-done(((bf16[128,2048]{1,0:T(8,128)(2,1)}), bf16[1024,2048]{1,0:T(8,128)(2,1)}) %all-gather.21.cloned.1.call-update) | async-done | bytes 4194320 | tf_op jit(solution)/shard_map/all_gather | solution.py:195
  81.6 39.3 %all-gather.13.cloned.1.call-done = bf16[1024,3072]{1,0:T(8,128)(2,1)} async-done(((bf16[128,3072]{1,0:T(8,128)(2,1)}), bf16[1024,3072]{1,0:T(8,128)(2,1)}) %all-gather.13.cloned.1.call-update) | async-done | bytes 6291472 | tf_op jit(solution)/shard_map/all_gather | solution.py:165
  158.0 25.9 %all-gather.27.cloned.1.call-done = bf16[1024,1024]{1,0:T(8,128)(2,1)} async-done(((bf16[128,1024]{1,0:T(8,128)(2,1)}), bf16[1024,1024]{1,0:T(8,128)(2,1)}) %all-gather.27.cloned.1.call-update) | async-done | bytes 2097168 | tf_op jit(solution)/shard_map/all_gather | solution.py:208
  187.9 26.7 %all-gather.15.cloned.1.call-done = bf16[1024,1024]{1,0:T(8,128)(2,1)} async-done(((bf16[128,1024]{1,0:T(8,128)(2,1)}), bf16[1024,1024]{1,0:T(8,128)(2,1)}) %all-gather.15.cloned.1.call-update) | async-done | bytes 2097168 | tf_op jit(solution)/shard_map/all_gather | solution.py:188
  217.5 27.8 %all-gather.17.cloned.1.call-done = bf16[1024,1024]{1,0:T(8,128)(2,1)} async-done(((bf16[128,1024]{1,0:T(8,128)(2,1)}), bf16[1024,1024]{1,0:T(8,128)(2,1)}) %all-gather.17.cloned.1.call-update) | async-done | bytes 2097168 | tf_op jit(solution)/shard_map/all_gather | solution.py:187
  249.2 18.4 %while.52 = (s32[]{:T(128)}, bf16[4,128,256]{1,2,0:T(8,128)(2,1)S(1)}, f32[4,4,128]{2,1,0:T(4,128)S(1)}, s32[4]{0:T(128)S(1)}, bf16[1024,1024]{0,1:T(8,128)(2,1)...) while((s32[]{:T(128)}, ...), condition=%wide.region_5.6_spmd, body=%wide.region_2.5_spmd.sunk | while | flops 140639872 | bytes 10372299 | solution.py:97
  278.0 27.7 %all-gather.25.cloned.1.call-done = bf16[1024,1024]{1,0:T(8,128)(2,1)} async-done(((bf16[128,1024]{1,0:T(8,128)(2,1)}), bf16[1024,1024]{1,0:T(8,128)(2,1)}) %all-gather.25.cloned.1.call-update) | async-done | bytes 2097168 | tf_op jit(solution)/shard_map/all_gather | solution.py:194
  309.7 17.5 %while.53 = (s32[]{:T(128)}, bf16[4,128,256]{1,2,0:T(8,128)(2,1)S(1)}, f32[4,4,128]{2,1,0:T(4,128)S(1)}, s32[4]{0:T(128)S(1)}, bf16[1024,1024]{0,1:T(8,128)(2,1)...) while((s32[]{:T(128)}, ...), condition=%wide.region_11.12_spmd, body=%wide.region_8.11_spmd.sunk | while | flops 138935808 | bytes 9846975 | solution.py:97
  338.4 78.0 %all-gather.31.cloned.1.call-done = bf16[1024,4096]{1,0:T(8,128)(2,1)} async-done(((bf16[128,4096]{1,0:T(8,128)(2,1)}), bf16[1024,4096]{1,0:T(8,128)(2,1)}) %all-gather.31.cloned.1.call-update) | async-done | bytes 8388624 | tf_op jit(solution)/shard_map/all_gather | solution.py:215
  425.7 72.9 %all-gather.33.cloned.1.call-done = bf16[4096,1024]{1,0:T(8,128)(2,1)} async-done(((bf16[512,1024]{1,0:T(8,128)(2,1)}), bf16[4096,1024]{1,0:T(8,128)(2,1)}) %all-gather.33.cloned.1.call-update) | async-done | bytes 8388624 | tf_op jit(solution)/shard_map/all_gather | solution.py:216
  519.4 43.5 %while.54 = (s32[]{:T(128)}, bf16[4,128,256]{1,2,0:T(8,128)(2,1)}, bf16[4,1024,256]{1,2,0:T(8,128)(2,1)}, bf16[4,1024,256]{1,2,0:T(8,128)(2,1)}, s32[4]{0:T(128)...) while((s32[]{:T(128)}, bf16[4,128,256]{1,2,0:T(8,128)(2,1)}, ...), condition=%wide.region_18.19_spmd, body=%wide.region_16.18_spmd.sunk | while | flops 340327936 | bytes 23472596 | solution.py:137
  581.9 47.9 %while.55 = (s32[]{:T(128)}, bf16[4,128,256]{1,2,0:T(8,128)(2,1)}, bf16[4,1024,256]{1,2,0:T(8,128)(2,1)}, bf16[4,1024,256]{1,2,0:T(8,128)(2,1)}, s32[4]{0:T(128)...) while((s32[]{:T(128)}, bf16[4,128,256]{1,2,0:T(8,128)(2,1)}, ...), condition=%wide.region_23.24_spmd, body=%wide.region_21.23_spmd.sunk | while | flops 340983424 | bytes 23670184 | solution.py:137
  675.6 36.0 %reduce-scatter.46.cloned.1.call-done = bf16[128,1024]{1,0:T(8,128)(2,1)} async-done(((bf16[1024,1024]{1,0:T(8,128)(2,1)}), bf16[128,1024]{1,0:T(8,128)(2,1)}) %reduce-scatter.46.cloned.1.call-update) | async-done | bytes 262160
  742.7 19.7 %reduce-scatter.62.cloned.1.call-done = bf16[128,2048]{1,0:T(8,128)(2,1)} async-done(((bf16[1024,2048]{1,0:T(8,128)(2,1)}), bf16[128,2048]{1,0:T(8,128)(2,1)}) %reduce-scatter.62.cloned.1.call-update) | async-done | bytes 524304
  764.5 34.2 %reduce-scatter.36.cloned.1.call-done = bf16[128,1024]{1,0:T(8,128)(2,1)} async-done(((bf16[1024,1024]{1,0:T(8,128)(2,1)}), bf16[128,1024]{1,0:T(8,128)(2,1)}) %reduce-scatter.36.cloned.1.call-update) | async-done | bytes 262160 | tf_op jit(solution)/shard_map/reduce_scatter | solution.py:339
  798.7 36.6 %reduce-scatter.38.cloned.1.call-done = bf16[128,1024]{1,0:T(8,128)(2,1)} async-done(((bf16[1024,1024]{1,0:T(8,128)(2,1)}), bf16[128,1024]{1,0:T(8,128)(2,1)}) %reduce-scatter.38.cloned.1.call-update) | async-done | bytes 262160 | tf_op jit(solution)/shard_map/reduce_scatter | solution.py:342
  835.2 36.9 %reduce-scatter.40.cloned.1.call-done = bf16[128,1024]{1,0:T(8,128)(2,1)} async-done(((bf16[1024,1024]{1,0:T(8,128)(2,1)}), bf16[128,1024]{1,0:T(8,128)(2,1)}) %reduce-scatter.40.cloned.1.call-update) | async-done | bytes 262160 | tf_op jit(solution)/shard_map/reduce_scatter | solution.py:348
  872.1 71.5 %reduce-scatter.34.cloned.1.call-done = bf16[128,3072]{1,0:T(8,128)(2,1)} async-done(((bf16[1024,3072]{1,0:T(8,128)(2,1)}), bf16[128,3072]{1,0:T(8,128)(2,1)}) %reduce-scatter.34.cloned.1.call-update) | async-done | bytes 786448 | tf_op jit(solution)/shard_map/reduce_scatter | solution.py:336
  943.7 90.3 %reduce-scatter.42.cloned.1.call-done = bf16[128,4096]{1,0:T(8,128)(2,1)} async-done(((bf16[1024,4096]{1,0:T(8,128)(2,1)}), bf16[128,4096]{1,0:T(8,128)(2,1)}) %reduce-scatter.42.cloned.1.call-update) | async-done | bytes 1048592 | tf_op jit(solution)/shard_map/reduce_scatter | solution.py:351
  1033.9 90.3 %reduce-scatter.44.cloned.1.call-done = bf16[512,1024]{1,0:T(8,128)(2,1)} async-done(((bf16[4096,1024]{1,0:T(8,128)(2,1)}), bf16[512,1024]{1,0:T(8,128)(2,1)}) %reduce-scatter.44.cloned.1.call-update) | async-done | bytes 1048592 | tf_op jit(solution)/shard_map/reduce_scatter | solution.py:357
  1162.5 23.9 %reduce-scatter.54.cloned.1.call-done = bf16[128,3]{1,0:T(8,128)(2,1)} async-done(((bf16[1024,3]{1,0:T(8,128)(2,1)}), bf16[128,3]{1,0:T(8,128)(2,1)}) %reduce-scatter.54.cloned.1.call-update) | async-done | bytes 784
  1187.3 30.6 %reduce-scatter.56.cloned.1.call-done = bf16[128,3]{1,0:T(8,128)(2,1)} async-done(((bf16[1024,3]{1,0:T(8,128)(2,1)}), bf16[128,3]{1,0:T(8,128)(2,1)}) %reduce-scatter.56.cloned.1.call-update) | async-done | bytes 784
  1218.7 30.5 %reduce-scatter.58.cloned.1.call-done = bf16[128,4]{1,0:T(8,128)(2,1)} async-done(((bf16[1024,4]{1,0:T(8,128)(2,1)}), bf16[128,4]{1,0:T(8,128)(2,1)}) %reduce-scatter.58.cloned.1.call-update) | async-done | bytes 1040
  1262.9 99.1 %all-reduce.5.cloned.1.call-done = (bf16[128,2048]{0,1:T(8,128)(2,1)}, bf16[128,3072]{1,0:T(8,128)(2,1)}, bf16[128,1024]{1,0:T(8,128)(2,1)}, bf16[128,1024]{1,0:...) async-done(((bf16[128,2048]{0,1:T(8,128)(2,1)}, bf16[128,3072]{1,0:T(8,128)(2,1)}, bf16[128,1024]{1,0:T(8,128)(2,1)}, ...) | async-done | bytes 4194320 | tf_op jit(solution)/shard_map/psum | solution.py:369
  (591 shorter events, 413.9 us)
Async XLA Ops:
  7.9 113.0 %all-gather.13.cloned.1.call-start = ((), (), s32[]{:S(2)}) async-start(), calls=%async_computation.15 | async-start | bytes 7077888 | tf_op jit(solution)/shard_map/all_gather | solution.py:165
  8.7 145.4 %all-gather.23.cloned.1.call-start = ((), (), s32[]{:S(2)}) async-start(), calls=%async_computation.20 | async-start | bytes 2359296 | tf_op jit(solution)/shard_map/all_gather | solution.py:209
  60.1 123.8 %all-gather.27.cloned.1.call-start = ((), (), s32[]{:S(2)}) async-start(), calls=%async_computation.22 | async-start | bytes 2359296 | tf_op jit(solution)/shard_map/all_gather | solution.py:208
  60.9 153.7 %all-gather.15.cloned.1.call-start = ((), (), s32[]{:S(2)}) async-start(), calls=%async_computation.16 | async-start | bytes 2359296 | tf_op jit(solution)/shard_map/all_gather | solution.py:188
  125.7 119.6 %all-gather.17.cloned.1.call-start = ((), (), s32[]{:S(2)}) async-start(), calls=%async_computation.17 | async-start | bytes 2359296 | tf_op jit(solution)/shard_map/all_gather | solution.py:187
  126.5 149.0 %all-gather.19.cloned.1.call-start = ((), (), s32[]{:S(2)}) async-start(), calls=%async_computation.18 | async-start | bytes 2359296 | tf_op jit(solution)/shard_map/all_gather | solution.py:166
  127.3 178.5 %all-gather.25.cloned.1.call-start = ((), (), s32[]{:S(2)}) async-start(), calls=%async_computation.21 | async-start | bytes 2359296 | tf_op jit(solution)/shard_map/all_gather | solution.py:194
  128.0 208.0 %all-gather.29.cloned.1.call-start = ((), (), s32[]{:S(2)}) async-start(), calls=%async_computation.23 | async-start | bytes 2359296 | tf_op jit(solution)/shard_map/all_gather | solution.py:196
  128.7 287.7 %all-gather.31.cloned.1.call-start = ((), (), s32[]{:S(2)}) async-start(), calls=%async_computation.24 | async-start | bytes 9437184 | tf_op jit(solution)/shard_map/all_gather | solution.py:215
  129.3 369.3 %all-gather.33.cloned.1.call-start = ((), (), s32[]{:S(2)}) async-start(), calls=%async_computation.25 | async-start | bytes 9437184 | tf_op jit(solution)/shard_map/all_gather | solution.py:216
  130.1 507.9 %reduce-scatter.52.cloned.1.call-start = ((), (), s32[]{:S(2)}) async-start(), calls=%async_computation.35 | async-start | bytes 2359296
  574.4 100.1 %reduce-scatter.48.cloned.1.call-start = ((), (), s32[]{:S(2)}) async-start(), calls=%async_computation.33 | async-start | bytes 2359296
  637.9 124.5 %reduce-scatter.62.cloned.1.call-start = ((), (), s32[]{:S(2)}) async-start(), calls=%async_computation.40 | async-start | bytes 4718592
  650.2 148.5 %reduce-scatter.36.cloned.1.call-start = ((), (), s32[]{:S(2)}) async-start(), calls=%async_computation.27 | async-start | bytes 2359296 | tf_op jit(solution)/shard_map/reduce_scatter | solution.py:339
  653.4 181.9 %reduce-scatter.38.cloned.1.call-start = ((), (), s32[]{:S(2)}) async-start(), calls=%async_computation.28 | async-start | bytes 2359296 | tf_op jit(solution)/shard_map/reduce_scatter | solution.py:342
  655.7 216.4 %reduce-scatter.40.cloned.1.call-start = ((), (), s32[]{:S(2)}) async-start(), calls=%async_computation.29 | async-start | bytes 2359296 | tf_op jit(solution)/shard_map/reduce_scatter | solution.py:348
  657.8 285.8 %reduce-scatter.34.cloned.1.call-start = ((), (), s32[]{:S(2)}) async-start(), calls=%async_computation.26 | async-start | bytes 7077888 | tf_op jit(solution)/shard_map/reduce_scatter | solution.py:336
  717.6 316.3 %reduce-scatter.42.cloned.1.call-start = ((), (), s32[]{:S(2)}) async-start(), calls=%async_computation.30 | async-start | bytes 9437184 | tf_op jit(solution)/shard_map/reduce_scatter | solution.py:351
  724.7 399.5 %reduce-scatter.44.cloned.1.call-start = ((), (), s32[]{:S(2)}) async-start(), calls=%async_computation.31 | async-start | bytes 9437184 | tf_op jit(solution)/shard_map/reduce_scatter | solution.py:357
  731.7 423.4 %reduce-scatter.60.cloned.1.call-start = ((), (), s32[]{:S(2)}) async-start(), calls=%async_computation.39 | async-start | bytes 294912
  733.4 453.0 %reduce-scatter.54.cloned.1.call-start = ((), (), s32[]{:S(2)}) async-start(), calls=%async_computation.36 | async-start | bytes 294912
  740.5 477.3 %reduce-scatter.56.cloned.1.call-start = ((), (), s32[]{:S(2)}) async-start(), calls=%async_computation.37 | async-start | bytes 294912
  741.7 507.5 %reduce-scatter.58.cloned.1.call-start = ((), (), s32[]{:S(2)}) async-start(), calls=%async_computation.38 | async-start | bytes 294912
  742.7 619.4 %all-reduce.5.cloned.1.call-start = ((), (), s32[]{:S(2)}) async-start(), calls=%async_computation.41 | async-start | bytes 8388608 | tf_op jit(solution)/shard_map/psum | solution.py:369
  (103 other events, 2174.4 us)
Sparse Core Ops, SparseCore 0:
  9.6 46.7 all-gather.20
  58.1 62.8 all-gather.12
  123.1 30.1 all-gather.22
  155.3 28.6 all-gather.26
  186.0 28.5 all-gather.14
  216.6 28.5 all-gather.16
  246.9 28.5 all-gather.18
  277.1 28.5 all-gather.24
  307.3 28.6 all-gather.28
  337.5 78.9 all-gather.30
  418.0 80.5 all-gather.32
  567.0 33.2 reduce-scatter.51
  602.6 34.4 reduce-scatter.49
  639.8 34.6 reduce-scatter.47
  677.2 34.4 reduce-scatter.45
  713.8 48.5 reduce-scatter.61
  764.6 34.0 reduce-scatter.35
  800.8 34.3 reduce-scatter.37
  837.5 34.5 reduce-scatter.39
  874.3 69.3 reduce-scatter.33
  946.0 87.9 reduce-scatter.41
  1036.2 87.9 reduce-scatter.43
  1220.6 28.5 reduce-scatter.57
  1254.1 107.8 all-reduce.4
  (3 shorter events, 84.9 us)
where the time goes:
time: 1390 us; the launch traced here: 1380 us
  waiting for transfers between devices  985 us (71%)
  local copies, waits for them, and re-layouts  148 us (11%)
  matrix products  114 us (8%)
  blocking collectives  75.8 us (5%)
  other arithmetic  26.7 us (2%)
  between operations  16.2 us (1%)
    unnamed x36, waiting for transfers between devices  173 us
    psum x1, waiting for transfers between devices, on_device(): lax.psum(owned[7].astype(jnp.bfloat16), 'replica').astype(jnp.float32)  99.1 us
    reduce_scatter x1, waiting for transfers between devices, on_device(): lax.psum_scatter(ffn_in_grad.astype(jnp.bfloat16), 'shard', scatter_dimen...  90.3 us
    reduce_scatter x1, waiting for transfers between devices, on_device(): lax.psum_scatter(ffn_out_grad.astype(jnp.bfloat16), 'shard', scatter_dime...  90.3 us
    all_gather x1, waiting for transfers between devices, on_device(): lax.all_gather(ffn_in, 'shard', axis=0, tiled=True)  78 us
    all_gather x1, waiting for transfers between devices, on_device(): lax.all_gather(ffn_out, 'shard', axis=0, tiled=True)  72.9 us
    reduce_scatter x1, waiting for transfers between devices, on_device(): lax.psum_scatter(self_qkv_grad.astype(jnp.bfloat16), 'shard', scatter_dim...  71.5 us
    dynamic_slice x56, local copies, waits for them, and re-layouts, head_slice(): lax.dynamic_slice_in_dim(values_in, column, group_width, 1)  53.1 us
  transfers between devices with their start and end apart: 27, of which 24 were waited for; matrix products, arithmetic and copies ran while one was open for 15% of the time, Pallas kernels for 0%

commit v1 on v0

v1 whole, which is shorter than its diff:
```python
import jax
import jax.numpy as jnp
from jax import lax
from jax.experimental import pallas as pl
from jax.experimental.pallas import tpu as pltpu
from jax.sharding import Mesh
from jax.sharding import PartitionSpec as P

HEAD_DIM = 64
AXES = ("r", "z", "c")
BF = jnp.bfloat16
F32 = jnp.float32


def mm(a, b):
    return jnp.dot(a, b, preferred_element_type=F32)


def mm_tn(a, b):
    return lax.dot_general(a, b, (((0,), (0,)), ((), ())), preferred_element_type=F32)


def mm_nt(a, b):
    return lax.dot_general(a, b, (((1,), (1,)), ((), ())), preferred_element_type=F32)


def layer_norm(v, gain, shift):
    average = jnp.mean(v, axis=-1, keepdims=True)
    centred = v - average
    variance = jnp.mean(centred * centred, axis=-1, keepdims=True)
    inverse = lax.rsqrt(variance + 1e-05)
    normed = centred * inverse
    return (normed * gain + shift).astype(BF), normed, inverse


def norm_backward(grad, normed, inverse, gain):
    gain_grad = jnp.sum(grad * normed, axis=0)
    shift_grad = jnp.sum(grad, axis=0)
    scaled = grad * gain
    projected = (
        scaled
        - jnp.mean(scaled, axis=-1, keepdims=True)
        - normed * jnp.mean(scaled * normed, axis=-1, keepdims=True)
    )
    return inverse * projected, gain_grad, shift_grad


class Links:
    def __init__(self, planes_r, planes_z):
        self.R = planes_r
        self.Z = planes_z
        self.K = planes_r.bit_length() - 1
        self.M = planes_z.bit_length() - 1
        assert planes_r == 1 << self.K and planes_z == 1 << self.M

    def go(self, x, move):
        pairs = []
        for r in range(self.R):
            for z in range(self.Z):
                for c in range(2):
                    r2, z2, c2 = move(r, z, c)
                    pairs.append(((r * self.Z + z) * 2 + c, (r2 * self.Z + z2) * 2 + c2))
        return lax.ppermute(x, AXES, pairs)

    def to_plane(self, x):
        return self.go(x, lambda r, z, c: (z ^ r, r, c))

    def from_plane(self, x):
        return self.go(x, lambda r, z, c: (z, r ^ z, c))

    def core(self, x):
        return self.go(x, lambda r, z, c: (r, z, 1 - c))

    def bit(self, i, c):
        return i if c == 0 else self.K - 1 - i

    def step(self, x, i):
        return self.go(x, lambda r, z, c: (r ^ (1 << self.bit(i, c)), z, c))

    def same_step(self, x, i):
        return self.go(x, lambda r, z, c: (r ^ (1 << i), z, c))

    def layer_step(self, x, i):
        return self.go(x, lambda r, z, c: (r, z ^ (1 << i), c))

    def offset(self, p, c):
        return sum(1 << self.bit(i, c) for i in range(self.K) if p >> i & 1)

    def reverse(self, p):
        return sum(1 << (self.K - 1 - i) for i in range(self.K) if p >> i & 1)

    def gather(self, x, axis=0):
        for i in range(self.K):
            x = jnp.concatenate([x, self.step(x, i)], axis=axis)
        return x, self.core(x)

    def by_rank(self, blocks, r, c):
        near, far = blocks[: self.R], blocks[self.R :]
        even = [jnp.where(c == 0, n, f) for n, f in zip(near, far)]
        odd = [jnp.where(c == 0, f, n) for n, f in zip(near, far)]
        even = ordered(even, r)
        odd = ordered([odd[self.reverse(p)] for p in range(self.R)], r)
        return [b for pair in zip(even, odd) for b in pair]

    def by_distance(self, blocks, r, c):
        even = ordered(blocks[0::2], r)
        odd = ordered(blocks[1::2], r)
        odd = [odd[self.reverse(p)] for p in range(self.R)]
        near = [jnp.where(c == 0, a, b) for a, b in zip(even, odd)]
        far = [jnp.where(c == 0, b, a) for a, b in zip(even, odd)]
        return near + far

    def scatter_sum(self, near, far):
        away = self.core(far().astype(BF))
        total = near() + away.astype(F32)
        for i in reversed(range(self.K)):
            half = total.shape[0] // 2
            got = self.step(total[half:].astype(BF), i)
            total = total[:half] + got.astype(F32)
        return total

    def to_rows(self, near, far):
        w = near.shape[1]
        block = {(0, 0): near, (1, 0): self.core(far)}
        for i in reversed(range(self.K)):
            keys = sorted(block)
            half = block[keys[0]].shape[0] // 2
            got = self.step(jnp.concatenate([block[k][half:] for k in keys], axis=1), i)
            for n, (e, p) in enumerate(keys):
                block[(e, p | 1 << i)] = got[:, n * w : (n + 1) * w]
                block[(e, p)] = block[(e, p)][:half]
        order = [(0, p) for p in range(self.R)] + [(1, self.reverse(p)) for p in range(self.R)]
        return [block[k] for k in order]

    def to_heads(self, blocks):
        w = blocks[0].shape[1]
        block = {}
        for p in range(self.R):
            block[(0, p)] = blocks[p]
            block[(1, p)] = blocks[self.R + self.reverse(p)]
        for i in range(self.K):
            keys = sorted(k for k in block if k[1] >> i & 1)
            got = self.step(jnp.concatenate([block.pop(k) for k in keys], axis=1), i)
            for n, (e, p) in enumerate(keys):
                k = (e, p ^ 1 << i)
                block[k] = jnp.concatenate([block[k], got[:, n * w : (n + 1) * w]], axis=0)
        return block[(0, 0)], self.core(block[(1, 0)])

    def gather_parts(self, x):
        parts = [x]
        for i in range(self.K):
            parts = parts + [self.step(p, i) for p in parts]
        return parts

    def sum_chips(self, x):
        for i in range(self.K):
            x = x + self.same_step(x, i)
        return x

    def scatter_layers(self, blocks, z):
        for i in reversed(range(self.M)):
            n = blocks.shape[0] // 2
            bit = (z >> i) & 1
            keep = lax.dynamic_slice_in_dim(blocks, bit * n, n, 0)
            send = lax.dynamic_slice_in_dim(blocks, (1 - bit) * n, n, 0)
            got = self.layer_step(send, i)
            blocks = (keep.astype(F32) + got.astype(F32)).astype(blocks.dtype)
        return blocks[0]


def attend(q, k, v, pos, causal):
    heads = q.shape[1] // HEAD_DIM
    outs, lses = [], []
    for h in range(heads):
        cut = slice(h * HEAD_DIM, (h + 1) * HEAD_DIM)
        s = mm_nt(q[:, cut], k[:, cut]) * HEAD_DIM ** (-0.5)
        if causal:
            s = jnp.where(pos[:, None] >= pos[None, :], s, -1e30)
        m = jnp.max(s, axis=-1, keepdims=True)
        p = jnp.exp(s - m)
        t = jnp.sum(p, axis=-1, keepdims=True)
        outs.append(mm((p / t).astype(BF), v[:, cut]).astype(BF))
        lses.append(m + jnp.log(t))
    return jnp.concatenate(outs, axis=1), lses


def attend_back(q, k, v, e, lses, pos, causal):
    heads = q.shape[1] // HEAD_DIM
    dqs, dks, dvs = [], [], []
    for h in range(heads):
        cut = slice(h * HEAD_DIM, (h + 1) * HEAD_DIM)
        s = mm_nt(q[:, cut], k[:, cut]) * HEAD_DIM ** (-0.5)
        if causal:
            s = jnp.where(pos[:, None] >= pos[None, :], s, -1e30)
        p = jnp.exp(s - lses[h])
        dp = mm_nt(e[:, cut], v[:, cut])
        inner = jnp.sum(dp * p, axis=-1, keepdims=True)
        ds = (p * (dp - inner)).astype(BF)
        dqs.append((mm(ds, k[:, cut]) * HEAD_DIM ** (-0.5)).astype(BF))
        dks.append((mm_tn(ds, q[:, cut]) * HEAD_DIM ** (-0.5)).astype(BF))
        dvs.append(mm_tn(p.astype(BF), e[:, cut]).astype(BF))
    return tuple(jnp.concatenate(g, axis=1) for g in (dqs, dks, dvs))


def after(x, *what):
    return lax.optimization_barrier((x,) + what)[0]


def col_sum(v):
    return jnp.sum(v.astype(F32), axis=0)


def ordered(parts, index):
    n = len(parts)
    outs = []
    for k in range(n):
        v = parts[k]
        for d in range(1, n):
            v = jnp.where(index == d, parts[k ^ d], v)
        outs.append(v)
    return outs


def place_blocks(links, here, parts, cuts, shapes):
    R = links.R
    aligned = all(w % 128 == 0 for _, _, w, _, _ in cuts)
    if not aligned:
        outs = [jnp.zeros(shape, F32) for shape in shapes]
        for p in range(R):
            for out, start, w, e, spot in cuts:
                chip = here[0] ^ jnp.where(here[1] == 0, links.offset(p, 0), links.offset(p, 1))
                at = tuple(jnp.int32(v) for v in spot(chip, here[1] ^ e))
                piece = parts[p][:, start : start + w].astype(F32)
                outs[out] = lax.dynamic_update_slice(outs[out], piece, at)
        return outs

    def kernel(here_ref, *refs):
        ins, outs = refs[:R], refs[R:]
        core = here_ref[1]
        for p in range(R):
            chip = here_ref[0] ^ jnp.where(core == 0, links.offset(p, 0), links.offset(p, 1))
            for out, start, w, e, spot in cuts:
                row, col = spot(chip, core ^ e)
                n = ins[p].shape[0]
                row = row if isinstance(row, int) else pl.multiple_of(row, n)
                col = col if isinstance(col, int) else pl.multiple_of(col, 128)
                piece = ins[p][:, start : start + w].astype(F32)
                outs[out][pl.ds(row, n), pl.ds(col, w)] = piece

    return pl.pallas_call(
        kernel,
        out_shape=[jax.ShapeDtypeStruct(shape, F32) for shape in shapes],
        in_specs=[pl.BlockSpec(memory_space=pltpu.SMEM)]
        + [pl.BlockSpec(memory_space=pltpu.VMEM)] * R,
        out_specs=[pl.BlockSpec(memory_space=pltpu.VMEM)] * len(shapes),
        compiler_params=pltpu.CompilerParams(vmem_limit_bytes=40 << 20),
        cost_estimate=pl.CostEstimate(flops=0, transcendentals=0, bytes_accessed=12 << 20),
    )(here, *parts)


def make(R, Z):
    links = Links(R, Z)

    def on_device(
        hidden, encoded, cotangent, norm_gain, norm_bias, attn_bias, out_bias,
        self_qkv, self_out, cross_q, cross_kv, cross_out, ffn_in, ffn_in_bias, ffn_out,
    ):
        r = lax.axis_index("r")
        z = lax.axis_index("z")
        c = lax.axis_index("c")
        rank = r * 2 + c
        rows = hidden.shape[1]
        D = hidden.shape[2]
        own = self_out.shape[0]
        rank_cols = D // (2 * R)
        FF = ffn_in.shape[1]
        sub = ffn_out.shape[0] // R
        up_rows = FF // D
        quarter = D // Z
        zero = jnp.int32(0)

        x_low = links.to_plane(hidden[0])

        def chip_columns(w, width):
            cut = lax.dynamic_index_in_dim(w.reshape(own, -1, R, 2, width), r, 2, False)
            return cut.transpose(2, 0, 1, 3).reshape(2, own, -1)

        def gather_layers(cut):
            full = lax.all_gather(cut, ("z", "c"), axis=1, tiled=True)
            return lax.dynamic_index_in_dim(full, c, 0, False)

        cut_self = chip_columns(jnp.concatenate([self_qkv, self_out], axis=1), rank_cols)
        w_self = gather_layers(after(cut_self, x_low))
        self_out_part = w_self[:, 3 * rank_cols :]
        w_self = w_self[:, : 3 * rank_cols]
        cut_cross = chip_columns(jnp.concatenate([cross_q, cross_kv, cross_out], axis=1), rank_cols)
        w_cross = gather_layers(after(cut_cross, w_self))
        w_cross_q = w_cross[:, :rank_cols]
        w_cross_kv = w_cross[:, rank_cols : 3 * rank_cols]
        cross_out_part = w_cross[:, 3 * rank_cols :]
        width = Z * sub
        groups = D // width
        cut_up = lax.dynamic_index_in_dim(ffn_in.reshape(own, Z, 2, R, sub), r, 3, False)
        cut_up = cut_up.transpose(2, 0, 1, 3).reshape(2, own, width)
        cut_down = lax.dynamic_slice_in_dim(ffn_out, r * sub, sub, 0)
        cut_down = jnp.concatenate(
            [cut_down[:, g * width : (g + 1) * width] for g in range(groups)], axis=0
        ).reshape(2, own, width)
        cut_ffn = after(jnp.concatenate([cut_up, cut_down], axis=2), w_cross)
        w_ffn = lax.all_gather(cut_ffn, ("z", "c"), axis=1, tiled=True)
        w_up = lax.dynamic_index_in_dim(w_ffn[:, :, :width], c, 0, False)
        w_down = w_ffn[:, :, width:].reshape(2, Z, 2, groups // 2, sub, width)
        w_down = lax.dynamic_index_in_dim(w_down, c, 2, False)
        w_down = jnp.concatenate(
            [w_down[g // (groups // 2), :, g % (groups // 2)].reshape(width, width) for g in range(groups)],
            axis=1,
        )

        vec = jnp.concatenate(
            [norm_gain.T, norm_bias.T, attn_bias.T, out_bias.T, ffn_in_bias.reshape(up_rows, own)],
            axis=0,
        )
        vec = after(vec, x_low)
        vec = jnp.concatenate(ordered([vec, links.core(vec)], c), axis=1)
        for i in range(links.M):
            vec = jnp.concatenate(ordered([vec, links.layer_step(vec, i)], (z >> i) & 1), axis=1)
        vec = vec.astype(F32)
        gains, shifts, branch = vec[0:3], vec[3:6], vec[10:13]
        pair_bias = lax.dynamic_slice_in_dim(vec[6:10], rank * rank_cols, rank_cols, 1)
        up_bias = vec[13:].reshape(up_rows, 2 * Z, own).transpose(1, 0, 2).reshape(Z, 2, R, sub)
        up_bias = lax.dynamic_index_in_dim(up_bias, c, 1, False)
        up_bias = lax.dynamic_index_in_dim(up_bias, r, 1, False).reshape(width)

        def chunks(core):
            first = jnp.array([links.offset(p, 0) for p in range(R)], jnp.int32)
            second = jnp.array([links.offset(p, 1) for p in range(R)], jnp.int32)
            return (jnp.where(core == 0, first, second) ^ r ^ z) * 2 + core

        pos = jnp.concatenate([chunks(c), chunks(1 - c)])
        pos = (pos[:, None] * rows + jnp.arange(rows, dtype=jnp.int32)[None, :]).reshape(-1)
        half = R * rows

        def both(f, pair):
            return f(pair[0]), f(pair[1])

        def join(pair):
            return jnp.concatenate(pair, axis=0)

        def halves(v):
            return v[:half], v[half:]

        def total_tn(x, y):
            return (mm_tn(x[0], y[0]) + mm_tn(x[1], y[1])).astype(BF)

        def plane_sum(x, w):
            return links.scatter_sum(lambda: mm_nt(x[0], w), lambda: mm_nt(x[1], w))

        def split(v):
            w = v.shape[1] // (2 * R)
            return [v[:, i * w : (i + 1) * w] for i in range(2 * R)]

        def project(c_heads, w_out):
            blocks = links.by_rank(links.to_rows(*halves(c_heads)), r, c)
            rows_all = jnp.concatenate(blocks, axis=1)
            near, far = mm(rows_all, w_out[0]), mm(rows_all, w_out[1])
            return jnp.concatenate(links.by_rank(split_half(near) + split_half(far), r, c), axis=1)

        def split_half(v):
            return [v[:, i * rank_cols : (i + 1) * rank_cols] for i in range(R)]

        def unproject(g, w_out):
            g = links.by_distance(split(g), r, c)
            near, far = jnp.concatenate(g[:R], axis=1), jnp.concatenate(g[R:], axis=1)
            e = (mm_nt(near, w_out[0]) + mm_nt(far, w_out[1])).astype(BF)
            return links.to_heads(links.by_distance(split(e), r, c))

        def sum_layers(g):
            return lax.psum_scatter(g, "z", scatter_dimension=0, tiled=True)

        def to_core(g):
            n = g.shape[0] // 2
            keep = lax.dynamic_slice_in_dim(g, c * n, n, 0)
            send = lax.dynamic_slice_in_dim(g, (1 - c) * n, n, 0)
            return jnp.concatenate([keep, links.core(send)], axis=1)

        def place(parts, index, cuts, shapes):
            here = jnp.stack([index, c]).astype(jnp.int32)
            return place_blocks(links, here, parts, cuts, shapes)

        def columns(start, span, outer, w, core_first, out):
            def spot(o, j, cc):
                return o * 2 * R * w + (cc * R + j if core_first else j * 2 + cc) * w

            return [
                (out, start + e * span + o * w, w, e, lambda j, cc, o=o: (0, spot(o, j, cc)))
                for o in range(outer)
                for e in range(2)
            ]

        x = x_low.astype(F32)
        a1, n1, i1 = layer_norm(x, gains[0], shifts[0])
        a1 = links.gather(a1)
        memory = links.to_plane(after(encoded[0], a1[0]))
        joined = join(both(lambda v: mm(v, w_self), a1))
        q1 = (joined[:, :rank_cols] + pair_bias[0]).astype(BF)
        k1 = joined[:, rank_cols : 2 * rank_cols].astype(BF)
        v1 = (joined[:, 2 * rank_cols :] + pair_bias[1]).astype(BF)
        c1, l1 = attend(q1, k1, v1, pos, True)
        w_self_out = links.gather(after(self_out_part, a1[1]), axis=1)
        h1 = x + (project(c1, w_self_out) + branch[0])
        a2, n2, i2 = layer_norm(h1, gains[1], shifts[1])
        memory_all = links.gather(after(memory, w_self_out[0]))
        joined = join(both(lambda v: mm(v, w_cross_kv), memory_all))
        k2 = joined[:, :rank_cols].astype(BF)
        v2 = (joined[:, rank_cols:] + pair_bias[3]).astype(BF)
        a2 = links.gather(a2)
        q2 = (join(both(lambda v: mm(v, w_cross_q), a2)) + pair_bias[2]).astype(BF)
        c2, l2 = attend(q2, k2, v2, pos, False)
        seed_low = links.to_plane(after(cotangent[0], a2[0]))
        seed = seed_low.astype(F32)
        w_cross_out = links.gather(after(cross_out_part, q2), axis=1)
        h2 = h1 + (project(c2, w_cross_out) + branch[1])
        a3, n3, i3 = layer_norm(h2, gains[2], shifts[2])
        seed_all = links.gather(after(seed_low, w_cross_out[0]))
        a3 = links.gather(a3)

        def feed(v, s):
            pre = mm(v, w_up) + up_bias
            cdf = 0.5 * (1.0 + lax.erf(pre * (0.5 ** 0.5)))
            slope = cdf + pre * (jnp.exp(-0.5 * pre * pre) * (0.5 / jnp.pi) ** 0.5)
            return (pre * cdf).astype(BF), (slope * mm_nt(s, w_down)).astype(BF)

        fed = [feed(a3[0], seed_all[0]), feed(a3[1], seed_all[1])]
        act = fed[0][0], fed[1][0]
        gz = fed[0][1], fed[1][1]

        lifted, s3, t3 = norm_backward(plane_sum(gz, w_up), n3, i3, gains[2])
        down_grad = total_tn(act, seed_all)
        up_grad = total_tn(a3, gz)
        d2 = seed + lifted
        g2 = d2.astype(BF)
        e2 = unproject(g2, w_cross_out)
        gq2, gk2, gv2 = attend_back(q2, k2, v2, join(e2), l2, pos, False)
        g2_all = links.gather(after(g2, e2[1]))
        output = (h2 + (plane_sum(act, after(w_down, g2_all[0]).T) + branch[2])).astype(BF)
        output = links.from_plane(output)
        cross_out_grad = total_tn(halves(c2), g2_all)
        pair2 = jnp.concatenate([gk2, gv2], axis=1)
        cross_grad = jnp.concatenate(
            [total_tn(a2, halves(gq2)), total_tn(memory_all, halves(pair2))], axis=1
        )
        lifted, s2, t2 = norm_backward(plane_sum(halves(gq2), w_cross_q), n2, i2, gains[1])
        d1 = d2 + lifted
        g1 = d1.astype(BF)
        e1 = unproject(g1, w_self_out)
        up_width, cross_width = width, 3 * rank_cols
        g = sum_layers(jnp.concatenate([up_grad, cross_grad], axis=1))
        pack = to_core(g)
        down = sum_layers(down_grad)
        span = up_width + cross_width
        cuts = columns(0, span, Z, sub, True, 0) + columns(up_width, span, 3, rank_cols, False, 1)
        shapes = [(own, FF), (own, 3 * D)]
        down_shape = (R * sub, D)
        if sub == own:
            pack = jnp.concatenate([pack, down], axis=1)
            cuts.append((2, 2 * span, D, 0, lambda j, cc: (j * sub, 0)))
            down_parts = []
        else:
            down_parts = links.gather_parts(after(down, e1[1]))
        parts = links.gather_parts(after(pack, e1[1]))

        gq1, gk1, gv1 = attend_back(q1, k1, v1, join(e1), l1, pos, True)
        g1_all = links.gather(after(g1, e1[1]))
        encoded_grad = links.from_plane(plane_sum(halves(after(pair2, g1_all[0])), w_cross_kv).astype(BF))
        self_out_grad = total_tn(halves(c1), g1_all)
        triple = after(jnp.concatenate([gq1, gk1, gv1], axis=1), *parts)
        self_grad = total_tn(a1, halves(triple))
        lifted, s1, t1 = norm_backward(plane_sum(halves(triple), w_self), n1, i1, gains[0])
        hidden_grad = links.from_plane((d1 + lifted).astype(BF))

        if sub == own:
            ffn_in_grad, cross_both, ffn_out_grad = place(parts, r, cuts, shapes + [down_shape])
        else:
            ffn_in_grad, cross_both = place(parts, r, cuts, shapes)
            cuts = [(0, 0, D, 0, lambda j, cc: (j * sub, 0))]
            (ffn_out_grad,) = place(down_parts, r, cuts, [down_shape])
        cross_q_grad = cross_both[:, :D]
        cross_kv_grad = cross_both[:, D:]
        pack = to_core(sum_layers(self_grad))
        (self_qkv_grad,) = place(
            links.gather_parts(pack),
            r,
            columns(0, 3 * rank_cols, 3, rank_cols, False, 0),
            [(own, 3 * D)],
        )
        g = jnp.concatenate([cross_out_grad, self_out_grad], axis=0)
        g = g.reshape(2 * rank_cols, Z, quarter).transpose(1, 0, 2)
        g = links.to_plane(links.scatter_layers(g, z))
        (both_out,) = place(
            links.gather_parts(g),
            r ^ z,
            [(0, 0, quarter, 0, lambda j, cc: (0, j * quarter))],
            [(2 * rank_cols, D)],
        )
        cross_out_grad, self_out_grad = both_out[:rank_cols], both_out[rank_cols:]

        def sum_small(v):
            k = v.shape[0]
            blocks = v.reshape(k, Z, 2, own).transpose(2, 1, 0, 3)
            away = lax.dynamic_index_in_dim(blocks, 1 - c, 0, False)
            near = lax.dynamic_index_in_dim(blocks, c, 0, False) + links.core(away)
            return links.sum_chips(links.scatter_layers(near, z))

        def spread(v):
            return lax.dynamic_update_slice(
                jnp.zeros((v.shape[0], D), F32), v, (zero, rank * rank_cols)
            )

        up_sums = (col_sum(gz[0]) + col_sum(gz[1])).reshape(Z, 1, 1, sub)
        up_sums = lax.dynamic_update_slice(jnp.zeros((Z, 2, R, sub), F32), up_sums, (zero, c, r, zero))
        up_sums = up_sums.reshape(2 * Z, up_rows, own).transpose(1, 0, 2).reshape(up_rows, D)
        sums = jnp.concatenate(
            [
                jnp.stack([s1, s2, s3, t1, t2, t3]),
                spread(jnp.stack([col_sum(gq1), col_sum(gv1), col_sum(gq2), col_sum(gv2)])),
                jnp.stack([col_sum(g1), col_sum(g2), col_sum(seed_low)]),
                up_sums,
            ],
            axis=0,
        )
        sums = sum_small(after(sums, hidden_grad))
        return (
            output[None],
            hidden_grad.astype(F32)[None],
            encoded_grad.astype(F32)[None],
            sums[0:3].T,
            sums[3:6].T,
            sums[6:10].T,
            sums[10:13].T,
            self_qkv_grad,
            self_out_grad,
            cross_q_grad,
            cross_kv_grad,
            cross_out_grad,
            ffn_in_grad,
            sums[13:].reshape(-1),
            ffn_out_grad,
        )

    return on_device


def solution(mesh):
    R = mesh.shape["replica"]
    Z = mesh.shape["shard"] // 2
    inner = Mesh(mesh.devices.reshape(R, Z, 2), AXES)
    rows = P("r", ("z", "c"), None)
    weight = P(("z", "c"), None)
    line = P(("z", "c"))
    return jax.shard_map(
        make(R, Z),
        mesh=inner,
        in_specs=(rows,) * 3 + (weight,) * 10 + (line, weight),
        out_specs=(rows,) * 3 + (weight,) * 10 + (line, weight),
        check_vma=False,
    )
```

time: 1390 us -> 536 us (0.39)
  the two profiles are of different devices: /device:TPU:8 before, /device:TPU:0 now
where the time goes in v1:
time: 536 us; the launch traced here: 525 us
  waiting for transfers between devices  153 us (29%)
  starting transfers between devices  141 us (26%)
  matrix products  88.6 us (17%)
  local copies, waits for them, and re-layouts  75.5 us (14%)
  other arithmetic  44.3 us (8%)
  between operations  17.6 us (3%)
  Pallas kernels  5.61 us (1%)
    ppermute x82, waiting for transfers between devices, go(): return lax.ppermute(x, AXES, pairs)  149 us
    ppermute x82, starting transfers between devices, go(): return lax.ppermute(x, AXES, pairs)  141 us
    dot_general x22, matrix products, mm_tn(): lax.dot_general(a, b, (((0,), (0,)), ((), ())), preferred_element_type=F32)  36.8 us
    unnamed x340, local copies, waits for them, and re-layouts  32.6 us
    dot_general x24, matrix products, mm_nt(): lax.dot_general(a, b, (((1,), (1,)), ((), ())), preferred_element_type=F32)  30 us
    dot_general x20, matrix products, mm(): return jnp.dot(a, b, preferred_element_type=F32)  21.8 us
  transfers between devices with their start and end apart: 88, of which 41 were waited for; matrix products, arithmetic and copies ran while one was open for 31% of the time, Pallas kernels for 1%

profile of v1, /device:TPU:0, one launch (start us, length us, event | category | flops | bytes accessed | tf_op | source)
XLA Modules:
  0.0 525.3 jit_solution(17956593105907650687)
XLA Ops:
  16.9 16.1 %collective-permute-start.2 = (bf16[17,256]{1,0:T(8,128)(2,1)S(1)}, bf16[17,256]{1,0:T(8,128)(2,1)S(1)}, u32[]{:S(2)}, u32[]{:S(2)}) collective-permute-start(bf16[17,256]{1,0:T(8,128)(2,1)S(1)} %pad_maximum_fusion.40), channel_id=1, source_target_pairs={{0,2},{1,3},{2,0},{3,1},{4,6},{5,7},{6,4},{7,5},{8,10},{9,11},{10,... | collective-permute-start | bytes 26120 | tf_op jit(solution)/shard_map/ppermute | solution.py:63
  34.7 4.7 collective-permute-done.3
  45.0 4.4 collective-permute-done.4
  49.6 9.1 %collective-permute-done.5 = bf16[256,1024]{0,1:T(8,128)(2,1)S(1)} collective-permute-done((bf16[256,1024]{0,1:T(8,128)(2,1)S(1)}, bf16[256,1024]{0,1:T(8,128)(2,1)S(1)}, u32[]{:S(2)}, u32[]{:S(2)}) %collective-permute-start.5) | collective-permute-done | bytes 524320 | tf_op jit(solution)/shard_map/ppermute | solution.py:63
  80.8 9.4 %collective-permute-done.10 = bf16[1024,128]{0,1:T(8,128)(2,1)S(1)} collective-permute-done((bf16[1024,128]{0,1:T(8,128)(2,1)S(1)}, bf16[1024,128]{0,1:T(8,128)(2,1)S(1)}, u32[]{:S(2)}, u32[]{:S(2)}) %collective-permute-start.10) | collective-permute-done | bytes 262176 | tf_op jit(solution)/shard_map/ppermute | solution.py:63
  92.4 8.3 %collective-permute-done.11 = bf16[1024,256]{0,1:T(8,128)(2,1)S(1)} collective-permute-done((bf16[1024,256]{0,1:T(8,128)(2,1)S(1)}, bf16[1024,256]{0,1:T(8,128)(2,1)S(1)}, u32[]{:S(2)}, u32[]{:S(2)}) %collective-permute-start.11) | collective-permute-done | bytes 524320 | tf_op jit(solution)/shard_map/ppermute | solution.py:63
  101.6 9.3 %collective-permute-start.17 = (bf16[128,1024]{1,0:T(8,128)(2,1)S(1)}, bf16[128,1024]{1,0:T(8,128)(2,1)S(1)}, u32[]{:S(2)}, u32[]{:S(2)}) collective-permute-start(bf16[128,1024]{1,0:T(8,128)(2,1)S(1)} %collective-permute-done.16), channel_id=1, source_target_pairs={{0,8},{1,17},{2,10},{3,19},{4,12},{5,21},{6,14},{7,23},{8,0},{9,25... | collective-permute-start | bytes 786440 | tf_op jit(solution)/shard_map/ppermute | solution.py:63
  111.4 5.8 %collective-permute-done.17 = bf16[128,1024]{1,0:T(8,128)(2,1)S(1)} collective-permute-done((bf16[128,1024]{1,0:T(8,128)(2,1)S(1)}, bf16[128,1024]{1,0:T(8,128)(2,1)S(1)}, u32[]{:S(2)}, u32[]{:S(2)}) %collective-permute-start.17) | collective-permute-done | bytes 262176 | tf_op jit(solution)/shard_map/ppermute | solution.py:63
  133.2 4.5 collective-permute-done.14
  169.5 7.6 %collective-permute-start.24 = (bf16[1024,256]{0,1:T(8,128)(2,1)S(1)}, bf16[1024,256]{0,1:T(8,128)(2,1)S(1)}, u32[]{:S(2)}, u32[]{:S(2)}) collective-permute-start(bf16[1024,256]{0,1:T(8,128)(2,1)S(1)} %pad_maximum_fusion.13), channel_id=1, source_target_pairs={{0,16},{1,9},{2,18},{3,11},{4,20},{5,13},{6,22},{7,15},{8,24},{9,1... | collective-permute-start | bytes 1572872 | tf_op jit(solution)/shard_map/ppermute | solution.py:63
  178.9 6.4 %collective-permute-done.24 = bf16[1024,256]{0,1:T(8,128)(2,1)S(1)} collective-permute-done((bf16[1024,256]{0,1:T(8,128)(2,1)S(1)}, bf16[1024,256]{0,1:T(8,128)(2,1)S(1)}, u32[]{:S(2)}, u32[]{:S(2)}) %collective-permute-start.24) | collective-permute-done | bytes 524320 | tf_op jit(solution)/shard_map/ppermute | solution.py:63
  193.2 4.3 collective-permute-done.26
  203.6 4.7 collective-permute-done.27
  216.0 4.7 fusion.264
  220.7 4.4 reshape.262
  225.1 5.0 constant_dynamic-slice_fusion
  249.9 4.6 collective-permute-start.34
  254.6 7.1 %collective-permute-done.34 = bf16[256,1024]{0,1:T(8,128)(2,1)S(1)} collective-permute-done((bf16[256,1024]{0,1:T(8,128)(2,1)S(1)}, bf16[256,1024]{0,1:T(8,128)(2,1)S(1)}, u32[]{:S(2)}, u32[]{:S(2)}) %collective-permute-start.34) | collective-permute-done | bytes 524320 | tf_op jit(solution)/shard_map/ppermute | solution.py:63
  313.7 5.4 %collective-permute-done.40 = bf16[256,1024]{0,1:T(8,128)(2,1)S(1)} collective-permute-done((bf16[256,1024]{0,1:T(8,128)(2,1)S(1)}, bf16[256,1024]{0,1:T(8,128)(2,1)S(1)}, u32[]{:S(2)}, u32[]{:S(2)}) %collective-permute-start.40) | collective-permute-done | bytes 524320 | tf_op jit(solution)/shard_map/ppermute | solution.py:63
  342.2 5.9 %collective-permute-done.42 = bf16[256,1024]{0,1:T(8,128)(2,1)S(1)} collective-permute-done((bf16[256,1024]{0,1:T(8,128)(2,1)S(1)}, bf16[256,1024]{0,1:T(8,128)(2,1)S(1)}, u32[]{:S(2)}, u32[]{:S(2)}) %collective-permute-start.42) | collective-permute-done | bytes 524320 | tf_op jit(solution)/shard_map/ppermute | solution.py:63
  348.9 5.9 %collective-permute-done.43 = bf16[128,1024]{0,1:T(8,128)(2,1)S(1)} collective-permute-done((bf16[128,1024]{0,1:T(8,128)(2,1)S(1)}, bf16[128,1024]{0,1:T(8,128)(2,1)S(1)}, u32[]{:S(2)}, u32[]{:S(2)}) %collective-permute-start.43) | collective-permute-done | bytes 262176 | tf_op jit(solution)/shard_map/ppermute | solution.py:63
  358.9 4.9 collective-permute-done.48
  422.2 4.5 collective-permute-done.54.refs_3_
  487.8 8.8 %collective-permute-start.66 = (f32[2,17,128]{2,0,1:T(2,128)S(1)}, f32[2,17,128]{2,0,1:T(2,128)S(1)}, u32[]{:S(2)}, u32[]{:S(2)}) collective-permute-start(f32[2,17,128]{2,0,1:T(2,128)S(1)} %constant_dynamic-slice_fusion.8), channel_id=1, source_target_pairs={{0,4},{1,5},{2,6},{3,7},{4,0},{5,1},{6,2},{7,3},{8,12},{9,13},{10,... | collective-permute-start | bytes 52232 | tf_op jit(solution)/shard_map/ppermute | solution.py:63
  (810 shorter events, 352.0 us)
Async XLA Ops:
  7.2 56.4 %all-gather.4.cloned.1.call-start = ((), (), s32[]{:S(2)}) async-start(), calls=%async_computation.3 | async-start | bytes 2359296 | tf_op jit(solution)/shard_map/all_gather | solution.py:289
  16.0 115.8 %all-gather.6.cloned.1.call-start = ((), (), s32[]{:S(2)}) async-start(), calls=%async_computation.4 | async-start | bytes 2359296 | tf_op jit(solution)/shard_map/all_gather | solution.py:289
  16.9 17.7 %collective-permute-start.2 = (bf16[17,256]{1,0:T(8,128)(2,1)S(1)}, bf16[17,256]{1,0:T(8,128)(2,1)S(1)}, u32[]{:S(2)}, u32[]{:S(2)}) collective-permute-start(bf16[17,256]{1,0:T(8,128)(2,1)S(1)} %pad_maximum_fusion.40), channel_id=1, source_target_pairs={{0,2},{1,3},{2,0},{3,1},{4,6},{5,7},{6,4},{7,5},{8,10},{9,11},{10,... | collective-permute-start | bytes 26120 | tf_op jit(solution)/shard_map/ppermute | solution.py:63
  76.2 139.8 %all-gather.8.cloned.1.call-start = ((), (), s32[]{:S(2)}) async-start(), calls=%async_computation.5 | async-start | bytes 4718592 | tf_op jit(solution)/shard_map/all_gather | solution.py:310
  76.3 25.4 %collective-permute-start.16 = (bf16[128,1024]{1,0:T(8,128)(2,1)S(1)}, bf16[128,1024]{1,0:T(8,128)(2,1)S(1)}, u32[]{:S(2)}, u32[]{:S(2)}) collective-permute-start(bf16[128,1024]{1,0:T(8,128)(2,1)S(1)} %bitcast.241), channel_id=1, source_target_pairs={{0,0},{1,1},{2,8},{3,9},{4,16},{5,17},{6,24},{7,25},{8,10},{9,11},... | collective-permute-start | bytes 786440 | tf_op jit(solution)/shard_map/ppermute | solution.py:63
  100.8 16.5 %collective-permute-start.12 = (bf16[1024,512]{0,1:T(8,128)(2,1)S(1)}, bf16[1024,512]{0,1:T(8,128)(2,1)S(1)}, u32[]{:S(2)}, u32[]{:S(2)}) collective-permute-start(bf16[1024,512]{0,1:T(8,128)(2,1)S(1)} %constant_dynamic-update-slice_fusion), channel_id=1, source_target_pairs={{0,1},{1,0},{2,3},{3,2},{4,5},{5,4},{6,7},{7,6},{8,9},{9,8},{10,11... | collective-permute-start | bytes 3145736 | tf_op jit(solution)/shard_map/ppermute | solution.py:63
  156.8 234.5 %reduce-scatter.4.cloned.1.call-start = ((), (), s32[]{:S(2)}) async-start(), calls=%async_computation.6 | async-start | bytes 2293760 | tf_op jit(solution)/shard_map/reduce_scatter | solution.py:378
  156.9 36.0 %collective-permute-start.28 = (bf16[128,1024]{0,1:T(8,128)(2,1)}, bf16[128,1024]{0,1:T(8,128)(2,1)S(1)}, u32[]{:S(2)}, u32[]{:S(2)}) collective-permute-start(bf16[128,1024]{0,1:T(8,128)(2,1)} %bitcast.40), channel_id=1, source_target_pairs={{0,0},{1,1},{2,8},{3,9},{4,16},{5,17},{6,24},{7,25},{8,10},{9,11},... | collective-permute-start | bytes 786440 | tf_op jit(solution)/shard_map/ppermute | solution.py:63
  169.5 15.7 %collective-permute-start.24 = (bf16[1024,256]{0,1:T(8,128)(2,1)S(1)}, bf16[1024,256]{0,1:T(8,128)(2,1)S(1)}, u32[]{:S(2)}, u32[]{:S(2)}) collective-permute-start(bf16[1024,256]{0,1:T(8,128)(2,1)S(1)} %pad_maximum_fusion.13), channel_id=1, source_target_pairs={{0,16},{1,9},{2,18},{3,11},{4,20},{5,13},{6,22},{7,15},{8,24},{9,1... | collective-permute-start | bytes 1572872 | tf_op jit(solution)/shard_map/ppermute | solution.py:63
  210.5 25.9 %collective-permute-start.31 = (bf16[512,1024]{0,1:T(8,128)(2,1)}, bf16[512,1024]{0,1:T(8,128)(2,1)}, u32[]{:S(2)}, u32[]{:S(2)}) collective-permute-start(bf16[512,1024]{0,1:T(8,128)(2,1)} %pad_maximum_fusion.7), channel_id=1, source_target_pairs={{0,1},{1,0},{2,3},{3,2},{4,5},{5,4},{6,7},{7,6},{8,9},{9,8},{10,11... | collective-permute-start | bytes 3145736 | tf_op jit(solution)/shard_map/ppermute | solution.py:63
  215.9 23.7 %collective-permute-start.32 = (bf16[512,1024]{0,1:T(8,128)(2,1)}, bf16[512,1024]{0,1:T(8,128)(2,1)}, u32[]{:S(2)}, u32[]{:S(2)}) collective-permute-start(bf16[512,1024]{0,1:T(8,128)(2,1)} %constant_dynamic-update-slice_fusion.41), channel_id=1, source_target_pairs={{0,1},{1,0},{2,3},{3,2},{4,5},{5,4},{6,7},{7,6},{8,9},{9,8},{10,11... | collective-permute-start | bytes 3145736 | tf_op jit(solution)/shard_map/ppermute | solution.py:63
  303.3 94.5 %reduce-scatter.6.cloned.1.call-start = ((), (), s32[]{:S(2)}) async-start(), calls=%async_computation.7 | async-start | bytes 1310720 | tf_op jit(solution)/shard_map/reduce_scatter | solution.py:378
  306.0 15.8 %collective-permute-start.45 = (bf16[512,1024]{0,1:T(8,128)(2,1)S(1)}, bf16[512,1024]{0,1:T(8,128)(2,1)S(1)}, u32[]{:S(2)}, u32[]{:S(2)}) collective-permute-start(bf16[512,1024]{0,1:T(8,128)(2,1)S(1)} %convolution_convert_fusion), channel_id=1, source_target_pairs={{0,1},{1,0},{2,3},{3,2},{4,5},{5,4},{6,7},{7,6},{8,9},{9,8},{10,11... | collective-permute-start | bytes 3145736 | tf_op jit(solution)/shard_map/ppermute | solution.py:63
  330.8 155.4 %reduce-scatter.8.cloned.1.call-start = ((), (), s32[]{:S(2)}) async-start(), calls=%async_computation.8 | async-start | bytes 983040 | tf_op jit(solution)/shard_map/reduce_scatter | solution.py:378
  330.9 17.5 %collective-permute-start.74 = (bf16[512,1024]{0,1:T(8,128)(2,1)}, bf16[512,1024]{0,1:T(8,128)(2,1)S(1)}, u32[]{:S(2)}, u32[]{:S(2)}) collective-permute-start(bf16[512,1024]{0,1:T(8,128)(2,1)} %constant_dynamic-update-slice_fusion.44), channel_id=1, source_target_pairs={{0,1},{1,0},{2,3},{3,2},{4,5},{5,4},{6,7},{7,6},{8,9},{9,8},{10,11... | collective-permute-start | bytes 3145736 | tf_op jit(solution)/shard_map/ppermute | solution.py:63
  371.6 58.6 %collective-permute-start.44 = (bf16[128,1024]{0,1:T(8,128)(2,1)}, bf16[128,1024]{0,1:T(8,128)(2,1)}, u32[]{:S(2)}, u32[]{:S(2)}) collective-permute-start(bf16[128,1024]{0,1:T(8,128)(2,1)} %get-tuple-element.239), channel_id=1, source_target_pairs={{0,0},{1,1},{2,10},{3,11},{4,20},{5,21},{6,30},{7,31},{8,2},{9,3},... | collective-permute-start | bytes 786440 | tf_op jit(solution)/shard_map/ppermute | solution.py:63
  397.8 15.6 %collective-permute-start.75 = (bf16[512,1024]{0,1:T(8,128)(2,1)}, bf16[512,1024]{0,1:T(8,128)(2,1)}, u32[]{:S(2)}, u32[]{:S(2)}) collective-permute-start(bf16[512,1024]{0,1:T(8,128)(2,1)} %constant_dynamic-update-slice_fusion.51), channel_id=1, source_target_pairs={{0,1},{1,0},{2,3},{3,2},{4,5},{5,4},{6,7},{7,6},{8,9},{9,8},{10,11... | collective-permute-start | bytes 3145736 | tf_op jit(solution)/shard_map/ppermute | solution.py:63
  406.7 30.5 %collective-permute-start.61 = (bf16[512,1024]{1,0:T(8,128)(2,1)}, bf16[512,1024]{1,0:T(8,128)(2,1)}, u32[]{:S(2)}, u32[]{:S(2)}) collective-permute-start(bf16[512,1024]{1,0:T(8,128)(2,1)} %convolution_convert_fusion.1), channel_id=1, source_target_pairs={{0,1},{1,0},{2,3},{3,2},{4,5},{5,4},{6,7},{7,6},{8,9},{9,8},{10,11... | collective-permute-start | bytes 3145736 | tf_op jit(solution)/shard_map/ppermute | solution.py:63
  410.2 16.6 %collective-permute-start.54 = (bf16[128,2816]{1,0:T(8,128)(2,1)S(1)}, bf16[128,2816]{1,0:T(8,128)(2,1)S(1)}, u32[]{:S(2)}, u32[]{:S(2)}) collective-permute-start(bf16[128,2816]{1,0:T(8,128)(2,1)S(1)} %collective-permute-done.52.refs_1_), channel_id=1, source_target_pairs={{0,16},{1,9},{2,18},{3,11},{4,20},{5,13},{6,22},{7,15},{8,24},{9,1... | collective-permute-start | bytes 2162696 | tf_op jit(solution)/shard_map/ppermute | solution.py:63
  440.1 21.5 %collective-permute-start.62 = (bf16[256,1024]{1,0:T(8,128)(2,1)}, bf16[256,1024]{1,0:T(8,128)(2,1)}, u32[]{:S(2)}, u32[]{:S(2)}) collective-permute-start(bf16[256,1024]{1,0:T(8,128)(2,1)} %slice.1387), channel_id=1, source_target_pairs={{0,16},{1,9},{2,18},{3,11},{4,20},{5,13},{6,22},{7,15},{8,24},{9,1... | collective-permute-start | bytes 1572872 | tf_op jit(solution)/shard_map/ppermute | solution.py:63
  443.1 21.6 %collective-permute-start.78 = (bf16[256,256]{1,0:T(8,128)(2,1)S(1)}, bf16[256,256]{1,0:T(8,128)(2,1)S(1)}, u32[]{:S(2)}, u32[]{:S(2)}) collective-permute-start(bf16[256,256]{1,0:T(8,128)(2,1)S(1)} %fusion.166), channel_id=1, source_target_pairs={{0,0},{1,1},{2,8},{3,9},{4,16},{5,17},{6,24},{7,25},{8,10},{9,11},... | collective-permute-start | bytes 393224 | tf_op jit(solution)/shard_map/ppermute | solution.py:63
  462.9 17.1 %collective-permute-start.63 = (bf16[128,1024]{1,0:T(8,128)(2,1)S(1)}, bf16[128,1024]{1,0:T(8,128)(2,1)S(1)}, u32[]{:S(2)}, u32[]{:S(2)}) collective-permute-start(bf16[128,1024]{1,0:T(8,128)(2,1)S(1)} %slice.1392), channel_id=1, source_target_pairs={{0,8},{1,17},{2,10},{3,19},{4,12},{5,21},{6,14},{7,23},{8,0},{9,25... | collective-permute-start | bytes 786440 | tf_op jit(solution)/shard_map/ppermute | solution.py:63
  469.2 16.7 %collective-permute-start.58 = (bf16[128,1024]{0,1:T(8,128)(2,1)}, bf16[128,1024]{0,1:T(8,128)(2,1)}, u32[]{:S(2)}, u32[]{:S(2)}) collective-permute-start(bf16[128,1024]{0,1:T(8,128)(2,1)} %fusion.90), channel_id=1, source_target_pairs={{0,0},{1,1},{2,10},{3,11},{4,20},{5,21},{6,30},{7,31},{8,2},{9,3},... | collective-permute-start | bytes 786440 | tf_op jit(solution)/shard_map/ppermute | solution.py:63
  480.1 26.4 %collective-permute-start.64 = (bf16[128,1024]{1,0:T(8,128)(2,1)S(1)}, bf16[128,1024]{1,0:T(8,128)(2,1)S(1)}, u32[]{:S(2)}, u32[]{:S(2)}) collective-permute-start(bf16[128,1024]{1,0:T(8,128)(2,1)S(1)} %fusion.102), channel_id=1, source_target_pairs={{0,0},{1,1},{2,10},{3,11},{4,20},{5,21},{6,30},{7,31},{8,2},{9,3},... | collective-permute-start | bytes 786440 | tf_op jit(solution)/shard_map/ppermute | solution.py:63
  (221 other events, 2364.3 us)
Sparse Core Ops, SparseCore 0:
  16.2 47.3 all-gather.3
  76.3 40.5 all-gather.5
  157.0 58.8 all-gather.7
  303.4 40.9 reduce-scatter.3
  346.6 26.2 reduce-scatter.5
  456.8 22.4 reduce-scatter.7

commit v2 on v1

--- a/solution.py
+++ b/solution.py
@@ -89,62 +89,28 @@
     def reverse(self, p):
         return sum(1 << (self.K - 1 - i) for i in range(self.K) if p >> i & 1)
 
-    def gather(self, x, axis=0):
+    def gather(self, *xs):
+        xs = list(xs)
         for i in range(self.K):
-            x = jnp.concatenate([x, self.step(x, i)], axis=axis)
-        return x, self.core(x)
-
-    def by_rank(self, blocks, r, c):
-        near, far = blocks[: self.R], blocks[self.R :]
-        even = [jnp.where(c == 0, n, f) for n, f in zip(near, far)]
-        odd = [jnp.where(c == 0, f, n) for n, f in zip(near, far)]
-        even = ordered(even, r)
-        odd = ordered([odd[self.reverse(p)] for p in range(self.R)], r)
-        return [b for pair in zip(even, odd) for b in pair]
-
-    def by_distance(self, blocks, r, c):
-        even = ordered(blocks[0::2], r)
-        odd = ordered(blocks[1::2], r)
-        odd = [odd[self.reverse(p)] for p in range(self.R)]
-        near = [jnp.where(c == 0, a, b) for a, b in zip(even, odd)]
-        far = [jnp.where(c == 0, b, a) for a, b in zip(even, odd)]
-        return near + far
-
-    def scatter_sum(self, near, far):
-        away = self.core(far().astype(BF))
-        total = near() + away.astype(F32)
-        for i in reversed(range(self.K)):
-            half = total.shape[0] // 2
-            got = self.step(total[half:].astype(BF), i)
-            total = total[:half] + got.astype(F32)
+            n = xs[0].shape[0]
+            got = self.step(jnp.concatenate(xs, axis=0) if len(xs) > 1 else xs[0], i)
+            got = [got[k * n : (k + 1) * n] for k in range(len(xs))]
+            if i < self.K - 1:
+                xs = [jnp.concatenate([x, g], axis=0) for x, g in zip(xs, got)]
+        far = [(self.core(x), self.core(g)) for x, g in zip(xs, got)]
+        out = [(x, g) + f for x, g, f in zip(xs, got, far)]
+        return out if len(out) > 1 else out[0]
+
+    def scatter_sum(self, term):
+        part = {}
+        for k in (1, 0):
+            away = self.core(term(2 + k).astype(BF))
+            part[k] = term(k) + away.astype(F32)
+        total = part[0] + self.step(part[1].astype(BF), self.K - 1).astype(F32)
+        for i in reversed(range(self.K - 1)):
+            n = total.shape[0] // 2
+            total = total[:n] + self.step(total[n:].astype(BF), i).astype(F32)
         return total
-
-    def to_rows(self, near, far):
-        w = near.shape[1]
-        block = {(0, 0): near, (1, 0): self.core(far)}
-        for i in reversed(range(self.K)):
-            keys = sorted(block)
-            half = block[keys[0]].shape[0] // 2
-            got = self.step(jnp.concatenate([block[k][half:] for k in keys], axis=1), i)
-            for n, (e, p) in enumerate(keys):
-                block[(e, p | 1 << i)] = got[:, n * w : (n + 1) * w]
-                block[(e, p)] = block[(e, p)][:half]
-        order = [(0, p) for p in range(self.R)] + [(1, self.reverse(p)) for p in range(self.R)]
-        return [block[k] for k in order]
-
-    def to_heads(self, blocks):
-        w = blocks[0].shape[1]
-        block = {}
-        for p in range(self.R):
-            block[(0, p)] = blocks[p]
-            block[(1, p)] = blocks[self.R + self.reverse(p)]
-        for i in range(self.K):
-            keys = sorted(k for k in block if k[1] >> i & 1)
-            got = self.step(jnp.concatenate([block.pop(k) for k in keys], axis=1), i)
-            for n, (e, p) in enumerate(keys):
-                k = (e, p ^ 1 << i)
-                block[k] = jnp.concatenate([block[k], got[:, n * w : (n + 1) * w]], axis=0)
-        return block[(0, 0)], self.core(block[(1, 0)])
 
     def gather_parts(self, x):
         parts = [x]
@@ -219,6 +185,66 @@
             v = jnp.where(index == d, parts[k ^ d], v)
         outs.append(v)
     return outs
+
+
+def pick_ffn(core, gathered, Z, own, sub, width, groups):
+    half = groups // 2
+
+    def kernel(core_ref, in_ref, up_ref, down_ref):
+        core = core_ref[0]
+        for s in range(2 * Z):
+            up_ref[pl.ds(s * own, own)] = in_ref[core, pl.ds(s * 2 * own, own)]
+        for z in range(Z):
+            for g in range(groups):
+                row = pl.multiple_of((z * 2 + core) * 2 * own + own + (g % half) * sub, 16)
+                piece = in_ref[g // half, pl.ds(row, sub)]
+                down_ref[pl.ds(z * sub, sub), pl.ds(g * width, width)] = piece
+
+    D = gathered.shape[1] // 2
+    vmem = pl.BlockSpec(memory_space=pltpu.VMEM)
+    return pl.pallas_call(
+        kernel,
+        out_shape=[jax.ShapeDtypeStruct((D, width), BF), jax.ShapeDtypeStruct((width, D), BF)],
+        in_specs=[pl.BlockSpec(memory_space=pltpu.SMEM), vmem],
+        out_specs=[vmem, vmem],
+        compiler_params=pltpu.CompilerParams(vmem_limit_bytes=24 << 20),
+        cost_estimate=pl.CostEstimate(flops=0, transcendentals=0, bytes_accessed=8 << 20),
+    )(core, gathered)
+
+
+def place_ffn(core, gathered, R, Z, own, sub, width, groups):
+    D = groups * width
+    shapes = [(own, 2 * R * width), (R * sub, D)]
+    gathered = gathered.reshape(R, 2, 2 * own, 2 * width)
+    if sub % 128 != 0:
+        up = lax.dynamic_slice_in_dim(gathered, core[0] * own, own, 2)[..., :width]
+        up = up.reshape(R, 2, own, Z, sub).transpose(2, 3, 1, 0, 4).reshape(shapes[0])
+        down = lax.dynamic_index_in_dim(gathered, core[0], 1, False)[..., width:]
+        down = down.reshape(R, groups, sub, width).transpose(0, 2, 1, 3).reshape(shapes[1])
+        return up.astype(F32), down.astype(F32)
+
+    def kernel(core_ref, in_ref, up_ref, down_ref):
+        me = core_ref[0]
+        rows = pl.ds(pl.multiple_of(me * own, own), own)
+        for j in range(R):
+            for cc in range(2):
+                for o in range(Z):
+                    col = ((o * 2 + cc) * R + j) * sub
+                    piece = in_ref[j, cc, rows, pl.ds(o * sub, sub)]
+                    up_ref[:, pl.ds(col, sub)] = piece.astype(F32)
+            for g in range(groups):
+                piece = in_ref[j, me, pl.ds(g * sub, sub), pl.ds(width, width)]
+                down_ref[pl.ds(j * sub, sub), pl.ds(g * width, width)] = piece.astype(F32)
+
+    vmem = pl.BlockSpec(memory_space=pltpu.VMEM)
+    return pl.pallas_call(
+        kernel,
+        out_shape=[jax.ShapeDtypeStruct(shape, F32) for shape in shapes],
+        in_specs=[pl.BlockSpec(memory_space=pltpu.SMEM), vmem],
+        out_specs=[vmem, vmem],
+        compiler_params=pltpu.CompilerParams(vmem_limit_bytes=32 << 20),
+        cost_estimate=pl.CostEstimate(flops=0, transcendentals=0, bytes_accessed=8 << 20),
+    )(core, gathered)
 
 
 def place_blocks(links, here, parts, cuts, shapes):
@@ -289,15 +315,20 @@
             full = lax.all_gather(cut, ("z", "c"), axis=1, tiled=True)
             return lax.dynamic_index_in_dim(full, c, 0, False)
 
-        cut_self = chip_columns(jnp.concatenate([self_qkv, self_out], axis=1), rank_cols)
-        w_self = gather_layers(after(cut_self, x_low))
-        self_out_part = w_self[:, 3 * rank_cols :]
-        w_self = w_self[:, : 3 * rank_cols]
-        cut_cross = chip_columns(jnp.concatenate([cross_q, cross_kv, cross_out], axis=1), rank_cols)
-        w_cross = gather_layers(after(cut_cross, w_self))
+        w_out = jnp.concatenate([self_out, cross_out], axis=0)
+        w_out = lax.dynamic_slice_in_dim(w_out, (r ^ z) * quarter, quarter, 1)
+        w_out = links.from_plane(w_out).reshape(2, own, quarter)
+        cut_self = jnp.concatenate([chip_columns(self_qkv, rank_cols), w_out], axis=2)
+        w_self = lax.all_gather(after(cut_self, x_low), ("z", "c"), axis=1, tiled=True)
+        w_out = w_self[:, :, 3 * rank_cols :].reshape(2, Z, 2, own, quarter)
+        w_out = lax.dynamic_index_in_dim(w_out, c, 2, False)
+        w_self_out = jnp.concatenate([w_out[0, i] for i in range(Z)], axis=1)
+        w_cross_out = jnp.concatenate([w_out[1, i] for i in range(Z)], axis=1)
+        w_self = lax.dynamic_index_in_dim(w_self[:, :, : 3 * rank_cols], c, 0, False)
+        cut_cross = chip_columns(jnp.concatenate([cross_q, cross_kv], axis=1), rank_cols)
+        w_cross = gather_layers(after(cut_cross, x_low))
         w_cross_q = w_cross[:, :rank_cols]
-        w_cross_kv = w_cross[:, rank_cols : 3 * rank_cols]
-        cross_out_part = w_cross[:, 3 * rank_cols :]
+        w_cross_kv = w_cross[:, rank_cols:]
         width = Z * sub
         groups = D // width
         cut_up = lax.dynamic_index_in_dim(ffn_in.reshape(own, Z, 2, R, sub), r, 3, False)
@@ -306,15 +337,9 @@
         cut_down = jnp.concatenate(
             [cut_down[:, g * width : (g + 1) * width] for g in range(groups)], axis=0
         ).reshape(2, own, width)
-        cut_ffn = after(jnp.concatenate([cut_up, cut_down], axis=2), w_cross)
+        cut_ffn = after(jnp.concatenate([cut_up, cut_down], axis=1), x_low)
         w_ffn = lax.all_gather(cut_ffn, ("z", "c"), axis=1, tiled=True)
-        w_up = lax.dynamic_index_in_dim(w_ffn[:, :, :width], c, 0, False)
-        w_down = w_ffn[:, :, width:].reshape(2, Z, 2, groups // 2, sub, width)
-        w_down = lax.dynamic_index_in_dim(w_down, c, 2, False)
-        w_down = jnp.concatenate(
-            [w_down[g // (groups // 2), :, g % (groups // 2)].reshape(width, width) for g in range(groups)],
-            axis=1,
-        )
+        w_up, w_down = pick_ffn(jnp.stack([c]).astype(jnp.int32), w_ffn, Z, own, sub, width, groups)
 
         vec = jnp.concatenate(
             [norm_gain.T, norm_bias.T, attn_bias.T, out_bias.T, ffn_in_bias.reshape(up_rows, own)],
@@ -338,41 +363,22 @@
 
         pos = jnp.concatenate([chunks(c), chunks(1 - c)])
         pos = (pos[:, None] * rows + jnp.arange(rows, dtype=jnp.int32)[None, :]).reshape(-1)
-        half = R * rows
-
-        def both(f, pair):
-            return f(pair[0]), f(pair[1])
-
-        def join(pair):
-            return jnp.concatenate(pair, axis=0)
-
-        def halves(v):
-            return v[:half], v[half:]
+        piece = R * rows // 2
+
+        def each(f, pieces):
+            return [f(v) for v in pieces]
+
+        def join(pieces):
+            return jnp.concatenate(pieces, axis=0)
+
+        def cut4(v):
+            return [v[k * piece : (k + 1) * piece] for k in range(4)]
 
         def total_tn(x, y):
-            return (mm_tn(x[0], y[0]) + mm_tn(x[1], y[1])).astype(BF)
-
-        def plane_sum(x, w):
-            return links.scatter_sum(lambda: mm_nt(x[0], w), lambda: mm_nt(x[1], w))
-
-        def split(v):
-            w = v.shape[1] // (2 * R)
-            return [v[:, i * w : (i + 1) * w] for i in range(2 * R)]
-
-        def project(c_heads, w_out):
-            blocks = links.by_rank(links.to_rows(*halves(c_heads)), r, c)
-            rows_all = jnp.concatenate(blocks, axis=1)
-            near, far = mm(rows_all, w_out[0]), mm(rows_all, w_out[1])
-            return jnp.concatenate(links.by_rank(split_half(near) + split_half(far), r, c), axis=1)
-
-        def split_half(v):
-            return [v[:, i * rank_cols : (i + 1) * rank_cols] for i in range(R)]
-
-        def unproject(g, w_out):
-            g = links.by_distance(split(g), r, c)
-            near, far = jnp.concatenate(g[:R], axis=1), jnp.concatenate(g[R:], axis=1)
-            e = (mm_nt(near, w_out[0]) + mm_nt(far, w_out[1])).astype(BF)
-            return links.to_heads(links.by_distance(split(e), r, c))
+            return mm_tn(join(x), join(y)).astype(BF)
+
+        def plane_sum(x, w, product=mm_nt):
+            return links.scatter_sum(lambda k: product(x[k], w))
 
         def sum_layers(g):
             return lax.psum_scatter(g, "z", scatter_dimension=0, tiled=True)
@@ -400,29 +406,27 @@
         x = x_low.astype(F32)
         a1, n1, i1 = layer_norm(x, gains[0], shifts[0])
         a1 = links.gather(a1)
-        memory = links.to_plane(after(encoded[0], a1[0]))
-        joined = join(both(lambda v: mm(v, w_self), a1))
-        q1 = (joined[:, :rank_cols] + pair_bias[0]).astype(BF)
-        k1 = joined[:, rank_cols : 2 * rank_cols].astype(BF)
-        v1 = (joined[:, 2 * rank_cols :] + pair_bias[1]).astype(BF)
+        memory = links.to_plane(after(encoded[0], w_self))
+        joined = each(lambda v: mm(v, w_self), a1)
+        q1 = join([(v[:, :rank_cols] + pair_bias[0]).astype(BF) for v in joined])
+        k1 = join([v[:, rank_cols : 2 * rank_cols].astype(BF) for v in joined])
+        v1 = join([(v[:, 2 * rank_cols :] + pair_bias[1]).astype(BF) for v in joined])
         c1, l1 = attend(q1, k1, v1, pos, True)
-        w_self_out = links.gather(after(self_out_part, a1[1]), axis=1)
-        h1 = x + (project(c1, w_self_out) + branch[0])
+        c1 = cut4(after(c1, memory))
+        h1 = after(x + (plane_sum(c1, w_self_out, mm) + branch[0]), w_cross)
         a2, n2, i2 = layer_norm(h1, gains[1], shifts[1])
-        memory_all = links.gather(after(memory, w_self_out[0]))
-        joined = join(both(lambda v: mm(v, w_cross_kv), memory_all))
-        k2 = joined[:, :rank_cols].astype(BF)
-        v2 = (joined[:, rank_cols:] + pair_bias[3]).astype(BF)
-        a2 = links.gather(a2)
-        q2 = (join(both(lambda v: mm(v, w_cross_q), a2)) + pair_bias[2]).astype(BF)
-        c2, l2 = attend(q2, k2, v2, pos, False)
-        seed_low = links.to_plane(after(cotangent[0], a2[0]))
+        seed_low = links.to_plane(after(cotangent[0], a2))
         seed = seed_low.astype(F32)
-        w_cross_out = links.gather(after(cross_out_part, q2), axis=1)
-        h2 = h1 + (project(c2, w_cross_out) + branch[1])
+        a2, memory_all = links.gather(a2, memory)
+        joined = each(lambda v: mm(v, w_cross_kv), memory_all)
+        k2 = join([v[:, :rank_cols].astype(BF) for v in joined])
+        v2 = join([(v[:, rank_cols:] + pair_bias[3]).astype(BF) for v in joined])
+        q2 = join([(mm(v, w_cross_q) + pair_bias[2]).astype(BF) for v in a2])
+        c2, l2 = attend(after(q2, seed_low), k2, v2, pos, False)
+        c2 = cut4(after(c2, w_up, w_down))
+        h2 = h1 + (plane_sum(c2, w_cross_out, mm) + branch[1])
         a3, n3, i3 = layer_norm(h2, gains[2], shifts[2])
-        seed_all = links.gather(after(seed_low, w_cross_out[0]))
-        a3 = links.gather(a3)
+        a3, seed_all = links.gather(a3, seed_low)
 
         def feed(v, s):
             pre = mm(v, w_up) + up_bias
@@ -430,74 +434,69 @@
             slope = cdf + pre * (jnp.exp(-0.5 * pre * pre) * (0.5 / jnp.pi) ** 0.5)
             return (pre * cdf).astype(BF), (slope * mm_nt(s, w_down)).astype(BF)
 
-        fed = [feed(a3[0], seed_all[0]), feed(a3[1], seed_all[1])]
-        act = fed[0][0], fed[1][0]
-        gz = fed[0][1], fed[1][1]
+        fed = [feed(a3[k], seed_all[k]) for k in range(4)]
+        act = [f[0] for f in fed]
+        gz = [f[1] for f in fed]
 
         lifted, s3, t3 = norm_backward(plane_sum(gz, w_up), n3, i3, gains[2])
-        down_grad = total_tn(act, seed_all)
-        up_grad = total_tn(a3, gz)
-        d2 = seed + lifted
+        act_all, seed_rows = join(act), join(seed_all)
+        down_grad = [
+            mm_tn(act_all, seed_rows[:, g * width : (g + 1) * width]).astype(BF).reshape(Z, sub, width)
+            for g in range(groups)
+        ]
+        down_grad = jnp.stack(down_grad, axis=1).reshape(D, width)
+        ffn_grad = jnp.concatenate([total_tn(a3, gz), down_grad], axis=1)
+        d2 = after(seed + lifted, ffn_grad)
+        ffn_grad = sum_layers(ffn_grad)
         g2 = d2.astype(BF)
-        e2 = unproject(g2, w_cross_out)
-        gq2, gk2, gv2 = attend_back(q2, k2, v2, join(e2), l2, pos, False)
-        g2_all = links.gather(after(g2, e2[1]))
-        output = (h2 + (plane_sum(act, after(w_down, g2_all[0]).T) + branch[2])).astype(BF)
-        output = links.from_plane(output)
-        cross_out_grad = total_tn(halves(c2), g2_all)
+        g2_all = links.gather(g2)
+        e2 = join([mm_nt(v, w_cross_out).astype(BF) for v in g2_all])
+        gq2, gk2, gv2 = attend_back(q2, k2, v2, e2, l2, pos, False)
+        output = (h2 + (plane_sum(act, after(w_down, g2_all[0]), mm) + branch[2])).astype(BF)
+        cross_out_grad = total_tn(c2, g2_all)
         pair2 = jnp.concatenate([gk2, gv2], axis=1)
         cross_grad = jnp.concatenate(
-            [total_tn(a2, halves(gq2)), total_tn(memory_all, halves(pair2))], axis=1
-        )
-        lifted, s2, t2 = norm_backward(plane_sum(halves(gq2), w_cross_q), n2, i2, gains[1])
-        d1 = d2 + lifted
+            [mm_tn(join(a2), gq2).astype(BF), mm_tn(join(memory_all), pair2).astype(BF)], axis=1
+        )
+        lifted, s2, t2 = norm_backward(plane_sum(cut4(gq2), w_cross_q), n2, i2, gains[1])
+        output = links.from_plane(output)
+        d1 = after(d2 + lifted, cross_grad, cross_out_grad, ffn_grad, output)
         g1 = d1.astype(BF)
-        e1 = unproject(g1, w_self_out)
-        up_width, cross_width = width, 3 * rank_cols
-        g = sum_layers(jnp.concatenate([up_grad, cross_grad], axis=1))
-        pack = to_core(g)
-        down = sum_layers(down_grad)
-        span = up_width + cross_width
-        cuts = columns(0, span, Z, sub, True, 0) + columns(up_width, span, 3, rank_cols, False, 1)
-        shapes = [(own, FF), (own, 3 * D)]
-        down_shape = (R * sub, D)
-        if sub == own:
-            pack = jnp.concatenate([pack, down], axis=1)
-            cuts.append((2, 2 * span, D, 0, lambda j, cc: (j * sub, 0)))
-            down_parts = []
-        else:
-            down_parts = links.gather_parts(after(down, e1[1]))
-        parts = links.gather_parts(after(pack, e1[1]))
-
-        gq1, gk1, gv1 = attend_back(q1, k1, v1, join(e1), l1, pos, True)
-        g1_all = links.gather(after(g1, e1[1]))
-        encoded_grad = links.from_plane(plane_sum(halves(after(pair2, g1_all[0])), w_cross_kv).astype(BF))
-        self_out_grad = total_tn(halves(c1), g1_all)
-        triple = after(jnp.concatenate([gq1, gk1, gv1], axis=1), *parts)
-        self_grad = total_tn(a1, halves(triple))
-        lifted, s1, t1 = norm_backward(plane_sum(halves(triple), w_self), n1, i1, gains[0])
-        hidden_grad = links.from_plane((d1 + lifted).astype(BF))
-
-        if sub == own:
-            ffn_in_grad, cross_both, ffn_out_grad = place(parts, r, cuts, shapes + [down_shape])
-        else:
-            ffn_in_grad, cross_both = place(parts, r, cuts, shapes)
-            cuts = [(0, 0, D, 0, lambda j, cc: (j * sub, 0))]
-            (ffn_out_grad,) = place(down_parts, r, cuts, [down_shape])
+        g1_all = links.gather(g1)
+        e1 = join([mm_nt(v, w_self_out).astype(BF) for v in g1_all])
+        gq1, gk1, gv1 = attend_back(q1, k1, v1, e1, l1, pos, True)
+        encoded_grad = plane_sum(cut4(after(pair2, g1_all[0])), w_cross_kv).astype(BF)
+
+        ffn_all = lax.all_gather(ffn_grad, ("r", "c"), axis=0, tiled=True)
+        ffn_in_grad, ffn_out_grad = place_ffn(
+            jnp.stack([c]).astype(jnp.int32), ffn_all, R, Z, own, sub, width, groups
+        )
+        triple = after(jnp.concatenate([gq1, gk1, gv1], axis=1), encoded_grad)
+        self_grad = mm_tn(join(a1), triple).astype(BF)
+        self_out_grad = total_tn(c1, g1_all)
+        triple = after(triple, self_grad)
+        lifted, s1, t1 = norm_backward(plane_sum(cut4(triple), w_self), n1, i1, gains[0])
+        encoded_grad = links.from_plane(encoded_grad)
+        hidden_grad = links.from_plane((after(d1, encoded_grad, ffn_in_grad) + lifted).astype(BF))
+
+        out_grad = jnp.concatenate([cross_out_grad, self_out_grad], axis=0)
+        out_grad = out_grad.reshape(2 * rank_cols, Z, quarter).transpose(1, 0, 2).reshape(D, quarter)
+        span = 6 * rank_cols
+        pack = sum_layers(jnp.concatenate([cross_grad, self_grad, out_grad], axis=1))
+        out_grad = pack[:, span:]
+        pack = links.gather_parts(to_core(after(pack[:, :span], hidden_grad)))
+        cross_both, self_qkv_grad = place(
+            pack,
+            r,
+            columns(0, span, 3, rank_cols, False, 0)
+            + columns(3 * rank_cols, span, 3, rank_cols, False, 1),
+            [(own, 3 * D), (own, 3 * D)],
+        )
         cross_q_grad = cross_both[:, :D]
         cross_kv_grad = cross_both[:, D:]
-        pack = to_core(sum_layers(self_grad))
-        (self_qkv_grad,) = place(
-            links.gather_parts(pack),
-            r,
-            columns(0, 3 * rank_cols, 3, rank_cols, False, 0),
-            [(own, 3 * D)],
-        )
-        g = jnp.concatenate([cross_out_grad, self_out_grad], axis=0)
-        g = g.reshape(2 * rank_cols, Z, quarter).transpose(1, 0, 2)
-        g = links.to_plane(links.scatter_layers(g, z))
+        out_parts = links.gather_parts(links.to_plane(after(out_grad, hidden_grad)))
         (both_out,) = place(
-            links.gather_parts(g),
+            out_parts,
             r ^ z,
             [(0, 0, quarter, 0, lambda j, cc: (0, j * quarter))],
             [(2 * rank_cols, D)],
@@ -516,7 +515,7 @@
                 jnp.zeros((v.shape[0], D), F32), v, (zero, rank * rank_cols)
             )
 
-        up_sums = (col_sum(gz[0]) + col_sum(gz[1])).reshape(Z, 1, 1, sub)
+        up_sums = sum(col_sum(v) for v in gz).reshape(Z, 1, 1, sub)
         up_sums = lax.dynamic_update_slice(jnp.zeros((Z, 2, R, sub), F32), up_sums, (zero, c, r, zero))
         up_sums = up_sums.reshape(2 * Z, up_rows, own).transpose(1, 0, 2).reshape(up_rows, D)
         sums = jnp.concatenate(

time: 536 us -> 517 us (0.965)
  waiting for transfers between devices: 153 us -> 127 us
  starting transfers between devices: 141 us -> 153 us
    ppermute x82 -> x75, waiting for transfers between devices: 149 us -> 115 us  [go(): return lax.ppermute(x, AXES, pairs)]
    dot_general x22 -> x16, matrix products: 36.8 us -> 24.4 us  [mm_tn(): lax.dot_general(a, b, (((0,), (0,)), ((), ())), preferred_element_type=F32)]
    ppermute x82 -> x75, starting transfers between devices: 141 us -> 152 us  [go(): return lax.ppermute(x, AXES, pairs)]
    dot_general x24 -> x38, matrix products: 30 us -> 39.5 us  [mm_nt(): lax.dot_general(a, b, (((1,), (1,)), ((), ())), preferred_element_type=F32)]
    slice x24 -> x21, local copies, waits for them, and re-layouts: 15.2 us -> 6.35 us  [the longest x7 1.64 us: scatter_sum(): total = total[:n] + self.step(total[n:].astype(BF), i).astype(F32)]
    all_gather x0 -> x1, local copies, waits for them, and re-layouts: none -> 6.41 us  [on_device(): ffn_all = lax.all_gather(ffn_grad, ('r', 'c'), axis=0, tiled=True)]
    all_gather x1, waiting for transfers between devices: 0.02 us -> 6.4 us  [on_device(): w_ffn = lax.all_gather(cut_ffn, ('z', 'c'), axis=1, tiled=True)]
    all_gather x0 -> x2, waiting for transfers between devices: none -> 5.85 us  [the longest x1 5.83 us: on_device(): lax.all_gather(after(cut_self, x_low), ('z', 'c'), axis=1, tiled=True)]
  transfers between devices with their start and end apart: 88 -> 81, of which waited for: 41 -> 36; matrix products, arithmetic and copies ran while one was open for 31% -> 33% of each run, Pallas kernels for 1% -> 1%
where the time goes in v2:
time: 517 us; the launch traced here: 508 us
  starting transfers between devices  153 us (30%)
  waiting for transfers between devices  127 us (25%)
  matrix products  84.4 us (16%)
  local copies, waits for them, and re-layouts  72.6 us (14%)
  other arithmetic  47.9 us (9%)
  between operations  17.3 us (3%)
  Pallas kernels  5.22 us (1%)
    ppermute x75, starting transfers between devices, go(): return lax.ppermute(x, AXES, pairs)  152 us
    ppermute x75, waiting for transfers between devices, go(): return lax.ppermute(x, AXES, pairs)  115 us
    dot_general x38, matrix products, mm_nt(): lax.dot_general(a, b, (((1,), (1,)), ((), ())), preferred_element_type=F32)  39.5 us
    unnamed x295, local copies, waits for them, and re-layouts  29.3 us
    dot_general x16, matrix products, mm_tn(): lax.dot_general(a, b, (((0,), (0,)), ((), ())), preferred_element_type=F32)  24.4 us
    dot_general x36, matrix products, mm(): return jnp.dot(a, b, preferred_element_type=F32)  20.5 us
  transfers between devices with their start and end apart: 81, of which 36 were waited for; matrix products, arithmetic and copies ran while one was open for 33% of the time, Pallas kernels for 1%

profile of v2, /device:TPU:0, one launch (start us, length us, event | category | flops | bytes accessed | tf_op | source)
XLA Modules:
  0.0 507.8 jit_solution(12456635966857114221)
XLA Ops:
  21.7 12.8 %collective-permute-start.2 = (bf16[17,256]{1,0:T(8,128)(2,1)S(1)}, bf16[17,256]{1,0:T(8,128)(2,1)S(1)}, u32[]{:S(2)}, u32[]{:S(2)}) collective-permute-start(bf16[17,256]{1,0:T(8,128)(2,1)S(1)} %pad_maximum_fusion.39), channel_id=1, source_target_pairs={{0,2},{1,3},{2,0},{3,1},{4,6},{5,7},{6,4},{7,5},{8,10},{9,11},{10,... | collective-permute-start | bytes 26120 | tf_op jit(solution)/shard_map/ppermute | solution.py:63
  36.3 4.7 collective-permute-done.3
  42.5 8.2 %collective-permute-start.4 = (bf16[128,1024]{1,0:T(8,128)(2,1)S(1)}, bf16[128,1024]{1,0:T(8,128)(2,1)S(1)}, u32[]{:S(2)}, u32[]{:S(2)}) collective-permute-start(bf16[128,1024]{1,0:T(8,128)(2,1)S(1)} %get-tuple-element.90), channel_id=1, source_target_pairs={{0,8},{1,17},{2,10},{3,19},{4,12},{5,21},{6,14},{7,23},{8,0},{9,25... | collective-permute-start | bytes 786440 | tf_op jit(solution)/shard_map/ppermute | solution.py:63
  56.5 7.8 %collective-permute-done.6 = bf16[256,1024]{1,0:T(8,128)(2,1)S(1)} collective-permute-done((bf16[256,1024]{1,0:T(8,128)(2,1)S(1)}, bf16[256,1024]{1,0:T(8,128)(2,1)S(1)}, u32[]{:S(2)}, u32[]{:S(2)}) %collective-permute-start.6) | collective-permute-done | bytes 524320 | tf_op jit(solution)/shard_map/ppermute | solution.py:63
  65.4 5.8 %all-gather.5.cloned.1.call-done = bf16[2,1024,640]{1,2,0:T(8,128)(2,1)} async-done(((bf16[2,128,640]{1,2,0:T(8,128)(2,1)}), bf16[2,1024,640]{1,2,0:T(8,128)(2,1)}) %all-gather.5.cloned.1.call-update) | async-done | bytes 2621456 | tf_op jit(solution)/shard_map/all_gather | solution.py:322
  96.9 15.9 %collective-permute-start.12 = (bf16[256,1024]{1,0:T(8,128)(2,1)S(1)}, bf16[256,1024]{1,0:T(8,128)(2,1)S(1)}, u32[]{:S(2)}, u32[]{:S(2)}) collective-permute-start(bf16[256,1024]{1,0:T(8,128)(2,1)S(1)} %fusion.23), channel_id=1, source_target_pairs={{0,16},{1,9},{2,18},{3,11},{4,20},{5,13},{6,22},{7,15},{8,24},{9,1... | collective-permute-start | bytes 1572872 | tf_op jit(solution)/shard_map/ppermute | solution.py:63
  112.8 7.2 %collective-permute-done.12 = bf16[256,1024]{1,0:T(8,128)(2,1)S(1)} collective-permute-done((bf16[256,1024]{1,0:T(8,128)(2,1)S(1)}, bf16[256,1024]{1,0:T(8,128)(2,1)S(1)}, u32[]{:S(2)}, u32[]{:S(2)}) %collective-permute-start.12) | collective-permute-done | bytes 524320 | tf_op jit(solution)/shard_map/ppermute | solution.py:63
  121.3 7.6 %collective-permute-start.13 = (bf16[128,1024]{1,0:T(8,128)(2,1)S(1)}, bf16[128,1024]{1,0:T(8,128)(2,1)S(1)}, u32[]{:S(2)}, u32[]{:S(2)}) collective-permute-start(bf16[128,1024]{1,0:T(8,128)(2,1)S(1)} %slice.969), channel_id=1, source_target_pairs={{0,8},{1,17},{2,10},{3,19},{4,12},{5,21},{6,14},{7,23},{8,0},{9,25... | collective-permute-start | bytes 786440 | tf_op jit(solution)/shard_map/ppermute | solution.py:63
  138.8 6.3 %collective-permute-done.14 = bf16[256,1024]{1,0:T(8,128)(2,1)S(1)} collective-permute-done((bf16[256,1024]{1,0:T(8,128)(2,1)S(1)}, bf16[256,1024]{1,0:T(8,128)(2,1)S(1)}, u32[]{:S(2)}, u32[]{:S(2)}) %collective-permute-start.14) | collective-permute-done | bytes 524320 | tf_op jit(solution)/shard_map/ppermute | solution.py:63
  154.2 6.7 %collective-permute-done.15 = bf16[512,1024]{1,0:T(8,128)(2,1)S(1)} collective-permute-done((bf16[512,1024]{1,0:T(8,128)(2,1)S(1)}, bf16[512,1024]{1,0:T(8,128)(2,1)S(1)}, u32[]{:S(2)}, u32[]{:S(2)}) %collective-permute-start.15) | collective-permute-done | bytes 1048608 | tf_op jit(solution)/shard_map/ppermute | solution.py:63
  163.3 4.7 collective-permute-start.20
  170.3 6.4 %all-gather.9.cloned.1.call-done.in_ref = bf16[2,2048,512]{2,1,0:T(8,128)(2,1)} async-done(((bf16[2,256,512]{2,1,0:T(8,128)(2,1)}), bf16[2,2048,512]{2,1,0:T(8,128)(2,1)}) %all-gather.9.cloned.1.call-update) | async-done | bytes 4194320 | tf_op jit(solution)/shard_map/all_gather | solution.py:341
  194.2 6.2 %collective-permute-done.23 = bf16[256,1024]{1,0:T(8,128)(2,1)S(1)} collective-permute-done((bf16[256,1024]{1,0:T(8,128)(2,1)S(1)}, bf16[256,1024]{1,0:T(8,128)(2,1)S(1)}, u32[]{:S(2)}, u32[]{:S(2)}) %collective-permute-start.23) | collective-permute-done | bytes 524320 | tf_op jit(solution)/shard_map/ppermute | solution.py:63
  212.2 6.3 %collective-permute-done.25 = bf16[256,1024]{1,0:T(8,128)(2,1)S(1)} collective-permute-done((bf16[256,1024]{1,0:T(8,128)(2,1)S(1)}, bf16[256,1024]{1,0:T(8,128)(2,1)S(1)}, u32[]{:S(2)}, u32[]{:S(2)}) %collective-permute-start.25) | collective-permute-done | bytes 524320 | tf_op jit(solution)/shard_map/ppermute | solution.py:63
  228.6 5.9 %collective-permute-done.29 = bf16[512,1024]{1,0:T(8,128)(2,1)S(1)} collective-permute-done((bf16[512,1024]{1,0:T(8,128)(2,1)S(1)}, bf16[512,1024]{1,0:T(8,128)(2,1)S(1)}, u32[]{:S(2)}, u32[]{:S(2)}) %collective-permute-start.29) | collective-permute-done | bytes 1048608 | tf_op jit(solution)/shard_map/ppermute | solution.py:63
  345.7 4.7 collective-permute-start.54
  353.9 9.3 %collective-permute-done.54 = bf16[256,1024]{1,0:T(8,128)(2,1)S(1)} collective-permute-done((bf16[256,1024]{1,0:T(8,128)(2,1)S(1)}, bf16[256,1024]{1,0:T(8,128)(2,1)S(1)}, u32[]{:S(2)}, u32[]{:S(2)}) %collective-permute-start.54) | collective-permute-done | bytes 524320 | tf_op jit(solution)/shard_map/ppermute | solution.py:63
  363.9 4.9 collective-permute-done.51
  393.5 7.3 %collective-permute-done.59 = bf16[256,1024]{1,0:T(8,128)(2,1)S(1)} collective-permute-done((bf16[256,1024]{1,0:T(8,128)(2,1)S(1)}, bf16[256,1024]{1,0:T(8,128)(2,1)S(1)}, u32[]{:S(2)}, u32[]{:S(2)}) %collective-permute-start.59) | collective-permute-done | bytes 524320 | tf_op jit(solution)/shard_map/ppermute | solution.py:63
  408.7 6.4 %copy.62 = bf16[2048,1024]{1,0:T(8,128)(2,1)} copy(bf16[2048,1024]{0,1:T(8,128)(2,1)} %all-gather.11.cloned.1.call-done) | data formatting | bytes 8388608 | tf_op jit(solution)/shard_map/all_gather | solution.py:470
  424.6 25.8 %collective-permute-start.63 = (f32[2,17,128]{2,0,1:T(2,128)S(1)}, f32[2,17,128]{2,0,1:T(2,128)S(1)}, u32[]{:S(2)}, u32[]{:S(2)}) collective-permute-start(f32[2,17,128]{2,0,1:T(2,128)S(1)} %constant_dynamic-slice_fusion.3), channel_id=1, source_target_pairs={{0,4},{1,5},{2,6},{3,7},{4,0},{5,1},{6,2},{7,3},{8,12},{9,13},{10,... | collective-permute-start | bytes 52232 | tf_op jit(solution)/shard_map/ppermute | solution.py:63
  455.9 9.3 %collective-permute-start.65 = (f32[17,128]{1,0:T(8,128)S(1)}, f32[17,128]{1,0:T(8,128)S(1)}, u32[]{:S(2)}, u32[]{:S(2)}) collective-permute-start(f32[17,128]{1,0:T(8,128)S(1)} %bitcast.252), channel_id=1, source_target_pairs={{0,8},{1,9},{2,10},{3,11},{4,12},{5,13},{6,14},{7,15},{8,0},{9,1},... | collective-permute-start | bytes 26120 | tf_op jit(solution)/shard_map/ppermute | solution.py:63
  472.3 7.4 %collective-permute-start.72 = (bf16[256,256]{1,0:T(8,128)(2,1)S(1)}, bf16[256,256]{1,0:T(8,128)(2,1)S(1)}, u32[]{:S(2)}, u32[]{:S(2)}) collective-permute-start(bf16[256,256]{1,0:T(8,128)(2,1)S(1)} %collective-permute-done.71.refs_0_), channel_id=1, source_target_pairs={{0,8},{1,17},{2,10},{3,19},{4,12},{5,21},{6,14},{7,23},{8,0},{9,25... | collective-permute-start | bytes 393224 | tf_op jit(solution)/shard_map/ppermute | solution.py:63
  486.4 4.5 collective-permute-done.74.refs_3_
  (710 shorter events, 298.5 us)
Async XLA Ops:
  7.2 64.1 %all-gather.5.cloned.1.call-start = ((), (), s32[]{:S(2)}) async-start(), calls=%async_computation.2 | async-start | bytes 2949120 | tf_op jit(solution)/shard_map/all_gather | solution.py:322
  17.9 111.1 %all-gather.7.cloned.1.call-start = ((), (), s32[]{:S(2)}) async-start(), calls=%async_computation.3 | async-start | bytes 1769472 | tf_op jit(solution)/shard_map/all_gather | solution.py:315
  20.9 155.8 %all-gather.9.cloned.1.call-start = ((), (), s32[]{:S(2)}) async-start(), calls=%async_computation.4 | async-start | bytes 4718592 | tf_op jit(solution)/shard_map/all_gather | solution.py:341
  21.7 14.4 %collective-permute-start.2 = (bf16[17,256]{1,0:T(8,128)(2,1)S(1)}, bf16[17,256]{1,0:T(8,128)(2,1)S(1)}, u32[]{:S(2)}, u32[]{:S(2)}) collective-permute-start(bf16[17,256]{1,0:T(8,128)(2,1)S(1)} %pad_maximum_fusion.39), channel_id=1, source_target_pairs={{0,2},{1,3},{2,0},{3,1},{4,6},{5,7},{6,4},{7,5},{8,10},{9,11},{10,... | collective-permute-start | bytes 26120 | tf_op jit(solution)/shard_map/ppermute | solution.py:63
  56.4 273.1 %reduce-scatter.3.cloned.1.call-start = ((), (), s32[]{:S(2)}) async-start(), calls=%async_computation.5 | async-start | bytes 2621440 | tf_op jit(solution)/shard_map/reduce_scatter | solution.py:384
  95.2 17.6 %collective-permute-start.10 = (bf16[256,1024]{1,0:T(8,128)(2,1)S(1)}, bf16[256,1024]{1,0:T(8,128)(2,1)S(1)}, u32[]{:S(2)}, u32[]{:S(2)}) collective-permute-start(bf16[256,1024]{1,0:T(8,128)(2,1)S(1)} %convolution_convert_fusion.18), channel_id=1, source_target_pairs={{0,1},{1,0},{2,3},{3,2},{4,5},{5,4},{6,7},{7,6},{8,9},{9,8},{10,11... | collective-permute-start | bytes 1572872 | tf_op jit(solution)/shard_map/ppermute | solution.py:63
  96.9 23.1 %collective-permute-start.12 = (bf16[256,1024]{1,0:T(8,128)(2,1)S(1)}, bf16[256,1024]{1,0:T(8,128)(2,1)S(1)}, u32[]{:S(2)}, u32[]{:S(2)}) collective-permute-start(bf16[256,1024]{1,0:T(8,128)(2,1)S(1)} %fusion.23), channel_id=1, source_target_pairs={{0,16},{1,9},{2,18},{3,11},{4,20},{5,13},{6,22},{7,15},{8,24},{9,1... | collective-permute-start | bytes 1572872 | tf_op jit(solution)/shard_map/ppermute | solution.py:63
  146.0 14.9 %collective-permute-start.15 = (bf16[512,1024]{1,0:T(8,128)(2,1)S(1)}, bf16[512,1024]{1,0:T(8,128)(2,1)S(1)}, u32[]{:S(2)}, u32[]{:S(2)}) collective-permute-start(bf16[512,1024]{1,0:T(8,128)(2,1)S(1)} %pad_maximum_fusion.2), channel_id=1, source_target_pairs={{0,16},{1,9},{2,18},{3,11},{4,20},{5,13},{6,22},{7,15},{8,24},{9,1... | collective-permute-start | bytes 3145736 | tf_op jit(solution)/shard_map/ppermute | solution.py:63
  146.2 36.7 %collective-permute-start.18 = (bf16[128,1024]{1,0:T(8,128)(2,1)}, bf16[128,1024]{1,0:T(8,128)(2,1)}, u32[]{:S(2)}, u32[]{:S(2)}) collective-permute-start(bf16[128,1024]{1,0:T(8,128)(2,1)} %bitcast.30), channel_id=1, source_target_pairs={{0,0},{1,1},{2,8},{3,9},{4,16},{5,17},{6,24},{7,25},{8,10},{9,11},... | collective-permute-start | bytes 786440 | tf_op jit(solution)/shard_map/ppermute | solution.py:63
  151.5 16.4 %collective-permute-start.16 = (bf16[256,1024]{1,0:T(8,128)(2,1)S(1)}, bf16[256,1024]{1,0:T(8,128)(2,1)S(1)}, u32[]{:S(2)}, u32[]{:S(2)}) collective-permute-start(bf16[256,1024]{1,0:T(8,128)(2,1)S(1)} %pad_maximum_fusion.8), channel_id=1, source_target_pairs={{0,1},{1,0},{2,3},{3,2},{4,5},{5,4},{6,7},{7,6},{8,9},{9,8},{10,11... | collective-permute-start | bytes 1572872 | tf_op jit(solution)/shard_map/ppermute | solution.py:63
  163.3 17.7 %collective-permute-start.20 = (bf16[256,1024]{1,0:T(8,128)(2,1)}, bf16[256,1024]{1,0:T(8,128)(2,1)}, u32[]{:S(2)}, u32[]{:S(2)}) collective-permute-start(bf16[256,1024]{1,0:T(8,128)(2,1)} %get-tuple-element.99), channel_id=1, source_target_pairs={{0,1},{1,0},{2,3},{3,2},{4,5},{5,4},{6,7},{7,6},{8,9},{9,8},{10,11... | collective-permute-start | bytes 1572872 | tf_op jit(solution)/shard_map/ppermute | solution.py:63
  219.7 14.9 %collective-permute-start.29 = (bf16[512,1024]{1,0:T(8,128)(2,1)S(1)}, bf16[512,1024]{1,0:T(8,128)(2,1)S(1)}, u32[]{:S(2)}, u32[]{:S(2)}) collective-permute-start(bf16[512,1024]{1,0:T(8,128)(2,1)S(1)} %pad_maximum_fusion.3), channel_id=1, source_target_pairs={{0,16},{1,9},{2,18},{3,11},{4,20},{5,13},{6,22},{7,15},{8,24},{9,1... | collective-permute-start | bytes 3145736 | tf_op jit(solution)/shard_map/ppermute | solution.py:63
  228.6 28.7 %collective-permute-start.28 = (bf16[256,1024]{1,0:T(8,128)(2,1)}, bf16[256,1024]{1,0:T(8,128)(2,1)}, u32[]{:S(2)}, u32[]{:S(2)}) collective-permute-start(bf16[256,1024]{1,0:T(8,128)(2,1)} %convolution_convert_fusion.9), channel_id=1, source_target_pairs={{0,1},{1,0},{2,3},{3,2},{4,5},{5,4},{6,7},{7,6},{8,9},{9,8},{10,11... | collective-permute-start | bytes 1572872 | tf_op jit(solution)/shard_map/ppermute | solution.py:63
  242.4 14.9 %collective-permute-start.33 = (bf16[256,1024]{1,0:T(8,128)(2,1)}, bf16[256,1024]{1,0:T(8,128)(2,1)}, u32[]{:S(2)}, u32[]{:S(2)}) collective-permute-start(bf16[256,1024]{1,0:T(8,128)(2,1)} %add_convert_fusion.4), channel_id=1, source_target_pairs={{0,16},{1,9},{2,18},{3,11},{4,20},{5,13},{6,22},{7,15},{8,24},{9,1... | collective-permute-start | bytes 1572872 | tf_op jit(solution)/shard_map/ppermute | solution.py:63
  280.2 128.6 %all-gather.11.cloned.1.call-start = ((), (), s32[]{:S(2)}) async-start(), calls=%async_computation.6 | async-start | bytes 4718592 | tf_op jit(solution)/shard_map/all_gather | solution.py:470
  288.0 15.3 %collective-permute-start.36 = (bf16[256,1024]{1,0:T(8,128)(2,1)S(1)}, bf16[256,1024]{1,0:T(8,128)(2,1)S(1)}, u32[]{:S(2)}, u32[]{:S(2)}) collective-permute-start(bf16[256,1024]{1,0:T(8,128)(2,1)S(1)} %convolution_convert_fusion.7), channel_id=1, source_target_pairs={{0,1},{1,0},{2,3},{3,2},{4,5},{5,4},{6,7},{7,6},{8,9},{9,8},{10,11... | collective-permute-start | bytes 1572872 | tf_op jit(solution)/shard_map/ppermute | solution.py:63
  303.9 19.9 %collective-permute-start.39 = (bf16[128,1024]{1,0:T(8,128)(2,1)S(1)}, bf16[128,1024]{1,0:T(8,128)(2,1)S(1)}, u32[]{:S(2)}, u32[]{:S(2)}) collective-permute-start(bf16[128,1024]{1,0:T(8,128)(2,1)S(1)} %slice.966), channel_id=1, source_target_pairs={{0,8},{1,17},{2,10},{3,19},{4,12},{5,21},{6,14},{7,23},{8,0},{9,25... | collective-permute-start | bytes 786440 | tf_op jit(solution)/shard_map/ppermute | solution.py:63
  337.8 115.3 %reduce-scatter.5.cloned.1.call-start = ((), (), s32[]{:S(2)}) async-start(), calls=%async_computation.7 | async-start | bytes 2621440 | tf_op jit(solution)/shard_map/reduce_scatter | solution.py:384
  345.7 17.5 %collective-permute-start.54 = (bf16[256,1024]{1,0:T(8,128)(2,1)S(1)}, bf16[256,1024]{1,0:T(8,128)(2,1)S(1)}, u32[]{:S(2)}, u32[]{:S(2)}) collective-permute-start(bf16[256,1024]{1,0:T(8,128)(2,1)S(1)} %pad_maximum_fusion.17), channel_id=1, source_target_pairs={{0,16},{1,9},{2,18},{3,11},{4,20},{5,13},{6,22},{7,15},{8,24},{9,1... | collective-permute-start | bytes 1572872 | tf_op jit(solution)/shard_map/ppermute | solution.py:63
  353.8 15.0 %collective-permute-start.51 = (bf16[256,1024]{1,0:T(8,128)(2,1)S(1)}, bf16[256,1024]{1,0:T(8,128)(2,1)S(1)}, u32[]{:S(2)}, u32[]{:S(2)}) collective-permute-start(bf16[256,1024]{1,0:T(8,128)(2,1)S(1)} %add_convert_fusion.1), channel_id=1, source_target_pairs={{0,16},{1,9},{2,18},{3,11},{4,20},{5,13},{6,22},{7,15},{8,24},{9,1... | collective-permute-start | bytes 1572872 | tf_op jit(solution)/shard_map/ppermute | solution.py:63
  369.1 14.8 %collective-permute-start.52 = (bf16[128,1024]{1,0:T(8,128)(2,1)S(1)}, bf16[128,1024]{1,0:T(8,128)(2,1)S(1)}, u32[]{:S(2)}, u32[]{:S(2)}) collective-permute-start(bf16[128,1024]{1,0:T(8,128)(2,1)S(1)} %slice.964), channel_id=1, source_target_pairs={{0,8},{1,17},{2,10},{3,19},{4,12},{5,21},{6,14},{7,23},{8,0},{9,25... | collective-permute-start | bytes 786440 | tf_op jit(solution)/shard_map/ppermute | solution.py:63
  403.3 16.5 %collective-permute-start.53 = (bf16[128,1024]{1,0:T(8,128)(2,1)}, bf16[128,1024]{1,0:T(8,128)(2,1)S(1)}, u32[]{:S(2)}, u32[]{:S(2)}) collective-permute-start(bf16[128,1024]{1,0:T(8,128)(2,1)} %fusion.101), channel_id=1, source_target_pairs={{0,0},{1,1},{2,10},{3,11},{4,20},{5,21},{6,30},{7,31},{8,2},{9,3},... | collective-permute-start | bytes 786440 | tf_op jit(solution)/shard_map/ppermute | solution.py:63
  424.6 27.6 %collective-permute-start.63 = (f32[2,17,128]{2,0,1:T(2,128)S(1)}, f32[2,17,128]{2,0,1:T(2,128)S(1)}, u32[]{:S(2)}, u32[]{:S(2)}) collective-permute-start(f32[2,17,128]{2,0,1:T(2,128)S(1)} %constant_dynamic-slice_fusion.3), channel_id=1, source_target_pairs={{0,4},{1,5},{2,6},{3,7},{4,0},{5,1},{6,2},{7,3},{8,12},{9,13},{10,... | collective-permute-start | bytes 52232 | tf_op jit(solution)/shard_map/ppermute | solution.py:63
  470.5 15.3 %collective-permute-start.68 = (bf16[128,1536]{1,0:T(8,128)(2,1)S(1)}, bf16[128,1536]{1,0:T(8,128)(2,1)S(1)}, u32[]{:S(2)}, u32[]{:S(2)}) collective-permute-start(bf16[128,1536]{1,0:T(8,128)(2,1)S(1)} %pad_maximum_fusion.20.refs_0_), channel_id=1, source_target_pairs={{0,8},{1,17},{2,10},{3,19},{4,12},{5,21},{6,14},{7,23},{8,0},{9,25... | collective-permute-start | bytes 1179656 | tf_op jit(solution)/shard_map/ppermute | solution.py:63
  (193 other events, 1336.0 us)
Sparse Core Ops, SparseCore 0:
  18.0 53.2 all-gather.4
  73.4 40.7 all-gather.6
  116.4 60.2 all-gather.8
  280.3 45.1 reduce-scatter.2
  337.9 49.3 all-gather.10
  389.5 43.8 reduce-scatter.4

commit v3 on v2

--- a/solution.py
+++ b/solution.py
@@ -2,6 +2,7 @@
 import jax.numpy as jnp
 from jax import lax
 from jax.experimental import pallas as pl
+from jax.experimental.layout import Layout, with_layout_constraint
 from jax.experimental.pallas import tpu as pltpu
 from jax.sharding import Mesh
 from jax.sharding import PartitionSpec as P
@@ -111,6 +112,16 @@
             n = total.shape[0] // 2
             total = total[:n] + self.step(total[n:].astype(BF), i).astype(F32)
         return total
+
+    def spread_chips(self, blocks):
+        held = [(p, b) for p, b in enumerate(blocks)]
+        for i in range(self.K):
+            away = [m for m, (left, _) in enumerate(held) if left >> i & 1]
+            n = held[0][1].shape[0]
+            got = self.step(jnp.concatenate([held[m][1] for m in away], axis=0), i)
+            for k, m in enumerate(away):
+                held[m] = (held[m][0] ^ 1 << i, got[k * n : (k + 1) * n])
+        return [b for _, b in held]
 
     def gather_parts(self, x):
         parts = [x]
@@ -150,7 +161,7 @@
     return jnp.concatenate(outs, axis=1), lses
 
 
-def attend_back(q, k, v, e, lses, pos, causal):
+def attend_back(q, k, v, e, context, lses, pos, causal):
     heads = q.shape[1] // HEAD_DIM
     dqs, dks, dvs = [], [], []
     for h in range(heads):
@@ -160,7 +171,7 @@
             s = jnp.where(pos[:, None] >= pos[None, :], s, -1e30)
         p = jnp.exp(s - lses[h])
         dp = mm_nt(e[:, cut], v[:, cut])
-        inner = jnp.sum(dp * p, axis=-1, keepdims=True)
+        inner = jnp.sum(e[:, cut].astype(F32) * context[:, cut].astype(F32), axis=-1, keepdims=True)
         ds = (p * (dp - inner)).astype(BF)
         dqs.append((mm(ds, k[:, cut]) * HEAD_DIM ** (-0.5)).astype(BF))
         dks.append((mm_tn(ds, q[:, cut]) * HEAD_DIM ** (-0.5)).astype(BF))
@@ -446,12 +457,12 @@
         ]
         down_grad = jnp.stack(down_grad, axis=1).reshape(D, width)
         ffn_grad = jnp.concatenate([total_tn(a3, gz), down_grad], axis=1)
-        d2 = after(seed + lifted, ffn_grad)
+        d2 = seed + lifted
         ffn_grad = sum_layers(ffn_grad)
         g2 = d2.astype(BF)
         g2_all = links.gather(g2)
         e2 = join([mm_nt(v, w_cross_out).astype(BF) for v in g2_all])
-        gq2, gk2, gv2 = attend_back(q2, k2, v2, e2, l2, pos, False)
+        gq2, gk2, gv2 = attend_back(q2, k2, v2, e2, join(c2), l2, pos, False)
         output = (h2 + (plane_sum(act, after(w_down, g2_all[0]), mm) + branch[2])).astype(BF)
         cross_out_grad = total_tn(c2, g2_all)
         pair2 = jnp.concatenate([gk2, gv2], axis=1)
@@ -459,34 +470,43 @@
             [mm_tn(join(a2), gq2).astype(BF), mm_tn(join(memory_all), pair2).astype(BF)], axis=1
         )
         lifted, s2, t2 = norm_backward(plane_sum(cut4(gq2), w_cross_q), n2, i2, gains[1])
-        output = links.from_plane(output)
         d1 = after(d2 + lifted, cross_grad, cross_out_grad, ffn_grad, output)
         g1 = d1.astype(BF)
         g1_all = links.gather(g1)
         e1 = join([mm_nt(v, w_self_out).astype(BF) for v in g1_all])
-        gq1, gk1, gv1 = attend_back(q1, k1, v1, e1, l1, pos, True)
-        encoded_grad = plane_sum(cut4(after(pair2, g1_all[0])), w_cross_kv).astype(BF)
-
+        gq1, gk1, gv1 = attend_back(q1, k1, v1, e1, join(c1), l1, pos, True)
+        encoded_grad = plane_sum(cut4(after(pair2, g1_all[3])), w_cross_kv).astype(BF)
+
+        ffn_grad = with_layout_constraint(ffn_grad, Layout((0, 1)))
         ffn_all = lax.all_gather(ffn_grad, ("r", "c"), axis=0, tiled=True)
         ffn_in_grad, ffn_out_grad = place_ffn(
             jnp.stack([c]).astype(jnp.int32), ffn_all, R, Z, own, sub, width, groups
         )
-        triple = after(jnp.concatenate([gq1, gk1, gv1], axis=1), encoded_grad)
+        output = links.from_plane(output)
+        triple = after(jnp.concatenate([gq1, gk1, gv1], axis=1), encoded_grad, output)
         self_grad = mm_tn(join(a1), triple).astype(BF)
         self_out_grad = total_tn(c1, g1_all)
+        out_grad = jnp.concatenate([cross_out_grad, self_out_grad], axis=0)
+        far_chip = [jnp.where(c == 0, links.offset(p, 0), links.offset(p, 1)) for p in range(R)]
+        out_grad = links.spread_chips(
+            [lax.dynamic_slice_in_dim(out_grad, (r ^ f) * quarter, quarter, 1) for f in far_chip]
+        )
+        turned = [out_grad[links.reverse(p)] for p in range(R)]
+        out_grad = ordered([jnp.where(c == 0, p, t) for p, t in zip(out_grad, turned)], r)
+        out_grad = lax.optimization_barrier(jnp.concatenate(lax.optimization_barrier(out_grad), axis=0))
         triple = after(triple, self_grad)
         lifted, s1, t1 = norm_backward(plane_sum(cut4(triple), w_self), n1, i1, gains[0])
-        encoded_grad = links.from_plane(encoded_grad)
-        hidden_grad = links.from_plane((after(d1, encoded_grad, ffn_in_grad) + lifted).astype(BF))
-
-        out_grad = jnp.concatenate([cross_out_grad, self_out_grad], axis=0)
-        out_grad = out_grad.reshape(2 * rank_cols, Z, quarter).transpose(1, 0, 2).reshape(D, quarter)
+        hidden_grad = links.from_plane((after(d1, ffn_in_grad) + lifted).astype(BF))
+        encoded_grad = links.from_plane(after(encoded_grad, hidden_grad))
+
         span = 6 * rank_cols
         pack = sum_layers(jnp.concatenate([cross_grad, self_grad, out_grad], axis=1))
+        pack = after(pack, hidden_grad)
         out_grad = pack[:, span:]
-        pack = links.gather_parts(to_core(after(pack[:, :span], hidden_grad)))
+        pack = [to_core(pack[:, :span]), out_grad[:own], out_grad[own:]]
+        parts = links.gather_parts(jnp.concatenate(pack, axis=1))
         cross_both, self_qkv_grad = place(
-            pack,
+            parts,
             r,
             columns(0, span, 3, rank_cols, False, 0)
             + columns(3 * rank_cols, span, 3, rank_cols, False, 1),
@@ -494,14 +514,12 @@
         )
         cross_q_grad = cross_both[:, :D]
         cross_kv_grad = cross_both[:, D:]
-        out_parts = links.gather_parts(links.to_plane(after(out_grad, hidden_grad)))
-        (both_out,) = place(
-            out_parts,
-            r ^ z,
-            [(0, 0, quarter, 0, lambda j, cc: (0, j * quarter))],
-            [(2 * rank_cols, D)],
-        )
-        cross_out_grad, self_out_grad = both_out[:rank_cols], both_out[rank_cols:]
+        cross_out_grad, self_out_grad = place(
+            parts,
+            r,
+            [(i, 2 * span + i * quarter, quarter, 0, lambda j, cc: (0, j * quarter)) for i in range(2)],
+            [(own, D), (own, D)],
+        )
 
         def sum_small(v):
             k = v.shape[0]

time: 517 us -> 503 us (0.973)
  the two profiles are of different devices: /device:TPU:0 before, /device:TPU:8 now
where the time goes in v3:
time: 503 us; the launch traced here: 494 us
  waiting for transfers between devices  226 us (45%)
  starting transfers between devices  81.2 us (16%)
  matrix products  78.1 us (16%)
  local copies, waits for them, and re-layouts  51.2 us (10%)
  other arithmetic  33.8 us (7%)
  between operations  17.5 us (3%)
  Pallas kernels  6.19 us (1%)
    ppermute x73, waiting for transfers between devices, go(): return lax.ppermute(x, AXES, pairs)  215 us
    ppermute x73, starting transfers between devices, go(): return lax.ppermute(x, AXES, pairs)  80.8 us
    dot_general x38, matrix products, mm_nt(): lax.dot_general(a, b, (((1,), (1,)), ((), ())), preferred_element_type=F32)  31.7 us
    unnamed x293, local copies, waits for them, and re-layouts  28.9 us
    dot_general x36, matrix products, mm(): return jnp.dot(a, b, preferred_element_type=F32)  26.5 us
    dot_general x16, matrix products, mm_tn(): lax.dot_general(a, b, (((0,), (0,)), ((), ())), preferred_element_type=F32)  20 us
  transfers between devices with their start and end apart: 79, of which 42 were waited for; matrix products, arithmetic and copies ran while one was open for 26% of the time, Pallas kernels for 1%

profile of v3, /device:TPU:8, one launch (start us, length us, event | category | flops | bytes accessed | tf_op | source)
XLA Modules:
  0.0 494.2 jit_solution(12734852183049687869)
XLA Ops:
  18.7 13.1 %collective-permute-done = bf16[128,1024]{1,0:T(8,128)(2,1)S(1)} collective-permute-done((bf16[128,1024]{1,0:T(8,128)(2,1)}, bf16[128,1024]{1,0:T(8,128)(2,1)S(1)}, u32[]{:S(2)}, u32[]{:S(2)}) %collective-permute-start) | collective-permute-done | bytes 262176 | tf_op jit(solution)/shard_map/ppermute | solution.py:64
  59.3 6.7 %collective-permute-done.6 = bf16[256,1024]{1,0:T(8,128)(2,1)S(1)} collective-permute-done((bf16[256,1024]{1,0:T(8,128)(2,1)}, bf16[256,1024]{1,0:T(8,128)(2,1)S(1)}, u32[]{:S(2)}, u32[]{:S(2)}) %collective-permute-start.6) | collective-permute-done | bytes 524320 | tf_op jit(solution)/shard_map/ppermute | solution.py:64
  75.5 6.5 %collective-permute-start.9 = (bf16[128,1024]{1,0:T(8,128)(2,1)}, bf16[128,1024]{1,0:T(8,128)(2,1)S(1)}, u32[]{:S(2)}, u32[]{:S(2)}) collective-permute-start(bf16[128,1024]{1,0:T(8,128)(2,1)} %bitcast.16), channel_id=1, source_target_pairs={{0,0},{1,1},{2,8},{3,9},{4,16},{5,17},{6,24},{7,25},{8,10},{9,11},... | collective-permute-start | bytes 786440 | tf_op jit(solution)/shard_map/ppermute | solution.py:64
  92.8 16.9 %collective-permute-done.9 = bf16[128,1024]{1,0:T(8,128)(2,1)S(1)} collective-permute-done((bf16[128,1024]{1,0:T(8,128)(2,1)}, bf16[128,1024]{1,0:T(8,128)(2,1)S(1)}, u32[]{:S(2)}, u32[]{:S(2)}) %collective-permute-start.9) | collective-permute-done | bytes 262176 | tf_op jit(solution)/shard_map/ppermute | solution.py:64
  114.6 8.1 %collective-permute-done.12 = bf16[256,1024]{1,0:T(8,128)(2,1)} collective-permute-done((bf16[256,1024]{1,0:T(8,128)(2,1)}, bf16[256,1024]{1,0:T(8,128)(2,1)}, u32[]{:S(2)}, u32[]{:S(2)}) %collective-permute-start.12) | collective-permute-done | bytes 524320 | tf_op jit(solution)/shard_map/ppermute | solution.py:64
  136.1 6.9 %collective-permute-done.14 = bf16[256,1024]{1,0:T(8,128)(2,1)S(1)} collective-permute-done((bf16[256,1024]{1,0:T(8,128)(2,1)S(1)}, bf16[256,1024]{1,0:T(8,128)(2,1)S(1)}, u32[]{:S(2)}, u32[]{:S(2)}) %collective-permute-start.14) | collective-permute-done | bytes 524320 | tf_op jit(solution)/shard_map/ppermute | solution.py:64
  143.9 5.4 %collective-permute-start.18 = (bf16[128,1024]{1,0:T(8,128)(2,1)}, bf16[128,1024]{1,0:T(8,128)(2,1)}, u32[]{:S(2)}, u32[]{:S(2)}) collective-permute-start(bf16[128,1024]{1,0:T(8,128)(2,1)} %bitcast.30), channel_id=1, source_target_pairs={{0,0},{1,1},{2,8},{3,9},{4,16},{5,17},{6,24},{7,25},{8,10},{9,11},... | collective-permute-start | bytes 786440 | tf_op jit(solution)/shard_map/ppermute | solution.py:64
  153.2 7.9 %collective-permute-done.15 = bf16[512,1024]{1,0:T(8,128)(2,1)S(1)} collective-permute-done((bf16[512,1024]{1,0:T(8,128)(2,1)S(1)}, bf16[512,1024]{1,0:T(8,128)(2,1)S(1)}, u32[]{:S(2)}, u32[]{:S(2)}) %collective-permute-start.15) | collective-permute-done | bytes 1048608 | tf_op jit(solution)/shard_map/ppermute | solution.py:64
  166.7 7.2 %all-gather.9.cloned.1.call-done.in_ref = bf16[2,2048,512]{2,1,0:T(8,128)(2,1)} async-done(((bf16[2,256,512]{2,1,0:T(8,128)(2,1)}), bf16[2,2048,512]{2,1,0:T(8,128)(2,1)}) %all-gather.9.cloned.1.call-update) | async-done | bytes 4194320 | tf_op jit(solution)/shard_map/all_gather | solution.py:352
  194.1 5.1 %collective-permute-done.23 = bf16[256,1024]{1,0:T(8,128)(2,1)S(1)} collective-permute-done((bf16[256,1024]{1,0:T(8,128)(2,1)S(1)}, bf16[256,1024]{1,0:T(8,128)(2,1)S(1)}, u32[]{:S(2)}, u32[]{:S(2)}) %collective-permute-start.23) | collective-permute-done | bytes 524320 | tf_op jit(solution)/shard_map/ppermute | solution.py:64
  210.9 5.9 %collective-permute-done.25 = bf16[256,1024]{1,0:T(8,128)(2,1)S(1)} collective-permute-done((bf16[256,1024]{1,0:T(8,128)(2,1)S(1)}, bf16[256,1024]{1,0:T(8,128)(2,1)S(1)}, u32[]{:S(2)}, u32[]{:S(2)}) %collective-permute-start.25) | collective-permute-done | bytes 524320 | tf_op jit(solution)/shard_map/ppermute | solution.py:64
  225.5 9.5 %collective-permute-done.29 = bf16[512,1024]{1,0:T(8,128)(2,1)S(1)} collective-permute-done((bf16[512,1024]{1,0:T(8,128)(2,1)S(1)}, bf16[512,1024]{1,0:T(8,128)(2,1)S(1)}, u32[]{:S(2)}, u32[]{:S(2)}) %collective-permute-start.29) | collective-permute-done | bytes 1048608 | tf_op jit(solution)/shard_map/ppermute | solution.py:64
  243.9 7.8 %collective-permute-done.33 = bf16[256,1024]{1,0:T(8,128)(2,1)S(1)} collective-permute-done((bf16[256,1024]{1,0:T(8,128)(2,1)S(1)}, bf16[256,1024]{1,0:T(8,128)(2,1)S(1)}, u32[]{:S(2)}, u32[]{:S(2)}) %collective-permute-start.33) | collective-permute-done | bytes 524320 | tf_op jit(solution)/shard_map/ppermute | solution.py:64
  253.0 5.5 %collective-permute-done.34 = bf16[128,1024]{1,0:T(8,128)(2,1)S(1)} collective-permute-done((bf16[128,1024]{1,0:T(8,128)(2,1)S(1)}, bf16[128,1024]{1,0:T(8,128)(2,1)S(1)}, u32[]{:S(2)}, u32[]{:S(2)}) %collective-permute-start.34) | collective-permute-done | bytes 262176 | tf_op jit(solution)/shard_map/ppermute | solution.py:64
  300.0 7.5 %collective-permute-done.46 = bf16[256,1024]{1,0:T(8,128)(2,1)S(1)} collective-permute-done((bf16[256,1024]{1,0:T(8,128)(2,1)S(1)}, bf16[256,1024]{1,0:T(8,128)(2,1)S(1)}, u32[]{:S(2)}, u32[]{:S(2)}) %collective-permute-start.46) | collective-permute-done | bytes 524320 | tf_op jit(solution)/shard_map/ppermute | solution.py:64
  309.3 4.9 %collective-permute-done.47 = bf16[128,1024]{1,0:T(8,128)(2,1)S(1)} collective-permute-done((bf16[128,1024]{1,0:T(8,128)(2,1)S(1)}, bf16[128,1024]{1,0:T(8,128)(2,1)S(1)}, u32[]{:S(2)}, u32[]{:S(2)}) %collective-permute-start.47) | collective-permute-done | bytes 262176 | tf_op jit(solution)/shard_map/ppermute | solution.py:64
  349.6 6.3 %collective-permute-start.68 = (bf16[512,256]{1,0:T(8,128)(2,1)S(1)}, bf16[512,256]{1,0:T(8,128)(2,1)S(1)}, u32[]{:S(2)}, u32[]{:S(2)}) collective-permute-start(bf16[512,256]{1,0:T(8,128)(2,1)S(1)} %pad_maximum_fusion.36), channel_id=1, source_target_pairs={{0,16},{1,9},{2,18},{3,11},{4,20},{5,13},{6,22},{7,15},{8,24},{9,1... | collective-permute-start | bytes 786440 | tf_op jit(solution)/shard_map/ppermute | solution.py:64
  361.1 15.6 %collective-permute-done.54 = bf16[256,1024]{1,0:T(8,128)(2,1)S(1)} collective-permute-done((bf16[256,1024]{1,0:T(8,128)(2,1)S(1)}, bf16[256,1024]{1,0:T(8,128)(2,1)S(1)}, u32[]{:S(2)}, u32[]{:S(2)}) %collective-permute-start.54) | collective-permute-done | bytes 524320 | tf_op jit(solution)/shard_map/ppermute | solution.py:64
  378.1 5.4 %collective-permute-done.55 = bf16[128,1024]{1,0:T(8,128)(2,1)S(1)} collective-permute-done((bf16[128,1024]{1,0:T(8,128)(2,1)S(1)}, bf16[128,1024]{1,0:T(8,128)(2,1)S(1)}, u32[]{:S(2)}, u32[]{:S(2)}) %collective-permute-start.55) | collective-permute-done | bytes 262176 | tf_op jit(solution)/shard_map/ppermute | solution.py:64
  396.1 6.6 %collective-permute-done.58 = bf16[256,1024]{1,0:T(8,128)(2,1)S(1)} collective-permute-done((bf16[256,1024]{1,0:T(8,128)(2,1)S(1)}, bf16[256,1024]{1,0:T(8,128)(2,1)S(1)}, u32[]{:S(2)}, u32[]{:S(2)}) %collective-permute-start.58) | collective-permute-done | bytes 524320 | tf_op jit(solution)/shard_map/ppermute | solution.py:64
  418.2 13.6 %collective-permute-done.60 = bf16[128,1024]{1,0:T(8,128)(2,1)S(1)} collective-permute-done((bf16[128,1024]{1,0:T(8,128)(2,1)S(1)}, bf16[128,1024]{1,0:T(8,128)(2,1)S(1)}, u32[]{:S(2)}, u32[]{:S(2)}) %collective-permute-start.60) | collective-permute-done | bytes 262176 | tf_op jit(solution)/shard_map/ppermute | solution.py:64
  441.8 10.9 %collective-permute-start.65 = (f32[17,128]{1,0:T(8,128)S(1)}, f32[17,128]{1,0:T(8,128)S(1)}, u32[]{:S(2)}, u32[]{:S(2)}) collective-permute-start(f32[17,128]{1,0:T(8,128)S(1)} %bitcast.247), channel_id=1, source_target_pairs={{0,8},{1,9},{2,10},{3,11},{4,12},{5,13},{6,14},{7,15},{8,0},{9,1},... | collective-permute-start | bytes 26120 | tf_op jit(solution)/shard_map/ppermute | solution.py:64
  464.4 7.3 %collective-permute-done.70.refs_1_ = bf16[128,2048]{1,0:T(8,128)(2,1)S(1)} collective-permute-done((bf16[128,2048]{1,0:T(8,128)(2,1)S(1)}, bf16[128,2048]{1,0:T(8,128)(2,1)S(1)}, u32[]{:S(2)}, u32[]{:S(2)}) %collective-permute-start.70) | collective-permute-done | bytes 524320 | tf_op jit(solution)/shard_map/ppermute | solution.py:64
  475.0 5.9 %collective-permute-done.72.refs_3_ = bf16[128,2048]{1,0:T(8,128)(2,1)S(1)} collective-permute-done((bf16[128,2048]{1,0:T(8,128)(2,1)S(1)}, bf16[128,2048]{1,0:T(8,128)(2,1)S(1)}, u32[]{:S(2)}, u32[]{:S(2)}) %collective-permute-start.72) | collective-permute-done | bytes 524320 | tf_op jit(solution)/shard_map/ppermute | solution.py:64
  (699 shorter events, 280.3 us)
Async XLA Ops:
  7.2 62.9 %all-gather.5.cloned.1.call-start = ((), (), s32[]{:S(2)}) async-start(), calls=%async_computation.2 | async-start | bytes 2949120 | tf_op jit(solution)/shard_map/all_gather | solution.py:333
  11.6 20.2 %collective-permute-start = (bf16[128,1024]{1,0:T(8,128)(2,1)}, bf16[128,1024]{1,0:T(8,128)(2,1)S(1)}, u32[]{:S(2)}, u32[]{:S(2)}) collective-permute-start(bf16[128,1024]{1,0:T(8,128)(2,1)} %bitcast.258), channel_id=1, source_target_pairs={{0,0},{1,1},{2,8},{3,9},{4,16},{5,17},{6,24},{7,25},{8,10},{9,11},... | collective-permute-start | bytes 786440 | tf_op jit(solution)/shard_map/ppermute | solution.py:64
  31.8 94.9 %all-gather.7.cloned.1.call-start = ((), (), s32[]{:S(2)}) async-start(), calls=%async_computation.3 | async-start | bytes 1769472 | tf_op jit(solution)/shard_map/all_gather | solution.py:326
  35.3 138.6 %all-gather.9.cloned.1.call-start = ((), (), s32[]{:S(2)}) async-start(), calls=%async_computation.4 | async-start | bytes 4718592 | tf_op jit(solution)/shard_map/all_gather | solution.py:352
  58.7 256.2 %reduce-scatter.3.cloned.1.call-start = ((), (), s32[]{:S(2)}) async-start(), calls=%async_computation.5 | async-start | bytes 2621440 | tf_op jit(solution)/shard_map/reduce_scatter | solution.py:395
  75.5 34.2 %collective-permute-start.9 = (bf16[128,1024]{1,0:T(8,128)(2,1)}, bf16[128,1024]{1,0:T(8,128)(2,1)S(1)}, u32[]{:S(2)}, u32[]{:S(2)}) collective-permute-start(bf16[128,1024]{1,0:T(8,128)(2,1)} %bitcast.16), channel_id=1, source_target_pairs={{0,0},{1,1},{2,8},{3,9},{4,16},{5,17},{6,24},{7,25},{8,10},{9,11},... | collective-permute-start | bytes 786440 | tf_op jit(solution)/shard_map/ppermute | solution.py:64
  143.2 17.9 %collective-permute-start.15 = (bf16[512,1024]{1,0:T(8,128)(2,1)S(1)}, bf16[512,1024]{1,0:T(8,128)(2,1)S(1)}, u32[]{:S(2)}, u32[]{:S(2)}) collective-permute-start(bf16[512,1024]{1,0:T(8,128)(2,1)S(1)} %pad_maximum_fusion.2), channel_id=1, source_target_pairs={{0,16},{1,9},{2,18},{3,11},{4,20},{5,13},{6,22},{7,15},{8,24},{9,1... | collective-permute-start | bytes 3145736 | tf_op jit(solution)/shard_map/ppermute | solution.py:64
  143.9 36.2 %collective-permute-start.18 = (bf16[128,1024]{1,0:T(8,128)(2,1)}, bf16[128,1024]{1,0:T(8,128)(2,1)}, u32[]{:S(2)}, u32[]{:S(2)}) collective-permute-start(bf16[128,1024]{1,0:T(8,128)(2,1)} %bitcast.30), channel_id=1, source_target_pairs={{0,0},{1,1},{2,8},{3,9},{4,16},{5,17},{6,24},{7,25},{8,10},{9,11},... | collective-permute-start | bytes 786440 | tf_op jit(solution)/shard_map/ppermute | solution.py:64
  150.6 14.4 %collective-permute-start.16 = (bf16[256,1024]{1,0:T(8,128)(2,1)S(1)}, bf16[256,1024]{1,0:T(8,128)(2,1)S(1)}, u32[]{:S(2)}, u32[]{:S(2)}) collective-permute-start(bf16[256,1024]{1,0:T(8,128)(2,1)S(1)} %pad_maximum_fusion.8), channel_id=1, source_target_pairs={{0,1},{1,0},{2,3},{3,2},{4,5},{5,4},{6,7},{7,6},{8,9},{9,8},{10,11... | collective-permute-start | bytes 1572872 | tf_op jit(solution)/shard_map/ppermute | solution.py:64
  163.2 15.1 %collective-permute-start.20 = (bf16[256,1024]{1,0:T(8,128)(2,1)}, bf16[256,1024]{1,0:T(8,128)(2,1)}, u32[]{:S(2)}, u32[]{:S(2)}) collective-permute-start(bf16[256,1024]{1,0:T(8,128)(2,1)} %get-tuple-element.116), channel_id=1, source_target_pairs={{0,1},{1,0},{2,3},{3,2},{4,5},{5,4},{6,7},{7,6},{8,9},{9,8},{10,11... | collective-permute-start | bytes 1572872 | tf_op jit(solution)/shard_map/ppermute | solution.py:64
  220.2 14.9 %collective-permute-start.29 = (bf16[512,1024]{1,0:T(8,128)(2,1)S(1)}, bf16[512,1024]{1,0:T(8,128)(2,1)S(1)}, u32[]{:S(2)}, u32[]{:S(2)}) collective-permute-start(bf16[512,1024]{1,0:T(8,128)(2,1)S(1)} %pad_maximum_fusion.3), channel_id=1, source_target_pairs={{0,16},{1,9},{2,18},{3,11},{4,20},{5,13},{6,22},{7,15},{8,24},{9,1... | collective-permute-start | bytes 3145736 | tf_op jit(solution)/shard_map/ppermute | solution.py:64
  225.4 18.5 %collective-permute-start.28 = (bf16[256,1024]{1,0:T(8,128)(2,1)S(1)}, bf16[256,1024]{1,0:T(8,128)(2,1)S(1)}, u32[]{:S(2)}, u32[]{:S(2)}) collective-permute-start(bf16[256,1024]{1,0:T(8,128)(2,1)S(1)} %convolution_convert_fusion.9), channel_id=1, source_target_pairs={{0,1},{1,0},{2,3},{3,2},{4,5},{5,4},{6,7},{7,6},{8,9},{9,8},{10,11... | collective-permute-start | bytes 1572872 | tf_op jit(solution)/shard_map/ppermute | solution.py:64
  263.6 146.2 %all-gather.11.cloned.1.call-start = ((), (), s32[]{:S(2)}) async-start(), calls=%async_computation.6 | async-start | bytes 4718592 | tf_op jit(solution)/shard_map/all_gather | solution.py:481
  287.0 21.5 %collective-permute-start.39 = (bf16[128,1024]{1,0:T(8,128)(2,1)S(1)}, bf16[128,1024]{1,0:T(8,128)(2,1)S(1)}, u32[]{:S(2)}, u32[]{:S(2)}) collective-permute-start(bf16[128,1024]{1,0:T(8,128)(2,1)S(1)} %slice.1015), channel_id=1, source_target_pairs={{0,8},{1,17},{2,10},{3,19},{4,12},{5,21},{6,14},{7,23},{8,0},{9,25... | collective-permute-start | bytes 786440 | tf_op jit(solution)/shard_map/ppermute | solution.py:64
  324.3 107.7 %reduce-scatter.5.cloned.1.call-start = ((), (), s32[]{:S(2)}) async-start(), calls=%async_computation.7 | async-start | bytes 2621440 | tf_op jit(solution)/shard_map/reduce_scatter | solution.py:395
  325.5 58.7 %collective-permute-start.40 = (bf16[128,1024]{1,0:T(8,128)(2,1)}, bf16[128,1024]{1,0:T(8,128)(2,1)S(1)}, u32[]{:S(2)}, u32[]{:S(2)}) collective-permute-start(bf16[128,1024]{1,0:T(8,128)(2,1)} %fusion.106), channel_id=1, source_target_pairs={{0,0},{1,1},{2,10},{3,11},{4,20},{5,21},{6,30},{7,31},{8,2},{9,3},... | collective-permute-start | bytes 786440 | tf_op jit(solution)/shard_map/ppermute | solution.py:64
  336.8 24.3 %collective-permute-start.52 = (bf16[256,1024]{1,0:T(8,128)(2,1)S(1)}, bf16[256,1024]{1,0:T(8,128)(2,1)S(1)}, u32[]{:S(2)}, u32[]{:S(2)}) collective-permute-start(bf16[256,1024]{1,0:T(8,128)(2,1)S(1)} %convolution_convert_fusion.5), channel_id=1, source_target_pairs={{0,1},{1,0},{2,3},{3,2},{4,5},{5,4},{6,7},{7,6},{8,9},{9,8},{10,11... | collective-permute-start | bytes 1572872 | tf_op jit(solution)/shard_map/ppermute | solution.py:64
  337.7 18.2 %collective-permute-start.53 = (bf16[256,1024]{1,0:T(8,128)(2,1)S(1)}, bf16[256,1024]{1,0:T(8,128)(2,1)S(1)}, u32[]{:S(2)}, u32[]{:S(2)}) collective-permute-start(bf16[256,1024]{1,0:T(8,128)(2,1)S(1)} %convolution_convert_fusion.4), channel_id=1, source_target_pairs={{0,1},{1,0},{2,3},{3,2},{4,5},{5,4},{6,7},{7,6},{8,9},{9,8},{10,11... | collective-permute-start | bytes 1572872 | tf_op jit(solution)/shard_map/ppermute | solution.py:64
  356.3 20.4 %collective-permute-start.54 = (bf16[256,1024]{1,0:T(8,128)(2,1)S(1)}, bf16[256,1024]{1,0:T(8,128)(2,1)S(1)}, u32[]{:S(2)}, u32[]{:S(2)}) collective-permute-start(bf16[256,1024]{1,0:T(8,128)(2,1)S(1)} %fusion.25), channel_id=1, source_target_pairs={{0,16},{1,9},{2,18},{3,11},{4,20},{5,13},{6,22},{7,15},{8,24},{9,1... | collective-permute-start | bytes 1572872 | tf_op jit(solution)/shard_map/ppermute | solution.py:64
  414.7 17.1 %collective-permute-start.60 = (bf16[128,1024]{1,0:T(8,128)(2,1)S(1)}, bf16[128,1024]{1,0:T(8,128)(2,1)S(1)}, u32[]{:S(2)}, u32[]{:S(2)}) collective-permute-start(bf16[128,1024]{1,0:T(8,128)(2,1)S(1)} %fusion.78), channel_id=1, source_target_pairs={{0,0},{1,1},{2,10},{3,11},{4,20},{5,21},{6,30},{7,31},{8,2},{9,3},... | collective-permute-start | bytes 786440 | tf_op jit(solution)/shard_map/ppermute | solution.py:64
  438.1 14.5 %collective-permute-start.69 = (bf16[128,768]{1,0:T(8,128)(2,1)S(1)}, bf16[128,768]{1,0:T(8,128)(2,1)S(1)}, u32[]{:S(2)}, u32[]{:S(2)}) collective-permute-start(bf16[128,768]{1,0:T(8,128)(2,1)S(1)} %get-tuple-element.151), channel_id=1, source_target_pairs={{0,1},{1,0},{2,3},{3,2},{4,5},{5,4},{6,7},{7,6},{8,9},{9,8},{10,11... | collective-permute-start | bytes 589832 | tf_op jit(solution)/shard_map/ppermute | solution.py:64
  441.8 15.0 %collective-permute-start.65 = (f32[17,128]{1,0:T(8,128)S(1)}, f32[17,128]{1,0:T(8,128)S(1)}, u32[]{:S(2)}, u32[]{:S(2)}) collective-permute-start(f32[17,128]{1,0:T(8,128)S(1)} %bitcast.247), channel_id=1, source_target_pairs={{0,8},{1,9},{2,10},{3,11},{4,12},{5,13},{6,14},{7,15},{8,0},{9,1},... | collective-permute-start | bytes 26120 | tf_op jit(solution)/shard_map/ppermute | solution.py:64
  452.7 18.9 %collective-permute-start.70 = (bf16[128,2048]{1,0:T(8,128)(2,1)S(1)}, bf16[128,2048]{1,0:T(8,128)(2,1)S(1)}, u32[]{:S(2)}, u32[]{:S(2)}) collective-permute-start(bf16[128,2048]{1,0:T(8,128)(2,1)S(1)} %pad_maximum_fusion.19.refs_0_), channel_id=1, source_target_pairs={{0,8},{1,17},{2,10},{3,19},{4,12},{5,21},{6,14},{7,23},{8,0},{9,25... | collective-permute-start | bytes 1572872 | tf_op jit(solution)/shard_map/ppermute | solution.py:64
  452.9 21.2 %collective-permute-start.61 = (bf16[128,1024]{1,0:T(8,128)(2,1)S(1)}, bf16[128,1024]{1,0:T(8,128)(2,1)S(1)}, u32[]{:S(2)}, u32[]{:S(2)}) collective-permute-start(bf16[128,1024]{1,0:T(8,128)(2,1)S(1)} %copy-done.78), channel_id=1, source_target_pairs={{0,0},{1,1},{2,10},{3,11},{4,20},{5,21},{6,30},{7,31},{8,2},{9,3},... | collective-permute-start | bytes 786440 | tf_op jit(solution)/shard_map/ppermute | solution.py:64
  (190 other events, 1505.7 us)
Sparse Core Ops, SparseCore 0:
  31.9 38.1 all-gather.4
  71.7 44.6 all-gather.6
  118.6 55.3 all-gather.8
  263.7 46.7 reduce-scatter.2
  324.5 54.3 all-gather.10
  389.1 41.0 reduce-scatter.4

commit v4 on v3

--- a/solution.py
+++ b/solution.py
@@ -2,7 +2,6 @@
 import jax.numpy as jnp
 from jax import lax
 from jax.experimental import pallas as pl
-from jax.experimental.layout import Layout, with_layout_constraint
 from jax.experimental.pallas import tpu as pltpu
 from jax.sharding import Mesh
 from jax.sharding import PartitionSpec as P
@@ -219,41 +218,6 @@
         in_specs=[pl.BlockSpec(memory_space=pltpu.SMEM), vmem],
         out_specs=[vmem, vmem],
         compiler_params=pltpu.CompilerParams(vmem_limit_bytes=24 << 20),
-        cost_estimate=pl.CostEstimate(flops=0, transcendentals=0, bytes_accessed=8 << 20),
-    )(core, gathered)
-
-
-def place_ffn(core, gathered, R, Z, own, sub, width, groups):
-    D = groups * width
-    shapes = [(own, 2 * R * width), (R * sub, D)]
-    gathered = gathered.reshape(R, 2, 2 * own, 2 * width)
-    if sub % 128 != 0:
-        up = lax.dynamic_slice_in_dim(gathered, core[0] * own, own, 2)[..., :width]
-        up = up.reshape(R, 2, own, Z, sub).transpose(2, 3, 1, 0, 4).reshape(shapes[0])
-        down = lax.dynamic_index_in_dim(gathered, core[0], 1, False)[..., width:]
-        down = down.reshape(R, groups, sub, width).transpose(0, 2, 1, 3).reshape(shapes[1])
-        return up.astype(F32), down.astype(F32)
-
-    def kernel(core_ref, in_ref, up_ref, down_ref):
-        me = core_ref[0]
-        rows = pl.ds(pl.multiple_of(me * own, own), own)
-        for j in range(R):
-            for cc in range(2):
-                for o in range(Z):
-                    col = ((o * 2 + cc) * R + j) * sub
-                    piece = in_ref[j, cc, rows, pl.ds(o * sub, sub)]
-                    up_ref[:, pl.ds(col, sub)] = piece.astype(F32)
-            for g in range(groups):
-                piece = in_ref[j, me, pl.ds(g * sub, sub), pl.ds(width, width)]
-                down_ref[pl.ds(j * sub, sub), pl.ds(g * width, width)] = piece.astype(F32)
-
-    vmem = pl.BlockSpec(memory_space=pltpu.VMEM)
-    return pl.pallas_call(
-        kernel,
-        out_shape=[jax.ShapeDtypeStruct(shape, F32) for shape in shapes],
-        in_specs=[pl.BlockSpec(memory_space=pltpu.SMEM), vmem],
-        out_specs=[vmem, vmem],
-        compiler_params=pltpu.CompilerParams(vmem_limit_bytes=32 << 20),
         cost_estimate=pl.CostEstimate(flops=0, transcendentals=0, bytes_accessed=8 << 20),
     )(core, gathered)
 
@@ -477,11 +441,6 @@
         gq1, gk1, gv1 = attend_back(q1, k1, v1, e1, join(c1), l1, pos, True)
         encoded_grad = plane_sum(cut4(after(pair2, g1_all[3])), w_cross_kv).astype(BF)
 
-        ffn_grad = with_layout_constraint(ffn_grad, Layout((0, 1)))
-        ffn_all = lax.all_gather(ffn_grad, ("r", "c"), axis=0, tiled=True)
-        ffn_in_grad, ffn_out_grad = place_ffn(
-            jnp.stack([c]).astype(jnp.int32), ffn_all, R, Z, own, sub, width, groups
-        )
         output = links.from_plane(output)
         triple = after(jnp.concatenate([gq1, gk1, gv1], axis=1), encoded_grad, output)
         self_grad = mm_tn(join(a1), triple).astype(BF)
@@ -496,15 +455,30 @@
         out_grad = lax.optimization_barrier(jnp.concatenate(lax.optimization_barrier(out_grad), axis=0))
         triple = after(triple, self_grad)
         lifted, s1, t1 = norm_backward(plane_sum(cut4(triple), w_self), n1, i1, gains[0])
-        hidden_grad = links.from_plane((after(d1, ffn_in_grad) + lifted).astype(BF))
+        hidden_grad = links.from_plane((d1 + lifted).astype(BF))
+        down = ffn_grad[:, width:]
+        cuts = columns(0, width, Z, sub, True, 0)
+        ffn_pack = to_core(ffn_grad[:, :width])
+        if sub == own:
+            ffn_pack = jnp.concatenate([ffn_pack, down[:own], down[own:]], axis=1)
+            cuts.append((1, 2 * width, D, 0, lambda j, cc: (j * sub, 0)))
+        ffn_parts = links.gather_parts(after(ffn_pack, lifted))
+        if sub == own:
+            ffn_in_grad, ffn_out_grad = place(ffn_parts, r, cuts, [(own, FF), (R * sub, D)])
+        else:
+            (ffn_in_grad,) = place(ffn_parts, r, cuts, [(own, FF)])
+            down = down.reshape(groups, sub, width).transpose(1, 0, 2).reshape(sub, D)
+            cuts = [(0, 0, D, 0, lambda j, cc: (j * sub, 0))]
+            (ffn_out_grad,) = place(links.gather_parts(down), r, cuts, [(R * sub, D)])
         encoded_grad = links.from_plane(after(encoded_grad, hidden_grad))
 
         span = 6 * rank_cols
         pack = sum_layers(jnp.concatenate([cross_grad, self_grad, out_grad], axis=1))
-        pack = after(pack, hidden_grad)
+        pack = after(pack, hidden_grad, *ffn_parts)
         out_grad = pack[:, span:]
         pack = [to_core(pack[:, :span]), out_grad[:own], out_grad[own:]]
         parts = links.gather_parts(jnp.concatenate(pack, axis=1))
+        parts = lax.optimization_barrier(tuple(parts) + (encoded_grad,))[:R]
         cross_both, self_qkv_grad = place(
             parts,
             r,
@@ -545,7 +519,7 @@
             ],
             axis=0,
         )
-        sums = sum_small(after(sums, hidden_grad))
+        sums = sum_small(after(sums, hidden_grad, *ffn_parts))
         return (
             output[None],
             hidden_grad.astype(F32)[None],

time: 503 us -> 493 us (0.980)
  waiting for transfers between devices: 226 us -> 205 us
  starting transfers between devices: 81.2 us -> 91.4 us
    ppermute x73 -> x77, waiting for transfers between devices: 215 us -> 195 us  [go(): return lax.ppermute(x, AXES, pairs)]
    ppermute x73 -> x77, starting transfers between devices: 80.8 us -> 91 us  [go(): return lax.ppermute(x, AXES, pairs)]
    unnamed x293 -> x283, local copies, waits for them, and re-layouts: 28.9 us -> 22.1 us
  transfers between devices with their start and end apart: 79 -> 82, of which waited for: 42 -> 44; matrix products, arithmetic and copies ran while one was open for 26% -> 27% of each run, Pallas kernels for 1% -> 1%
where the time goes in v4:
time: 493 us; the launch traced here: 484 us
  waiting for transfers between devices  205 us (42%)
  starting transfers between devices  91.4 us (19%)
  matrix products  78.9 us (16%)
  local copies, waits for them, and re-layouts  47.2 us (10%)
  other arithmetic  38.2 us (8%)
  between operations  17 us (3%)
  Pallas kernels  6.77 us (1%)
    ppermute x77, waiting for transfers between devices, go(): return lax.ppermute(x, AXES, pairs)  195 us
    ppermute x77, starting transfers between devices, go(): return lax.ppermute(x, AXES, pairs)  91 us
    dot_general x38, matrix products, mm_nt(): lax.dot_general(a, b, (((1,), (1,)), ((), ())), preferred_element_type=F32)  31.8 us
    dot_general x36, matrix products, mm(): return jnp.dot(a, b, preferred_element_type=F32)  27.1 us
    unnamed x283, local copies, waits for them, and re-layouts  22.1 us
    dot_general x16, matrix products, mm_tn(): lax.dot_general(a, b, (((0,), (0,)), ((), ())), preferred_element_type=F32)  20 us
  transfers between devices with their start and end apart: 82, of which 44 were waited for; matrix products, arithmetic and copies ran while one was open for 27% of the time, Pallas kernels for 1%

profile of v4, /device:TPU:8, one launch (start us, length us, event | category | flops | bytes accessed | tf_op | source)
XLA Modules:
  0.0 484.4 jit_solution(3194262527080458364)
XLA Ops:
  42.8 8.5 %collective-permute-start.4 = (bf16[128,1024]{1,0:T(8,128)(2,1)S(1)}, bf16[128,1024]{1,0:T(8,128)(2,1)S(1)}, u32[]{:S(2)}, u32[]{:S(2)}) collective-permute-start(bf16[128,1024]{1,0:T(8,128)(2,1)S(1)} %get-tuple-element.119), channel_id=1, source_target_pairs={{0,8},{1,17},{2,10},{3,19},{4,12},{5,21},{6,14},{7,23},{8,0},{9,25... | collective-permute-start | bytes 786440 | tf_op jit(solution)/shard_map/ppermute | solution.py:63
  57.6 8.3 %collective-permute-done.6 = bf16[256,1024]{1,0:T(8,128)(2,1)S(1)} collective-permute-done((bf16[256,1024]{1,0:T(8,128)(2,1)}, bf16[256,1024]{1,0:T(8,128)(2,1)S(1)}, u32[]{:S(2)}, u32[]{:S(2)}) %collective-permute-start.6) | collective-permute-done | bytes 524320 | tf_op jit(solution)/shard_map/ppermute | solution.py:63
  74.7 7.4 %collective-permute-start.9 = (bf16[128,1024]{1,0:T(8,128)(2,1)}, bf16[128,1024]{1,0:T(8,128)(2,1)S(1)}, u32[]{:S(2)}, u32[]{:S(2)}) collective-permute-start(bf16[128,1024]{1,0:T(8,128)(2,1)} %bitcast.16), channel_id=1, source_target_pairs={{0,0},{1,1},{2,8},{3,9},{4,16},{5,17},{6,24},{7,25},{8,10},{9,11},... | collective-permute-start | bytes 786440 | tf_op jit(solution)/shard_map/ppermute | solution.py:63
  92.9 17.0 %collective-permute-done.9 = bf16[128,1024]{1,0:T(8,128)(2,1)S(1)} collective-permute-done((bf16[128,1024]{1,0:T(8,128)(2,1)}, bf16[128,1024]{1,0:T(8,128)(2,1)S(1)}, u32[]{:S(2)}, u32[]{:S(2)}) %collective-permute-start.9) | collective-permute-done | bytes 262176 | tf_op jit(solution)/shard_map/ppermute | solution.py:63
  114.8 8.1 %collective-permute-done.12 = bf16[256,1024]{1,0:T(8,128)(2,1)} collective-permute-done((bf16[256,1024]{1,0:T(8,128)(2,1)}, bf16[256,1024]{1,0:T(8,128)(2,1)}, u32[]{:S(2)}, u32[]{:S(2)}) %collective-permute-start.12) | collective-permute-done | bytes 524320 | tf_op jit(solution)/shard_map/ppermute | solution.py:63
  136.4 6.9 %collective-permute-done.14 = bf16[256,1024]{1,0:T(8,128)(2,1)S(1)} collective-permute-done((bf16[256,1024]{1,0:T(8,128)(2,1)S(1)}, bf16[256,1024]{1,0:T(8,128)(2,1)S(1)}, u32[]{:S(2)}, u32[]{:S(2)}) %collective-permute-start.14) | collective-permute-done | bytes 524320 | tf_op jit(solution)/shard_map/ppermute | solution.py:63
  144.2 5.7 %collective-permute-start.18 = (bf16[128,1024]{1,0:T(8,128)(2,1)}, bf16[128,1024]{1,0:T(8,128)(2,1)}, u32[]{:S(2)}, u32[]{:S(2)}) collective-permute-start(bf16[128,1024]{1,0:T(8,128)(2,1)} %bitcast.30), channel_id=1, source_target_pairs={{0,0},{1,1},{2,8},{3,9},{4,16},{5,17},{6,24},{7,25},{8,10},{9,11},... | collective-permute-start | bytes 786440 | tf_op jit(solution)/shard_map/ppermute | solution.py:63
  153.0 8.3 %collective-permute-done.15 = bf16[512,1024]{1,0:T(8,128)(2,1)S(1)} collective-permute-done((bf16[512,1024]{1,0:T(8,128)(2,1)S(1)}, bf16[512,1024]{1,0:T(8,128)(2,1)S(1)}, u32[]{:S(2)}, u32[]{:S(2)}) %collective-permute-start.15) | collective-permute-done | bytes 1048608 | tf_op jit(solution)/shard_map/ppermute | solution.py:63
  167.5 5.4 %all-gather.8.cloned.1.call-done.in_ref = bf16[2,2048,512]{2,1,0:T(8,128)(2,1)} async-done(((bf16[2,256,512]{2,1,0:T(8,128)(2,1)}), bf16[2,2048,512]{2,1,0:T(8,128)(2,1)}) %all-gather.8.cloned.1.call-update) | async-done | bytes 4194320 | tf_op jit(solution)/shard_map/all_gather | solution.py:316
  199.3 5.5 %collective-permute-done.24 = bf16[128,1024]{1,0:T(8,128)(2,1)S(1)} collective-permute-done((bf16[128,1024]{1,0:T(8,128)(2,1)S(1)}, bf16[128,1024]{1,0:T(8,128)(2,1)S(1)}, u32[]{:S(2)}, u32[]{:S(2)}) %collective-permute-start.24) | collective-permute-done | bytes 262176 | tf_op jit(solution)/shard_map/ppermute | solution.py:63
  209.8 5.8 %collective-permute-done.25 = bf16[256,1024]{1,0:T(8,128)(2,1)S(1)} collective-permute-done((bf16[256,1024]{1,0:T(8,128)(2,1)S(1)}, bf16[256,1024]{1,0:T(8,128)(2,1)S(1)}, u32[]{:S(2)}, u32[]{:S(2)}) %collective-permute-start.25) | collective-permute-done | bytes 524320 | tf_op jit(solution)/shard_map/ppermute | solution.py:63
  224.1 7.6 %collective-permute-done.29 = bf16[512,1024]{1,0:T(8,128)(2,1)S(1)} collective-permute-done((bf16[512,1024]{1,0:T(8,128)(2,1)S(1)}, bf16[512,1024]{1,0:T(8,128)(2,1)S(1)}, u32[]{:S(2)}, u32[]{:S(2)}) %collective-permute-start.29) | collective-permute-done | bytes 1048608 | tf_op jit(solution)/shard_map/ppermute | solution.py:63
  240.2 7.8 %collective-permute-done.33 = bf16[256,1024]{1,0:T(8,128)(2,1)S(1)} collective-permute-done((bf16[256,1024]{1,0:T(8,128)(2,1)S(1)}, bf16[256,1024]{1,0:T(8,128)(2,1)S(1)}, u32[]{:S(2)}, u32[]{:S(2)}) %collective-permute-start.33) | collective-permute-done | bytes 524320 | tf_op jit(solution)/shard_map/ppermute | solution.py:63
  249.3 5.5 %collective-permute-done.34 = bf16[128,1024]{1,0:T(8,128)(2,1)S(1)} collective-permute-done((bf16[128,1024]{1,0:T(8,128)(2,1)S(1)}, bf16[128,1024]{1,0:T(8,128)(2,1)S(1)}, u32[]{:S(2)}, u32[]{:S(2)}) %collective-permute-start.34) | collective-permute-done | bytes 262176 | tf_op jit(solution)/shard_map/ppermute | solution.py:63
  290.8 7.1 %collective-permute-done.46 = bf16[256,1024]{1,0:T(8,128)(2,1)S(1)} collective-permute-done((bf16[256,1024]{1,0:T(8,128)(2,1)S(1)}, bf16[256,1024]{1,0:T(8,128)(2,1)S(1)}, u32[]{:S(2)}, u32[]{:S(2)}) %collective-permute-start.46) | collective-permute-done | bytes 524320 | tf_op jit(solution)/shard_map/ppermute | solution.py:63
  342.2 6.5 %collective-permute-done.71 = bf16[512,256]{1,0:T(8,128)(2,1)S(1)} collective-permute-done((bf16[512,256]{1,0:T(8,128)(2,1)S(1)}, bf16[512,256]{1,0:T(8,128)(2,1)S(1)}, u32[]{:S(2)}, u32[]{:S(2)}) %collective-permute-start.71) | collective-permute-done | bytes 262176 | tf_op jit(solution)/shard_map/ppermute | solution.py:63
  350.8 6.2 %collective-permute-done.72 = bf16[512,256]{1,0:T(8,128)(2,1)S(1)} collective-permute-done((bf16[512,256]{1,0:T(8,128)(2,1)S(1)}, bf16[512,256]{1,0:T(8,128)(2,1)S(1)}, u32[]{:S(2)}, u32[]{:S(2)}) %collective-permute-start.72) | collective-permute-done | bytes 262176 | tf_op jit(solution)/shard_map/ppermute | solution.py:63
  371.4 7.3 %collective-permute-done.58 = bf16[256,1024]{1,0:T(8,128)(2,1)} collective-permute-done((bf16[256,1024]{1,0:T(8,128)(2,1)}, bf16[256,1024]{1,0:T(8,128)(2,1)}, u32[]{:S(2)}, u32[]{:S(2)}) %collective-permute-start.58) | collective-permute-done | bytes 524320 | tf_op jit(solution)/shard_map/ppermute | solution.py:63
  390.8 12.6 %collective-permute-done.63.refs_1_ = bf16[128,2048]{1,0:T(8,128)(2,1)S(1)} collective-permute-done((bf16[128,2048]{1,0:T(8,128)(2,1)S(1)}, bf16[128,2048]{1,0:T(8,128)(2,1)S(1)}, u32[]{:S(2)}, u32[]{:S(2)}) %collective-permute-start.63) | collective-permute-done | bytes 524320 | tf_op jit(solution)/shard_map/ppermute | solution.py:63
  411.9 9.4 %collective-permute-done.60 = bf16[128,1024]{1,0:T(8,128)(2,1)S(1)} collective-permute-done((bf16[128,1024]{1,0:T(8,128)(2,1)}, bf16[128,1024]{1,0:T(8,128)(2,1)S(1)}, u32[]{:S(2)}, u32[]{:S(2)}) %collective-permute-start.60) | collective-permute-done | bytes 262176 | tf_op jit(solution)/shard_map/ppermute | solution.py:63
  422.7 7.6 %collective-permute-start.67 = (f32[2,17,128]{2,0,1:T(2,128)S(1)}, f32[2,17,128]{2,0,1:T(2,128)S(1)}, u32[]{:S(2)}, u32[]{:S(2)}) collective-permute-start(f32[2,17,128]{2,0,1:T(2,128)S(1)} %constant_dynamic-slice_fusion.4), channel_id=1, source_target_pairs={{0,4},{1,5},{2,6},{3,7},{4,0},{5,1},{6,2},{7,3},{8,12},{9,13},{10,... | collective-permute-start | bytes 52232 | tf_op jit(solution)/shard_map/ppermute | solution.py:63
  430.4 4.9 %collective-permute-start.61 = (bf16[128,1024]{1,0:T(8,128)(2,1)}, bf16[128,1024]{1,0:T(8,128)(2,1)S(1)}, u32[]{:S(2)}, u32[]{:S(2)}) collective-permute-start(bf16[128,1024]{1,0:T(8,128)(2,1)} %fusion.101), channel_id=1, source_target_pairs={{0,0},{1,1},{2,10},{3,11},{4,20},{5,21},{6,30},{7,31},{8,2},{9,3},... | collective-permute-start | bytes 786440 | tf_op jit(solution)/shard_map/ppermute | solution.py:63
  447.6 9.0 %collective-permute-start.70 = (f32[17,128]{1,0:T(8,128)S(1)}, f32[17,128]{1,0:T(8,128)S(1)}, u32[]{:S(2)}, u32[]{:S(2)}) collective-permute-start(f32[17,128]{1,0:T(8,128)S(1)} %fusion.221), channel_id=1, source_target_pairs={{0,16},{1,17},{2,18},{3,19},{4,20},{5,21},{6,22},{7,23},{8,24},{9,... | collective-permute-start | bytes 26120 | tf_op jit(solution)/shard_map/ppermute | solution.py:63
  465.8 5.6 %collective-permute-done.76.refs_3_ = bf16[128,2048]{1,0:T(8,128)(2,1)S(1)} collective-permute-done((bf16[128,2048]{1,0:T(8,128)(2,1)S(1)}, bf16[128,2048]{1,0:T(8,128)(2,1)S(1)}, u32[]{:S(2)}, u32[]{:S(2)}) %collective-permute-start.76) | collective-permute-done | bytes 524320 | tf_op jit(solution)/shard_map/ppermute | solution.py:63
  (699 shorter events, 283.4 us)
Async XLA Ops:
  7.2 62.3 %all-gather.4.cloned.1.call-start = ((), (), s32[]{:S(2)}) async-start(), calls=%async_computation.2 | async-start | bytes 2949120 | tf_op jit(solution)/shard_map/all_gather | solution.py:297
  7.2 20.4 %collective-permute-start = (bf16[128,1024]{1,0:T(8,128)(2,1)}, bf16[128,1024]{1,0:T(8,128)(2,1)S(1)}, u32[]{:S(2)}, u32[]{:S(2)}) collective-permute-start(bf16[128,1024]{1,0:T(8,128)(2,1)} %bitcast.256), channel_id=1, source_target_pairs={{0,0},{1,1},{2,8},{3,9},{4,16},{5,17},{6,24},{7,25},{8,10},{9,11},... | collective-permute-start | bytes 786440 | tf_op jit(solution)/shard_map/ppermute | solution.py:63
  27.6 99.3 %all-gather.6.cloned.1.call-start = ((), (), s32[]{:S(2)}) async-start(), calls=%async_computation.3 | async-start | bytes 1769472 | tf_op jit(solution)/shard_map/all_gather | solution.py:290
  31.6 141.4 %all-gather.8.cloned.1.call-start = ((), (), s32[]{:S(2)}) async-start(), calls=%async_computation.4 | async-start | bytes 4718592 | tf_op jit(solution)/shard_map/all_gather | solution.py:316
  57.5 249.9 %reduce-scatter.3.cloned.1.call-start = ((), (), s32[]{:S(2)}) async-start(), calls=%async_computation.5 | async-start | bytes 2621440 | tf_op jit(solution)/shard_map/reduce_scatter | solution.py:359
  74.7 35.3 %collective-permute-start.9 = (bf16[128,1024]{1,0:T(8,128)(2,1)}, bf16[128,1024]{1,0:T(8,128)(2,1)S(1)}, u32[]{:S(2)}, u32[]{:S(2)}) collective-permute-start(bf16[128,1024]{1,0:T(8,128)(2,1)} %bitcast.16), channel_id=1, source_target_pairs={{0,0},{1,1},{2,8},{3,9},{4,16},{5,17},{6,24},{7,25},{8,10},{9,11},... | collective-permute-start | bytes 786440 | tf_op jit(solution)/shard_map/ppermute | solution.py:63
  143.4 17.9 %collective-permute-start.15 = (bf16[512,1024]{1,0:T(8,128)(2,1)S(1)}, bf16[512,1024]{1,0:T(8,128)(2,1)S(1)}, u32[]{:S(2)}, u32[]{:S(2)}) collective-permute-start(bf16[512,1024]{1,0:T(8,128)(2,1)S(1)} %pad_maximum_fusion.2), channel_id=1, source_target_pairs={{0,16},{1,9},{2,18},{3,11},{4,20},{5,13},{6,22},{7,15},{8,24},{9,1... | collective-permute-start | bytes 3145736 | tf_op jit(solution)/shard_map/ppermute | solution.py:63
  144.2 34.5 %collective-permute-start.18 = (bf16[128,1024]{1,0:T(8,128)(2,1)}, bf16[128,1024]{1,0:T(8,128)(2,1)}, u32[]{:S(2)}, u32[]{:S(2)}) collective-permute-start(bf16[128,1024]{1,0:T(8,128)(2,1)} %bitcast.30), channel_id=1, source_target_pairs={{0,0},{1,1},{2,8},{3,9},{4,16},{5,17},{6,24},{7,25},{8,10},{9,11},... | collective-permute-start | bytes 786440 | tf_op jit(solution)/shard_map/ppermute | solution.py:63
  150.0 15.8 %collective-permute-start.16 = (bf16[256,1024]{1,0:T(8,128)(2,1)S(1)}, bf16[256,1024]{1,0:T(8,128)(2,1)S(1)}, u32[]{:S(2)}, u32[]{:S(2)}) collective-permute-start(bf16[256,1024]{1,0:T(8,128)(2,1)S(1)} %pad_maximum_fusion.8), channel_id=1, source_target_pairs={{0,1},{1,0},{2,3},{3,2},{4,5},{5,4},{6,7},{7,6},{8,9},{9,8},{10,11... | collective-permute-start | bytes 1572872 | tf_op jit(solution)/shard_map/ppermute | solution.py:63
  216.9 14.9 %collective-permute-start.29 = (bf16[512,1024]{1,0:T(8,128)(2,1)S(1)}, bf16[512,1024]{1,0:T(8,128)(2,1)S(1)}, u32[]{:S(2)}, u32[]{:S(2)}) collective-permute-start(bf16[512,1024]{1,0:T(8,128)(2,1)S(1)} %pad_maximum_fusion.3), channel_id=1, source_target_pairs={{0,16},{1,9},{2,18},{3,11},{4,20},{5,13},{6,22},{7,15},{8,24},{9,1... | collective-permute-start | bytes 3145736 | tf_op jit(solution)/shard_map/ppermute | solution.py:63
  224.1 16.2 %collective-permute-start.28 = (bf16[256,1024]{1,0:T(8,128)(2,1)S(1)}, bf16[256,1024]{1,0:T(8,128)(2,1)S(1)}, u32[]{:S(2)}, u32[]{:S(2)}) collective-permute-start(bf16[256,1024]{1,0:T(8,128)(2,1)S(1)} %convolution_convert_fusion.9), channel_id=1, source_target_pairs={{0,1},{1,0},{2,3},{3,2},{4,5},{5,4},{6,7},{7,6},{8,9},{9,8},{10,11... | collective-permute-start | bytes 1572872 | tf_op jit(solution)/shard_map/ppermute | solution.py:63
  259.9 175.5 %reduce-scatter.5.cloned.1.call-start = ((), (), s32[]{:S(2)}) async-start(), calls=%async_computation.6 | async-start | bytes 2621440 | tf_op jit(solution)/shard_map/reduce_scatter | solution.py:359
  269.2 13.8 %collective-permute-start.36 = (bf16[256,1024]{1,0:T(8,128)(2,1)S(1)}, bf16[256,1024]{1,0:T(8,128)(2,1)S(1)}, u32[]{:S(2)}, u32[]{:S(2)}) collective-permute-start(bf16[256,1024]{1,0:T(8,128)(2,1)S(1)} %convolution_convert_fusion.7), channel_id=1, source_target_pairs={{0,1},{1,0},{2,3},{3,2},{4,5},{5,4},{6,7},{7,6},{8,9},{9,8},{10,11... | collective-permute-start | bytes 1572872 | tf_op jit(solution)/shard_map/ppermute | solution.py:63
  283.3 17.0 %collective-permute-start.39 = (bf16[128,1024]{1,0:T(8,128)(2,1)S(1)}, bf16[128,1024]{1,0:T(8,128)(2,1)S(1)}, u32[]{:S(2)}, u32[]{:S(2)}) collective-permute-start(bf16[128,1024]{1,0:T(8,128)(2,1)S(1)} %slice.1033), channel_id=1, source_target_pairs={{0,8},{1,17},{2,10},{3,19},{4,12},{5,21},{6,14},{7,23},{8,0},{9,25... | collective-permute-start | bytes 786440 | tf_op jit(solution)/shard_map/ppermute | solution.py:63
  318.0 40.0 %collective-permute-start.40 = (bf16[128,1024]{1,0:T(8,128)(2,1)S(1)}, bf16[128,1024]{1,0:T(8,128)(2,1)S(1)}, u32[]{:S(2)}, u32[]{:S(2)}) collective-permute-start(bf16[128,1024]{1,0:T(8,128)(2,1)S(1)} %copy-done.79), channel_id=1, source_target_pairs={{0,0},{1,1},{2,10},{3,11},{4,20},{5,21},{6,30},{7,31},{8,2},{9,3},... | collective-permute-start | bytes 786440 | tf_op jit(solution)/shard_map/ppermute | solution.py:63
  326.4 23.6 %collective-permute-start.52 = (bf16[256,1024]{1,0:T(8,128)(2,1)S(1)}, bf16[256,1024]{1,0:T(8,128)(2,1)S(1)}, u32[]{:S(2)}, u32[]{:S(2)}) collective-permute-start(bf16[256,1024]{1,0:T(8,128)(2,1)S(1)} %convolution_convert_fusion.5), channel_id=1, source_target_pairs={{0,1},{1,0},{2,3},{3,2},{4,5},{5,4},{6,7},{7,6},{8,9},{9,8},{10,11... | collective-permute-start | bytes 1572872 | tf_op jit(solution)/shard_map/ppermute | solution.py:63
  388.6 14.8 %collective-permute-start.63 = (bf16[128,2048]{1,0:T(8,128)(2,1)S(1)}, bf16[128,2048]{1,0:T(8,128)(2,1)S(1)}, u32[]{:S(2)}, u32[]{:S(2)}) collective-permute-start(bf16[128,2048]{1,0:T(8,128)(2,1)S(1)} %pad_maximum_fusion.18.refs_0_), channel_id=1, source_target_pairs={{0,8},{1,17},{2,10},{3,19},{4,12},{5,21},{6,14},{7,23},{8,0},{9,25... | collective-permute-start | bytes 1572872 | tf_op jit(solution)/shard_map/ppermute | solution.py:63
  390.3 31.0 %collective-permute-start.64 = (bf16[128,2048]{1,0:T(8,128)(2,1)S(1)}, bf16[128,2048]{1,0:T(8,128)(2,1)S(1)}, u32[]{:S(2)}, u32[]{:S(2)}) collective-permute-start(bf16[128,2048]{1,0:T(8,128)(2,1)S(1)} %pad_maximum_fusion.18.refs_0_), channel_id=1, source_target_pairs={{0,16},{1,9},{2,18},{3,11},{4,20},{5,13},{6,22},{7,15},{8,24},{9,1... | collective-permute-start | bytes 1572872 | tf_op jit(solution)/shard_map/ppermute | solution.py:63
  403.4 17.8 %collective-permute-start.65 = (bf16[128,2048]{1,0:T(8,128)(2,1)S(1)}, bf16[128,2048]{1,0:T(8,128)(2,1)S(1)}, u32[]{:S(2)}, u32[]{:S(2)}) collective-permute-start(bf16[128,2048]{1,0:T(8,128)(2,1)S(1)} %collective-permute-done.63.refs_1_), channel_id=1, source_target_pairs={{0,16},{1,9},{2,18},{3,11},{4,20},{5,13},{6,22},{7,15},{8,24},{9,1... | collective-permute-start | bytes 1572872 | tf_op jit(solution)/shard_map/ppermute | solution.py:63
  404.8 16.4 %collective-permute-start.60 = (bf16[128,1024]{1,0:T(8,128)(2,1)}, bf16[128,1024]{1,0:T(8,128)(2,1)S(1)}, u32[]{:S(2)}, u32[]{:S(2)}) collective-permute-start(bf16[128,1024]{1,0:T(8,128)(2,1)} %add_convert_fusion.5), channel_id=1, source_target_pairs={{0,0},{1,1},{2,10},{3,11},{4,20},{5,21},{6,30},{7,31},{8,2},{9,3},... | collective-permute-start | bytes 786440 | tf_op jit(solution)/shard_map/ppermute | solution.py:63
  430.4 28.3 %collective-permute-start.61 = (bf16[128,1024]{1,0:T(8,128)(2,1)}, bf16[128,1024]{1,0:T(8,128)(2,1)S(1)}, u32[]{:S(2)}, u32[]{:S(2)}) collective-permute-start(bf16[128,1024]{1,0:T(8,128)(2,1)} %fusion.101), channel_id=1, source_target_pairs={{0,0},{1,1},{2,10},{3,11},{4,20},{5,21},{6,30},{7,31},{8,2},{9,3},... | collective-permute-start | bytes 786440 | tf_op jit(solution)/shard_map/ppermute | solution.py:63
  438.1 18.6 %collective-permute-start.74 = (bf16[128,2048]{1,0:T(8,128)(2,1)S(1)}, bf16[128,2048]{1,0:T(8,128)(2,1)S(1)}, u32[]{:S(2)}, u32[]{:S(2)}) collective-permute-start(bf16[128,2048]{1,0:T(8,128)(2,1)S(1)} %pad_maximum_fusion.20.refs_0_), channel_id=1, source_target_pairs={{0,8},{1,17},{2,10},{3,19},{4,12},{5,21},{6,14},{7,23},{8,0},{9,25... | collective-permute-start | bytes 1572872 | tf_op jit(solution)/shard_map/ppermute | solution.py:63
  447.6 14.9 %collective-permute-start.70 = (f32[17,128]{1,0:T(8,128)S(1)}, f32[17,128]{1,0:T(8,128)S(1)}, u32[]{:S(2)}, u32[]{:S(2)}) collective-permute-start(f32[17,128]{1,0:T(8,128)S(1)} %fusion.221), channel_id=1, source_target_pairs={{0,16},{1,17},{2,18},{3,19},{4,20},{5,21},{6,22},{7,23},{8,24},{9,... | collective-permute-start | bytes 26120 | tf_op jit(solution)/shard_map/ppermute | solution.py:63
  456.6 14.8 %collective-permute-start.76 = (bf16[128,2048]{1,0:T(8,128)(2,1)S(1)}, bf16[128,2048]{1,0:T(8,128)(2,1)S(1)}, u32[]{:S(2)}, u32[]{:S(2)}) collective-permute-start(bf16[128,2048]{1,0:T(8,128)(2,1)S(1)} %collective-permute-done.74.refs_1_), channel_id=1, source_target_pairs={{0,16},{1,9},{2,18},{3,11},{4,20},{5,13},{6,22},{7,15},{8,24},{9,1... | collective-permute-start | bytes 1572872 | tf_op jit(solution)/shard_map/ppermute | solution.py:63
  (189 other events, 1627.2 us)
Sparse Core Ops, SparseCore 0:
  27.8 41.6 all-gather.3
  71.0 44.8 all-gather.5
  118.2 54.7 all-gather.7
  260.0 47.2 reduce-scatter.2
  365.9 50.2 reduce-scatter.4

commit v5 on v4

--- a/solution.py
+++ b/solution.py
@@ -439,7 +439,7 @@
         g1_all = links.gather(g1)
         e1 = join([mm_nt(v, w_self_out).astype(BF) for v in g1_all])
         gq1, gk1, gv1 = attend_back(q1, k1, v1, e1, join(c1), l1, pos, True)
-        encoded_grad = plane_sum(cut4(after(pair2, g1_all[3])), w_cross_kv).astype(BF)
+        encoded_grad = plane_sum(cut4(after(pair2, g1_all[0])), w_cross_kv).astype(BF)
 
         output = links.from_plane(output)
         triple = after(jnp.concatenate([gq1, gk1, gv1], axis=1), encoded_grad, output)

time: 493 us -> 488 us (0.990)
  waiting for transfers between devices: 205 us -> 197 us
    ppermute x77, waiting for transfers between devices: 195 us -> 187 us  [go(): return lax.ppermute(x, AXES, pairs)]
    unnamed x283 -> x279, local copies, waits for them, and re-layouts: 22.1 us -> 23.6 us
  transfers between devices with their start and end apart: 82 -> 82, of which waited for: 44 -> 41; matrix products, arithmetic and copies ran while one was open for 27% -> 29% of each run, Pallas kernels for 1% -> 1%
where the time goes in v5:
time: 488 us; the launch traced here: 480 us
  waiting for transfers between devices  197 us (40%)
  starting transfers between devices  93 us (19%)
  matrix products  78.4 us (16%)
  local copies, waits for them, and re-layouts  48.7 us (10%)
  other arithmetic  39.3 us (8%)
  between operations  16.9 us (3%)
  Pallas kernels  6.77 us (1%)
    ppermute x77, waiting for transfers between devices, go(): return lax.ppermute(x, AXES, pairs)  187 us
    ppermute x77, starting transfers between devices, go(): return lax.ppermute(x, AXES, pairs)  92.6 us
    dot_general x38, matrix products, mm_nt(): lax.dot_general(a, b, (((1,), (1,)), ((), ())), preferred_element_type=F32)  31.9 us
    dot_general x36, matrix products, mm(): return jnp.dot(a, b, preferred_element_type=F32)  27.1 us
    unnamed x279, local copies, waits for them, and re-layouts  23.6 us
    dot_general x16, matrix products, mm_tn(): lax.dot_general(a, b, (((0,), (0,)), ((), ())), preferred_element_type=F32)  19.4 us
  transfers between devices with their start and end apart: 82, of which 41 were waited for; matrix products, arithmetic and copies ran while one was open for 29% of the time, Pallas kernels for 1%

profile of v5, /device:TPU:8, one launch (start us, length us, event | category | flops | bytes accessed | tf_op | source)
XLA Modules:
  0.0 479.7 jit_solution(17834205978749478351)
XLA Ops:
  42.8 8.5 %collective-permute-start.4 = (bf16[128,1024]{1,0:T(8,128)(2,1)S(1)}, bf16[128,1024]{1,0:T(8,128)(2,1)S(1)}, u32[]{:S(2)}, u32[]{:S(2)}) collective-permute-start(bf16[128,1024]{1,0:T(8,128)(2,1)S(1)} %get-tuple-element.119), channel_id=1, source_target_pairs={{0,8},{1,17},{2,10},{3,19},{4,12},{5,21},{6,14},{7,23},{8,0},{9,25... | collective-permute-start | bytes 786440 | tf_op jit(solution)/shard_map/ppermute | solution.py:63
  57.6 8.3 %collective-permute-done.6 = bf16[256,1024]{1,0:T(8,128)(2,1)S(1)} collective-permute-done((bf16[256,1024]{1,0:T(8,128)(2,1)}, bf16[256,1024]{1,0:T(8,128)(2,1)S(1)}, u32[]{:S(2)}, u32[]{:S(2)}) %collective-permute-start.6) | collective-permute-done | bytes 524320 | tf_op jit(solution)/shard_map/ppermute | solution.py:63
  74.7 7.4 %collective-permute-start.9 = (bf16[128,1024]{1,0:T(8,128)(2,1)}, bf16[128,1024]{1,0:T(8,128)(2,1)S(1)}, u32[]{:S(2)}, u32[]{:S(2)}) collective-permute-start(bf16[128,1024]{1,0:T(8,128)(2,1)} %bitcast.16), channel_id=1, source_target_pairs={{0,0},{1,1},{2,8},{3,9},{4,16},{5,17},{6,24},{7,25},{8,10},{9,11},... | collective-permute-start | bytes 786440 | tf_op jit(solution)/shard_map/ppermute | solution.py:63
  92.9 17.0 %collective-permute-done.9 = bf16[128,1024]{1,0:T(8,128)(2,1)S(1)} collective-permute-done((bf16[128,1024]{1,0:T(8,128)(2,1)}, bf16[128,1024]{1,0:T(8,128)(2,1)S(1)}, u32[]{:S(2)}, u32[]{:S(2)}) %collective-permute-start.9) | collective-permute-done | bytes 262176 | tf_op jit(solution)/shard_map/ppermute | solution.py:63
  114.8 8.1 %collective-permute-done.12 = bf16[256,1024]{1,0:T(8,128)(2,1)} collective-permute-done((bf16[256,1024]{1,0:T(8,128)(2,1)}, bf16[256,1024]{1,0:T(8,128)(2,1)}, u32[]{:S(2)}, u32[]{:S(2)}) %collective-permute-start.12) | collective-permute-done | bytes 524320 | tf_op jit(solution)/shard_map/ppermute | solution.py:63
  136.4 6.9 %collective-permute-done.14 = bf16[256,1024]{1,0:T(8,128)(2,1)S(1)} collective-permute-done((bf16[256,1024]{1,0:T(8,128)(2,1)S(1)}, bf16[256,1024]{1,0:T(8,128)(2,1)S(1)}, u32[]{:S(2)}, u32[]{:S(2)}) %collective-permute-start.14) | collective-permute-done | bytes 524320 | tf_op jit(solution)/shard_map/ppermute | solution.py:63
  144.2 5.7 %collective-permute-start.18 = (bf16[128,1024]{1,0:T(8,128)(2,1)}, bf16[128,1024]{1,0:T(8,128)(2,1)}, u32[]{:S(2)}, u32[]{:S(2)}) collective-permute-start(bf16[128,1024]{1,0:T(8,128)(2,1)} %bitcast.30), channel_id=1, source_target_pairs={{0,0},{1,1},{2,8},{3,9},{4,16},{5,17},{6,24},{7,25},{8,10},{9,11},... | collective-permute-start | bytes 786440 | tf_op jit(solution)/shard_map/ppermute | solution.py:63
  153.0 8.3 %collective-permute-done.15 = bf16[512,1024]{1,0:T(8,128)(2,1)S(1)} collective-permute-done((bf16[512,1024]{1,0:T(8,128)(2,1)S(1)}, bf16[512,1024]{1,0:T(8,128)(2,1)S(1)}, u32[]{:S(2)}, u32[]{:S(2)}) %collective-permute-start.15) | collective-permute-done | bytes 1048608 | tf_op jit(solution)/shard_map/ppermute | solution.py:63
  167.5 5.4 %all-gather.8.cloned.1.call-done.in_ref = bf16[2,2048,512]{2,1,0:T(8,128)(2,1)} async-done(((bf16[2,256,512]{2,1,0:T(8,128)(2,1)}), bf16[2,2048,512]{2,1,0:T(8,128)(2,1)}) %all-gather.8.cloned.1.call-update) | async-done | bytes 4194320 | tf_op jit(solution)/shard_map/all_gather | solution.py:316
  199.3 5.5 %collective-permute-done.24 = bf16[128,1024]{1,0:T(8,128)(2,1)S(1)} collective-permute-done((bf16[128,1024]{1,0:T(8,128)(2,1)S(1)}, bf16[128,1024]{1,0:T(8,128)(2,1)S(1)}, u32[]{:S(2)}, u32[]{:S(2)}) %collective-permute-start.24) | collective-permute-done | bytes 262176 | tf_op jit(solution)/shard_map/ppermute | solution.py:63
  209.9 5.8 %collective-permute-done.25 = bf16[256,1024]{1,0:T(8,128)(2,1)S(1)} collective-permute-done((bf16[256,1024]{1,0:T(8,128)(2,1)S(1)}, bf16[256,1024]{1,0:T(8,128)(2,1)S(1)}, u32[]{:S(2)}, u32[]{:S(2)}) %collective-permute-start.25) | collective-permute-done | bytes 524320 | tf_op jit(solution)/shard_map/ppermute | solution.py:63
  224.2 7.6 %collective-permute-done.29 = bf16[512,1024]{1,0:T(8,128)(2,1)S(1)} collective-permute-done((bf16[512,1024]{1,0:T(8,128)(2,1)S(1)}, bf16[512,1024]{1,0:T(8,128)(2,1)S(1)}, u32[]{:S(2)}, u32[]{:S(2)}) %collective-permute-start.29) | collective-permute-done | bytes 1048608 | tf_op jit(solution)/shard_map/ppermute | solution.py:63
  240.3 7.8 %collective-permute-done.33 = bf16[256,1024]{1,0:T(8,128)(2,1)S(1)} collective-permute-done((bf16[256,1024]{1,0:T(8,128)(2,1)S(1)}, bf16[256,1024]{1,0:T(8,128)(2,1)S(1)}, u32[]{:S(2)}, u32[]{:S(2)}) %collective-permute-start.33) | collective-permute-done | bytes 524320 | tf_op jit(solution)/shard_map/ppermute | solution.py:63
  249.3 5.5 %collective-permute-done.34 = bf16[128,1024]{1,0:T(8,128)(2,1)S(1)} collective-permute-done((bf16[128,1024]{1,0:T(8,128)(2,1)S(1)}, bf16[128,1024]{1,0:T(8,128)(2,1)S(1)}, u32[]{:S(2)}, u32[]{:S(2)}) %collective-permute-start.34) | collective-permute-done | bytes 262176 | tf_op jit(solution)/shard_map/ppermute | solution.py:63
  292.0 6.4 %collective-permute-done.46 = bf16[256,1024]{1,0:T(8,128)(2,1)S(1)} collective-permute-done((bf16[256,1024]{1,0:T(8,128)(2,1)S(1)}, bf16[256,1024]{1,0:T(8,128)(2,1)S(1)}, u32[]{:S(2)}, u32[]{:S(2)}) %collective-permute-start.46) | collective-permute-done | bytes 524320 | tf_op jit(solution)/shard_map/ppermute | solution.py:63
  315.2 7.4 %collective-permute-start.49 = (bf16[256,1024]{1,0:T(8,128)(2,1)S(1)}, bf16[256,1024]{1,0:T(8,128)(2,1)S(1)}, u32[]{:S(2)}, u32[]{:S(2)}) collective-permute-start(bf16[256,1024]{1,0:T(8,128)(2,1)S(1)} %pad_maximum_fusion.16), channel_id=1, source_target_pairs={{0,16},{1,9},{2,18},{3,11},{4,20},{5,13},{6,22},{7,15},{8,24},{9,1... | collective-permute-start | bytes 1572872 | tf_op jit(solution)/shard_map/ppermute | solution.py:63
  370.9 8.5 %collective-permute-done.58 = bf16[256,1024]{1,0:T(8,128)(2,1)} collective-permute-done((bf16[256,1024]{1,0:T(8,128)(2,1)}, bf16[256,1024]{1,0:T(8,128)(2,1)}, u32[]{:S(2)}, u32[]{:S(2)}) %collective-permute-start.58) | collective-permute-done | bytes 524320 | tf_op jit(solution)/shard_map/ppermute | solution.py:63
  381.2 6.2 %collective-permute-done.59 = bf16[128,1024]{1,0:T(8,128)(2,1)S(1)} collective-permute-done((bf16[128,1024]{1,0:T(8,128)(2,1)S(1)}, bf16[128,1024]{1,0:T(8,128)(2,1)S(1)}, u32[]{:S(2)}, u32[]{:S(2)}) %collective-permute-start.59) | collective-permute-done | bytes 262176 | tf_op jit(solution)/shard_map/ppermute | solution.py:63
  389.8 11.9 %collective-permute-done.63.refs_1_ = bf16[128,2048]{1,0:T(8,128)(2,1)S(1)} collective-permute-done((bf16[128,2048]{1,0:T(8,128)(2,1)S(1)}, bf16[128,2048]{1,0:T(8,128)(2,1)S(1)}, u32[]{:S(2)}, u32[]{:S(2)}) %collective-permute-start.63) | collective-permute-done | bytes 524320 | tf_op jit(solution)/shard_map/ppermute | solution.py:63
  416.2 5.5 %collective-permute-start.67 = (f32[2,17,128]{2,0,1:T(2,128)S(1)}, f32[2,17,128]{2,0,1:T(2,128)S(1)}, u32[]{:S(2)}, u32[]{:S(2)}) collective-permute-start(f32[2,17,128]{2,0,1:T(2,128)S(1)} %constant_dynamic-slice_fusion.4), channel_id=1, source_target_pairs={{0,4},{1,5},{2,6},{3,7},{4,0},{5,1},{6,2},{7,3},{8,12},{9,13},{10,... | collective-permute-start | bytes 52232 | tf_op jit(solution)/shard_map/ppermute | solution.py:63
  421.8 5.3 %collective-permute-start.61 = (bf16[128,1024]{1,0:T(8,128)(2,1)}, bf16[128,1024]{1,0:T(8,128)(2,1)S(1)}, u32[]{:S(2)}, u32[]{:S(2)}) collective-permute-start(bf16[128,1024]{1,0:T(8,128)(2,1)} %fusion.99), channel_id=1, source_target_pairs={{0,0},{1,1},{2,10},{3,11},{4,20},{5,21},{6,30},{7,31},{8,2},{9,3},... | collective-permute-start | bytes 786440 | tf_op jit(solution)/shard_map/ppermute | solution.py:63
  435.4 5.8 %collective-permute-done.69 = f32[17,128]{1,0:T(8,128)S(1)} collective-permute-done((f32[17,128]{1,0:T(8,128)S(1)}, f32[17,128]{1,0:T(8,128)S(1)}, u32[]{:S(2)}, u32[]{:S(2)}) %collective-permute-start.69) | collective-permute-done | bytes 8736 | tf_op jit(solution)/shard_map/ppermute | solution.py:63
  441.2 10.7 %collective-permute-start.70 = (f32[17,128]{1,0:T(8,128)S(1)}, f32[17,128]{1,0:T(8,128)S(1)}, u32[]{:S(2)}, u32[]{:S(2)}) collective-permute-start(f32[17,128]{1,0:T(8,128)S(1)} %fusion.223), channel_id=1, source_target_pairs={{0,16},{1,17},{2,18},{3,19},{4,20},{5,21},{6,22},{7,23},{8,24},{9,... | collective-permute-start | bytes 26120 | tf_op jit(solution)/shard_map/ppermute | solution.py:63
  461.1 5.6 %collective-permute-done.76.refs_3_ = bf16[128,2048]{1,0:T(8,128)(2,1)S(1)} collective-permute-done((bf16[128,2048]{1,0:T(8,128)(2,1)S(1)}, bf16[128,2048]{1,0:T(8,128)(2,1)S(1)}, u32[]{:S(2)}, u32[]{:S(2)}) %collective-permute-start.76) | collective-permute-done | bytes 524320 | tf_op jit(solution)/shard_map/ppermute | solution.py:63
  (696 shorter events, 281.7 us)
Async XLA Ops:
  7.2 62.3 %all-gather.4.cloned.1.call-start = ((), (), s32[]{:S(2)}) async-start(), calls=%async_computation.2 | async-start | bytes 2949120 | tf_op jit(solution)/shard_map/all_gather | solution.py:297
  7.2 20.4 %collective-permute-start = (bf16[128,1024]{1,0:T(8,128)(2,1)}, bf16[128,1024]{1,0:T(8,128)(2,1)S(1)}, u32[]{:S(2)}, u32[]{:S(2)}) collective-permute-start(bf16[128,1024]{1,0:T(8,128)(2,1)} %bitcast.256), channel_id=1, source_target_pairs={{0,0},{1,1},{2,8},{3,9},{4,16},{5,17},{6,24},{7,25},{8,10},{9,11},... | collective-permute-start | bytes 786440 | tf_op jit(solution)/shard_map/ppermute | solution.py:63
  27.6 99.3 %all-gather.6.cloned.1.call-start = ((), (), s32[]{:S(2)}) async-start(), calls=%async_computation.3 | async-start | bytes 1769472 | tf_op jit(solution)/shard_map/all_gather | solution.py:290
  31.6 141.4 %all-gather.8.cloned.1.call-start = ((), (), s32[]{:S(2)}) async-start(), calls=%async_computation.4 | async-start | bytes 4718592 | tf_op jit(solution)/shard_map/all_gather | solution.py:316
  57.5 249.9 %reduce-scatter.3.cloned.1.call-start = ((), (), s32[]{:S(2)}) async-start(), calls=%async_computation.5 | async-start | bytes 2621440 | tf_op jit(solution)/shard_map/reduce_scatter | solution.py:359
  74.7 35.3 %collective-permute-start.9 = (bf16[128,1024]{1,0:T(8,128)(2,1)}, bf16[128,1024]{1,0:T(8,128)(2,1)S(1)}, u32[]{:S(2)}, u32[]{:S(2)}) collective-permute-start(bf16[128,1024]{1,0:T(8,128)(2,1)} %bitcast.16), channel_id=1, source_target_pairs={{0,0},{1,1},{2,8},{3,9},{4,16},{5,17},{6,24},{7,25},{8,10},{9,11},... | collective-permute-start | bytes 786440 | tf_op jit(solution)/shard_map/ppermute | solution.py:63
  143.5 17.9 %collective-permute-start.15 = (bf16[512,1024]{1,0:T(8,128)(2,1)S(1)}, bf16[512,1024]{1,0:T(8,128)(2,1)S(1)}, u32[]{:S(2)}, u32[]{:S(2)}) collective-permute-start(bf16[512,1024]{1,0:T(8,128)(2,1)S(1)} %pad_maximum_fusion.2), channel_id=1, source_target_pairs={{0,16},{1,9},{2,18},{3,11},{4,20},{5,13},{6,22},{7,15},{8,24},{9,1... | collective-permute-start | bytes 3145736 | tf_op jit(solution)/shard_map/ppermute | solution.py:63
  144.2 34.5 %collective-permute-start.18 = (bf16[128,1024]{1,0:T(8,128)(2,1)}, bf16[128,1024]{1,0:T(8,128)(2,1)}, u32[]{:S(2)}, u32[]{:S(2)}) collective-permute-start(bf16[128,1024]{1,0:T(8,128)(2,1)} %bitcast.30), channel_id=1, source_target_pairs={{0,0},{1,1},{2,8},{3,9},{4,16},{5,17},{6,24},{7,25},{8,10},{9,11},... | collective-permute-start | bytes 786440 | tf_op jit(solution)/shard_map/ppermute | solution.py:63
  150.0 15.8 %collective-permute-start.16 = (bf16[256,1024]{1,0:T(8,128)(2,1)S(1)}, bf16[256,1024]{1,0:T(8,128)(2,1)S(1)}, u32[]{:S(2)}, u32[]{:S(2)}) collective-permute-start(bf16[256,1024]{1,0:T(8,128)(2,1)S(1)} %pad_maximum_fusion.8), channel_id=1, source_target_pairs={{0,1},{1,0},{2,3},{3,2},{4,5},{5,4},{6,7},{7,6},{8,9},{9,8},{10,11... | collective-permute-start | bytes 1572872 | tf_op jit(solution)/shard_map/ppermute | solution.py:63
  163.5 13.8 %collective-permute-start.17 = (bf16[256,1024]{1,0:T(8,128)(2,1)}, bf16[256,1024]{1,0:T(8,128)(2,1)}, u32[]{:S(2)}, u32[]{:S(2)}) collective-permute-start(bf16[256,1024]{1,0:T(8,128)(2,1)} %get-tuple-element.127), channel_id=1, source_target_pairs={{0,1},{1,0},{2,3},{3,2},{4,5},{5,4},{6,7},{7,6},{8,9},{9,8},{10,11... | collective-permute-start | bytes 1572872 | tf_op jit(solution)/shard_map/ppermute | solution.py:63
  216.9 14.9 %collective-permute-start.29 = (bf16[512,1024]{1,0:T(8,128)(2,1)S(1)}, bf16[512,1024]{1,0:T(8,128)(2,1)S(1)}, u32[]{:S(2)}, u32[]{:S(2)}) collective-permute-start(bf16[512,1024]{1,0:T(8,128)(2,1)S(1)} %pad_maximum_fusion.3), channel_id=1, source_target_pairs={{0,16},{1,9},{2,18},{3,11},{4,20},{5,13},{6,22},{7,15},{8,24},{9,1... | collective-permute-start | bytes 3145736 | tf_op jit(solution)/shard_map/ppermute | solution.py:63
  224.1 16.2 %collective-permute-start.28 = (bf16[256,1024]{1,0:T(8,128)(2,1)S(1)}, bf16[256,1024]{1,0:T(8,128)(2,1)S(1)}, u32[]{:S(2)}, u32[]{:S(2)}) collective-permute-start(bf16[256,1024]{1,0:T(8,128)(2,1)S(1)} %convolution_convert_fusion.9), channel_id=1, source_target_pairs={{0,1},{1,0},{2,3},{3,2},{4,5},{5,4},{6,7},{7,6},{8,9},{9,8},{10,11... | collective-permute-start | bytes 1572872 | tf_op jit(solution)/shard_map/ppermute | solution.py:63
  260.0 167.3 %reduce-scatter.5.cloned.1.call-start = ((), (), s32[]{:S(2)}) async-start(), calls=%async_computation.6 | async-start | bytes 2621440 | tf_op jit(solution)/shard_map/reduce_scatter | solution.py:359
  269.2 13.8 %collective-permute-start.36 = (bf16[256,1024]{1,0:T(8,128)(2,1)S(1)}, bf16[256,1024]{1,0:T(8,128)(2,1)S(1)}, u32[]{:S(2)}, u32[]{:S(2)}) collective-permute-start(bf16[256,1024]{1,0:T(8,128)(2,1)S(1)} %convolution_convert_fusion.7), channel_id=1, source_target_pairs={{0,1},{1,0},{2,3},{3,2},{4,5},{5,4},{6,7},{7,6},{8,9},{9,8},{10,11... | collective-permute-start | bytes 1572872 | tf_op jit(solution)/shard_map/ppermute | solution.py:63
  283.3 17.4 %collective-permute-start.39 = (bf16[128,1024]{1,0:T(8,128)(2,1)S(1)}, bf16[128,1024]{1,0:T(8,128)(2,1)S(1)}, u32[]{:S(2)}, u32[]{:S(2)}) collective-permute-start(bf16[128,1024]{1,0:T(8,128)(2,1)S(1)} %slice.1035), channel_id=1, source_target_pairs={{0,8},{1,17},{2,10},{3,19},{4,12},{5,21},{6,14},{7,23},{8,0},{9,25... | collective-permute-start | bytes 786440 | tf_op jit(solution)/shard_map/ppermute | solution.py:63
  311.8 38.4 %collective-permute-start.40 = (bf16[128,1024]{1,0:T(8,128)(2,1)S(1)}, bf16[128,1024]{1,0:T(8,128)(2,1)S(1)}, u32[]{:S(2)}, u32[]{:S(2)}) collective-permute-start(bf16[128,1024]{1,0:T(8,128)(2,1)S(1)} %copy-done.77), channel_id=1, source_target_pairs={{0,0},{1,1},{2,10},{3,11},{4,20},{5,21},{6,30},{7,31},{8,2},{9,3},... | collective-permute-start | bytes 786440 | tf_op jit(solution)/shard_map/ppermute | solution.py:63
  315.2 14.6 %collective-permute-start.49 = (bf16[256,1024]{1,0:T(8,128)(2,1)S(1)}, bf16[256,1024]{1,0:T(8,128)(2,1)S(1)}, u32[]{:S(2)}, u32[]{:S(2)}) collective-permute-start(bf16[256,1024]{1,0:T(8,128)(2,1)S(1)} %pad_maximum_fusion.16), channel_id=1, source_target_pairs={{0,16},{1,9},{2,18},{3,11},{4,20},{5,13},{6,22},{7,15},{8,24},{9,1... | collective-permute-start | bytes 1572872 | tf_op jit(solution)/shard_map/ppermute | solution.py:63
  335.7 13.8 %collective-permute-start.55 = (bf16[128,1024]{1,0:T(8,128)(2,1)S(1)}, bf16[128,1024]{1,0:T(8,128)(2,1)S(1)}, u32[]{:S(2)}, u32[]{:S(2)}) collective-permute-start(bf16[128,1024]{1,0:T(8,128)(2,1)S(1)} %slice.1033), channel_id=1, source_target_pairs={{0,8},{1,17},{2,10},{3,19},{4,12},{5,21},{6,14},{7,23},{8,0},{9,25... | collective-permute-start | bytes 786440 | tf_op jit(solution)/shard_map/ppermute | solution.py:63
  354.6 16.4 %collective-permute-start.56 = (bf16[256,1024]{1,0:T(8,128)(2,1)}, bf16[256,1024]{1,0:T(8,128)(2,1)}, u32[]{:S(2)}, u32[]{:S(2)}) collective-permute-start(bf16[256,1024]{1,0:T(8,128)(2,1)} %convolution_convert_fusion.3), channel_id=1, source_target_pairs={{0,1},{1,0},{2,3},{3,2},{4,5},{5,4},{6,7},{7,6},{8,9},{9,8},{10,11... | collective-permute-start | bytes 1572872 | tf_op jit(solution)/shard_map/ppermute | solution.py:63
  389.4 25.4 %collective-permute-start.64 = (bf16[128,2048]{1,0:T(8,128)(2,1)S(1)}, bf16[128,2048]{1,0:T(8,128)(2,1)S(1)}, u32[]{:S(2)}, u32[]{:S(2)}) collective-permute-start(bf16[128,2048]{1,0:T(8,128)(2,1)S(1)} %pad_maximum_fusion.18.refs_0_), channel_id=1, source_target_pairs={{0,16},{1,9},{2,18},{3,11},{4,20},{5,13},{6,22},{7,15},{8,24},{9,1... | collective-permute-start | bytes 1572872 | tf_op jit(solution)/shard_map/ppermute | solution.py:63
  421.8 32.1 %collective-permute-start.61 = (bf16[128,1024]{1,0:T(8,128)(2,1)}, bf16[128,1024]{1,0:T(8,128)(2,1)S(1)}, u32[]{:S(2)}, u32[]{:S(2)}) collective-permute-start(bf16[128,1024]{1,0:T(8,128)(2,1)} %fusion.99), channel_id=1, source_target_pairs={{0,0},{1,1},{2,10},{3,11},{4,20},{5,21},{6,30},{7,31},{8,2},{9,3},... | collective-permute-start | bytes 786440 | tf_op jit(solution)/shard_map/ppermute | solution.py:63
  429.9 22.1 %collective-permute-start.74 = (bf16[128,2048]{1,0:T(8,128)(2,1)S(1)}, bf16[128,2048]{1,0:T(8,128)(2,1)S(1)}, u32[]{:S(2)}, u32[]{:S(2)}) collective-permute-start(bf16[128,2048]{1,0:T(8,128)(2,1)S(1)} %pad_maximum_fusion.20.refs_0_), channel_id=1, source_target_pairs={{0,8},{1,17},{2,10},{3,19},{4,12},{5,21},{6,14},{7,23},{8,0},{9,25... | collective-permute-start | bytes 1572872 | tf_op jit(solution)/shard_map/ppermute | solution.py:63
  441.2 16.5 %collective-permute-start.70 = (f32[17,128]{1,0:T(8,128)S(1)}, f32[17,128]{1,0:T(8,128)S(1)}, u32[]{:S(2)}, u32[]{:S(2)}) collective-permute-start(f32[17,128]{1,0:T(8,128)S(1)} %fusion.223), channel_id=1, source_target_pairs={{0,16},{1,17},{2,18},{3,19},{4,20},{5,21},{6,22},{7,23},{8,24},{9,... | collective-permute-start | bytes 26120 | tf_op jit(solution)/shard_map/ppermute | solution.py:63
  451.9 14.8 %collective-permute-start.76 = (bf16[128,2048]{1,0:T(8,128)(2,1)S(1)}, bf16[128,2048]{1,0:T(8,128)(2,1)S(1)}, u32[]{:S(2)}, u32[]{:S(2)}) collective-permute-start(bf16[128,2048]{1,0:T(8,128)(2,1)S(1)} %collective-permute-done.74.refs_1_), channel_id=1, source_target_pairs={{0,16},{1,9},{2,18},{3,11},{4,20},{5,13},{6,22},{7,15},{8,24},{9,1... | collective-permute-start | bytes 1572872 | tf_op jit(solution)/shard_map/ppermute | solution.py:63
  (187 other events, 1557.5 us)
Sparse Core Ops, SparseCore 0:
  27.8 41.6 all-gather.3
  71.0 44.9 all-gather.5
  118.2 54.7 all-gather.7
  260.1 47.2 reduce-scatter.2
  366.7 41.7 reduce-scatter.4

commit v6 on v5

--- a/solution.py
+++ b/solution.py
@@ -149,13 +149,13 @@
     outs, lses = [], []
     for h in range(heads):
         cut = slice(h * HEAD_DIM, (h + 1) * HEAD_DIM)
-        s = mm_nt(q[:, cut], k[:, cut]) * HEAD_DIM ** (-0.5)
+        s = mm_nt(q[:, cut] * BF(HEAD_DIM ** (-0.5)), k[:, cut])
         if causal:
             s = jnp.where(pos[:, None] >= pos[None, :], s, -1e30)
         m = jnp.max(s, axis=-1, keepdims=True)
         p = jnp.exp(s - m)
         t = jnp.sum(p, axis=-1, keepdims=True)
-        outs.append(mm((p / t).astype(BF), v[:, cut]).astype(BF))
+        outs.append(mm((p * (1.0 / t)).astype(BF), v[:, cut]).astype(BF))
         lses.append(m + jnp.log(t))
     return jnp.concatenate(outs, axis=1), lses
 
@@ -165,7 +165,7 @@
     dqs, dks, dvs = [], [], []
     for h in range(heads):
         cut = slice(h * HEAD_DIM, (h + 1) * HEAD_DIM)
-        s = mm_nt(q[:, cut], k[:, cut]) * HEAD_DIM ** (-0.5)
+        s = mm_nt(q[:, cut] * BF(HEAD_DIM ** (-0.5)), k[:, cut])
         if causal:
             s = jnp.where(pos[:, None] >= pos[None, :], s, -1e30)
         p = jnp.exp(s - lses[h])

time: 488 us -> 490 us (level)
    unnamed x279 -> x261, local copies, waits for them, and re-layouts: 23.6 us -> 23.4 us
  transfers between devices with their start and end apart: 82 -> 82, of which waited for: 41 -> 43; matrix products, arithmetic and copies ran while one was open for 29% -> 28% of each run, Pallas kernels for 1% -> 1%
where the time goes in v6:
time: 490 us; the launch traced here: 481 us
  waiting for transfers between devices  201 us (41%)
  starting transfers between devices  91.9 us (19%)
  matrix products  74.9 us (15%)
  local copies, waits for them, and re-layouts  46.5 us (9%)
  other arithmetic  42.4 us (9%)
  between operations  16.9 us (3%)
  Pallas kernels  6.77 us (1%)
    ppermute x77, waiting for transfers between devices, go(): return lax.ppermute(x, AXES, pairs)  192 us
    ppermute x77, starting transfers between devices, go(): return lax.ppermute(x, AXES, pairs)  91.3 us
    dot_general x38, matrix products, mm_nt(): lax.dot_general(a, b, (((1,), (1,)), ((), ())), preferred_element_type=F32)  33.6 us
    dot_general x36, matrix products, mm(): return jnp.dot(a, b, preferred_element_type=F32)  24.4 us
    unnamed x261, local copies, waits for them, and re-layouts  23.4 us
    dot_general x16, matrix products, mm_tn(): lax.dot_general(a, b, (((0,), (0,)), ((), ())), preferred_element_type=F32)  16.9 us
  transfers between devices with their start and end apart: 82, of which 43 were waited for; matrix products, arithmetic and copies ran while one was open for 28% of the time, Pallas kernels for 1%

profile of v6, /device:TPU:8, one launch (start us, length us, event | category | flops | bytes accessed | tf_op | source)
XLA Modules:
  0.0 480.7 jit_solution(15293932557338738059)
XLA Ops:
  42.8 8.5 %collective-permute-start.4 = (bf16[128,1024]{1,0:T(8,128)(2,1)S(1)}, bf16[128,1024]{1,0:T(8,128)(2,1)S(1)}, u32[]{:S(2)}, u32[]{:S(2)}) collective-permute-start(bf16[128,1024]{1,0:T(8,128)(2,1)S(1)} %get-tuple-element.123), channel_id=1, source_target_pairs={{0,8},{1,17},{2,10},{3,19},{4,12},{5,21},{6,14},{7,23},{8,0},{9,25... | collective-permute-start | bytes 786440 | tf_op jit(solution)/shard_map/ppermute | solution.py:63
  57.6 8.3 %collective-permute-done.6 = bf16[256,1024]{1,0:T(8,128)(2,1)S(1)} collective-permute-done((bf16[256,1024]{1,0:T(8,128)(2,1)}, bf16[256,1024]{1,0:T(8,128)(2,1)S(1)}, u32[]{:S(2)}, u32[]{:S(2)}) %collective-permute-start.6) | collective-permute-done | bytes 524320 | tf_op jit(solution)/shard_map/ppermute | solution.py:63
  79.2 7.5 %collective-permute-start.9 = (bf16[128,1024]{1,0:T(8,128)(2,1)}, bf16[128,1024]{1,0:T(8,128)(2,1)S(1)}, u32[]{:S(2)}, u32[]{:S(2)}) collective-permute-start(bf16[128,1024]{1,0:T(8,128)(2,1)} %bitcast.16), channel_id=1, source_target_pairs={{0,0},{1,1},{2,8},{3,9},{4,16},{5,17},{6,24},{7,25},{8,10},{9,11},... | collective-permute-start | bytes 786440 | tf_op jit(solution)/shard_map/ppermute | solution.py:63
  95.8 16.0 %collective-permute-done.9 = bf16[128,1024]{1,0:T(8,128)(2,1)S(1)} collective-permute-done((bf16[128,1024]{1,0:T(8,128)(2,1)}, bf16[128,1024]{1,0:T(8,128)(2,1)S(1)}, u32[]{:S(2)}, u32[]{:S(2)}) %collective-permute-start.9) | collective-permute-done | bytes 262176 | tf_op jit(solution)/shard_map/ppermute | solution.py:63
  114.9 8.8 %collective-permute-done.12 = bf16[256,1024]{1,0:T(8,128)(2,1)S(1)} collective-permute-done((bf16[256,1024]{1,0:T(8,128)(2,1)S(1)}, bf16[256,1024]{1,0:T(8,128)(2,1)S(1)}, u32[]{:S(2)}, u32[]{:S(2)}) %collective-permute-start.12) | collective-permute-done | bytes 524320 | tf_op jit(solution)/shard_map/ppermute | solution.py:63
  135.4 8.7 %collective-permute-done.14 = bf16[256,1024]{1,0:T(8,128)(2,1)S(1)} collective-permute-done((bf16[256,1024]{1,0:T(8,128)(2,1)}, bf16[256,1024]{1,0:T(8,128)(2,1)S(1)}, u32[]{:S(2)}, u32[]{:S(2)}) %collective-permute-start.14) | collective-permute-done | bytes 524320 | tf_op jit(solution)/shard_map/ppermute | solution.py:63
  145.8 5.5 %collective-permute-start.18 = (bf16[128,1024]{1,0:T(8,128)(2,1)}, bf16[128,1024]{1,0:T(8,128)(2,1)}, u32[]{:S(2)}, u32[]{:S(2)}) collective-permute-start(bf16[128,1024]{1,0:T(8,128)(2,1)} %bitcast.30), channel_id=1, source_target_pairs={{0,0},{1,1},{2,8},{3,9},{4,16},{5,17},{6,24},{7,25},{8,10},{9,11},... | collective-permute-start | bytes 786440 | tf_op jit(solution)/shard_map/ppermute | solution.py:63
  154.5 8.1 %collective-permute-done.15 = bf16[512,1024]{1,0:T(8,128)(2,1)S(1)} collective-permute-done((bf16[512,1024]{1,0:T(8,128)(2,1)S(1)}, bf16[512,1024]{1,0:T(8,128)(2,1)S(1)}, u32[]{:S(2)}, u32[]{:S(2)}) %collective-permute-start.15) | collective-permute-done | bytes 1048608 | tf_op jit(solution)/shard_map/ppermute | solution.py:63
  169.3 5.3 %all-gather.8.cloned.1.call-done.in_ref = bf16[2,2048,512]{2,1,0:T(8,128)(2,1)} async-done(((bf16[2,256,512]{2,1,0:T(8,128)(2,1)}), bf16[2,2048,512]{2,1,0:T(8,128)(2,1)}) %all-gather.8.cloned.1.call-update) | async-done | bytes 4194320 | tf_op jit(solution)/shard_map/all_gather | solution.py:316
  192.5 6.2 %collective-permute-done.23 = bf16[256,1024]{1,0:T(8,128)(2,1)S(1)} collective-permute-done((bf16[256,1024]{1,0:T(8,128)(2,1)S(1)}, bf16[256,1024]{1,0:T(8,128)(2,1)S(1)}, u32[]{:S(2)}, u32[]{:S(2)}) %collective-permute-start.23) | collective-permute-done | bytes 524320 | tf_op jit(solution)/shard_map/ppermute | solution.py:63
  224.7 7.6 %collective-permute-done.29 = bf16[512,1024]{1,0:T(8,128)(2,1)S(1)} collective-permute-done((bf16[512,1024]{1,0:T(8,128)(2,1)S(1)}, bf16[512,1024]{1,0:T(8,128)(2,1)S(1)}, u32[]{:S(2)}, u32[]{:S(2)}) %collective-permute-start.29) | collective-permute-done | bytes 1048608 | tf_op jit(solution)/shard_map/ppermute | solution.py:63
  240.8 7.8 %collective-permute-done.33 = bf16[256,1024]{1,0:T(8,128)(2,1)S(1)} collective-permute-done((bf16[256,1024]{1,0:T(8,128)(2,1)S(1)}, bf16[256,1024]{1,0:T(8,128)(2,1)S(1)}, u32[]{:S(2)}, u32[]{:S(2)}) %collective-permute-start.33) | collective-permute-done | bytes 524320 | tf_op jit(solution)/shard_map/ppermute | solution.py:63
  249.8 5.4 %collective-permute-done.34 = bf16[128,1024]{1,0:T(8,128)(2,1)S(1)} collective-permute-done((bf16[128,1024]{1,0:T(8,128)(2,1)S(1)}, bf16[128,1024]{1,0:T(8,128)(2,1)S(1)}, u32[]{:S(2)}, u32[]{:S(2)}) %collective-permute-start.34) | collective-permute-done | bytes 262176 | tf_op jit(solution)/shard_map/ppermute | solution.py:63
  291.9 6.3 %collective-permute-done.46 = bf16[256,1024]{1,0:T(8,128)(2,1)S(1)} collective-permute-done((bf16[256,1024]{1,0:T(8,128)(2,1)S(1)}, bf16[256,1024]{1,0:T(8,128)(2,1)S(1)}, u32[]{:S(2)}, u32[]{:S(2)}) %collective-permute-start.46) | collective-permute-done | bytes 524320 | tf_op jit(solution)/shard_map/ppermute | solution.py:63
  314.8 6.5 %collective-permute-start.49 = (bf16[256,1024]{1,0:T(8,128)(2,1)S(1)}, bf16[256,1024]{1,0:T(8,128)(2,1)S(1)}, u32[]{:S(2)}, u32[]{:S(2)}) collective-permute-start(bf16[256,1024]{1,0:T(8,128)(2,1)S(1)} %pad_maximum_fusion.16), channel_id=1, source_target_pairs={{0,16},{1,9},{2,18},{3,11},{4,20},{5,13},{6,22},{7,15},{8,24},{9,1... | collective-permute-start | bytes 1572872 | tf_op jit(solution)/shard_map/ppermute | solution.py:63
  323.2 5.3 %collective-permute-done.49 = bf16[256,1024]{1,0:T(8,128)(2,1)S(1)} collective-permute-done((bf16[256,1024]{1,0:T(8,128)(2,1)S(1)}, bf16[256,1024]{1,0:T(8,128)(2,1)S(1)}, u32[]{:S(2)}, u32[]{:S(2)}) %collective-permute-start.49) | collective-permute-done | bytes 524320 | tf_op jit(solution)/shard_map/ppermute | solution.py:63
  368.8 8.3 %collective-permute-done.58 = bf16[256,1024]{1,0:T(8,128)(2,1)S(1)} collective-permute-done((bf16[256,1024]{1,0:T(8,128)(2,1)}, bf16[256,1024]{1,0:T(8,128)(2,1)S(1)}, u32[]{:S(2)}, u32[]{:S(2)}) %collective-permute-start.58) | collective-permute-done | bytes 524320 | tf_op jit(solution)/shard_map/ppermute | solution.py:63
  378.6 6.2 %collective-permute-done.59 = bf16[128,1024]{1,0:T(8,128)(2,1)S(1)} collective-permute-done((bf16[128,1024]{1,0:T(8,128)(2,1)S(1)}, bf16[128,1024]{1,0:T(8,128)(2,1)S(1)}, u32[]{:S(2)}, u32[]{:S(2)}) %collective-permute-start.59) | collective-permute-done | bytes 262176 | tf_op jit(solution)/shard_map/ppermute | solution.py:63
  387.5 13.3 %collective-permute-done.63.refs_1_ = bf16[128,2048]{1,0:T(8,128)(2,1)S(1)} collective-permute-done((bf16[128,2048]{1,0:T(8,128)(2,1)S(1)}, bf16[128,2048]{1,0:T(8,128)(2,1)S(1)}, u32[]{:S(2)}, u32[]{:S(2)}) %collective-permute-start.63) | collective-permute-done | bytes 524320 | tf_op jit(solution)/shard_map/ppermute | solution.py:63
  408.3 7.2 %collective-permute-done.60 = bf16[128,1024]{1,0:T(8,128)(2,1)S(1)} collective-permute-done((bf16[128,1024]{1,0:T(8,128)(2,1)}, bf16[128,1024]{1,0:T(8,128)(2,1)S(1)}, u32[]{:S(2)}, u32[]{:S(2)}) %collective-permute-start.60) | collective-permute-done | bytes 262176 | tf_op jit(solution)/shard_map/ppermute | solution.py:63
  421.6 6.5 %collective-permute-start.61 = (bf16[128,1024]{1,0:T(8,128)(2,1)}, bf16[128,1024]{1,0:T(8,128)(2,1)S(1)}, u32[]{:S(2)}, u32[]{:S(2)}) collective-permute-start(bf16[128,1024]{1,0:T(8,128)(2,1)} %fusion.103), channel_id=1, source_target_pairs={{0,0},{1,1},{2,10},{3,11},{4,20},{5,21},{6,30},{7,31},{8,2},{9,3},... | collective-permute-start | bytes 786440 | tf_op jit(solution)/shard_map/ppermute | solution.py:63
  436.3 5.8 %collective-permute-done.69 = f32[17,128]{1,0:T(8,128)S(1)} collective-permute-done((f32[17,128]{1,0:T(8,128)S(1)}, f32[17,128]{1,0:T(8,128)S(1)}, u32[]{:S(2)}, u32[]{:S(2)}) %collective-permute-start.69) | collective-permute-done | bytes 8736 | tf_op jit(solution)/shard_map/ppermute | solution.py:63
  442.1 10.8 %collective-permute-start.70 = (f32[17,128]{1,0:T(8,128)S(1)}, f32[17,128]{1,0:T(8,128)S(1)}, u32[]{:S(2)}, u32[]{:S(2)}) collective-permute-start(f32[17,128]{1,0:T(8,128)S(1)} %fusion.241), channel_id=1, source_target_pairs={{0,16},{1,17},{2,18},{3,19},{4,20},{5,21},{6,22},{7,23},{8,24},{9,... | collective-permute-start | bytes 26120 | tf_op jit(solution)/shard_map/ppermute | solution.py:63
  462.1 5.6 %collective-permute-done.76.refs_3_ = bf16[128,2048]{1,0:T(8,128)(2,1)S(1)} collective-permute-done((bf16[128,2048]{1,0:T(8,128)(2,1)S(1)}, bf16[128,2048]{1,0:T(8,128)(2,1)S(1)}, u32[]{:S(2)}, u32[]{:S(2)}) %collective-permute-start.76) | collective-permute-done | bytes 524320 | tf_op jit(solution)/shard_map/ppermute | solution.py:63
  (677 shorter events, 278.2 us)
Async XLA Ops:
  7.2 62.3 %all-gather.4.cloned.1.call-start = ((), (), s32[]{:S(2)}) async-start(), calls=%async_computation.2 | async-start | bytes 2949120 | tf_op jit(solution)/shard_map/all_gather | solution.py:297
  7.2 20.4 %collective-permute-start = (bf16[128,1024]{1,0:T(8,128)(2,1)}, bf16[128,1024]{1,0:T(8,128)(2,1)S(1)}, u32[]{:S(2)}, u32[]{:S(2)}) collective-permute-start(bf16[128,1024]{1,0:T(8,128)(2,1)} %bitcast.256), channel_id=1, source_target_pairs={{0,0},{1,1},{2,8},{3,9},{4,16},{5,17},{6,24},{7,25},{8,10},{9,11},... | collective-permute-start | bytes 786440 | tf_op jit(solution)/shard_map/ppermute | solution.py:63
  27.6 97.5 %all-gather.6.cloned.1.call-start = ((), (), s32[]{:S(2)}) async-start(), calls=%async_computation.3 | async-start | bytes 1769472 | tf_op jit(solution)/shard_map/all_gather | solution.py:290
  31.6 143.0 %all-gather.8.cloned.1.call-start = ((), (), s32[]{:S(2)}) async-start(), calls=%async_computation.4 | async-start | bytes 4718592 | tf_op jit(solution)/shard_map/all_gather | solution.py:316
  57.5 249.9 %reduce-scatter.3.cloned.1.call-start = ((), (), s32[]{:S(2)}) async-start(), calls=%async_computation.5 | async-start | bytes 2621440 | tf_op jit(solution)/shard_map/reduce_scatter | solution.py:359
  79.2 32.7 %collective-permute-start.9 = (bf16[128,1024]{1,0:T(8,128)(2,1)}, bf16[128,1024]{1,0:T(8,128)(2,1)S(1)}, u32[]{:S(2)}, u32[]{:S(2)}) collective-permute-start(bf16[128,1024]{1,0:T(8,128)(2,1)} %bitcast.16), channel_id=1, source_target_pairs={{0,0},{1,1},{2,8},{3,9},{4,16},{5,17},{6,24},{7,25},{8,10},{9,11},... | collective-permute-start | bytes 786440 | tf_op jit(solution)/shard_map/ppermute | solution.py:63
  145.0 17.6 %collective-permute-start.15 = (bf16[512,1024]{1,0:T(8,128)(2,1)S(1)}, bf16[512,1024]{1,0:T(8,128)(2,1)S(1)}, u32[]{:S(2)}, u32[]{:S(2)}) collective-permute-start(bf16[512,1024]{1,0:T(8,128)(2,1)S(1)} %pad_maximum_fusion.2), channel_id=1, source_target_pairs={{0,16},{1,9},{2,18},{3,11},{4,20},{5,13},{6,22},{7,15},{8,24},{9,1... | collective-permute-start | bytes 3145736 | tf_op jit(solution)/shard_map/ppermute | solution.py:63
  145.8 34.4 %collective-permute-start.18 = (bf16[128,1024]{1,0:T(8,128)(2,1)}, bf16[128,1024]{1,0:T(8,128)(2,1)}, u32[]{:S(2)}, u32[]{:S(2)}) collective-permute-start(bf16[128,1024]{1,0:T(8,128)(2,1)} %bitcast.30), channel_id=1, source_target_pairs={{0,0},{1,1},{2,8},{3,9},{4,16},{5,17},{6,24},{7,25},{8,10},{9,11},... | collective-permute-start | bytes 786440 | tf_op jit(solution)/shard_map/ppermute | solution.py:63
  151.5 16.1 %collective-permute-start.16 = (bf16[256,1024]{1,0:T(8,128)(2,1)S(1)}, bf16[256,1024]{1,0:T(8,128)(2,1)S(1)}, u32[]{:S(2)}, u32[]{:S(2)}) collective-permute-start(bf16[256,1024]{1,0:T(8,128)(2,1)S(1)} %pad_maximum_fusion.8), channel_id=1, source_target_pairs={{0,1},{1,0},{2,3},{3,2},{4,5},{5,4},{6,7},{7,6},{8,9},{9,8},{10,11... | collective-permute-start | bytes 1572872 | tf_op jit(solution)/shard_map/ppermute | solution.py:63
  217.4 14.9 %collective-permute-start.29 = (bf16[512,1024]{1,0:T(8,128)(2,1)S(1)}, bf16[512,1024]{1,0:T(8,128)(2,1)S(1)}, u32[]{:S(2)}, u32[]{:S(2)}) collective-permute-start(bf16[512,1024]{1,0:T(8,128)(2,1)S(1)} %pad_maximum_fusion.3), channel_id=1, source_target_pairs={{0,16},{1,9},{2,18},{3,11},{4,20},{5,13},{6,22},{7,15},{8,24},{9,1... | collective-permute-start | bytes 3145736 | tf_op jit(solution)/shard_map/ppermute | solution.py:63
  224.6 16.1 %collective-permute-start.28 = (bf16[256,1024]{1,0:T(8,128)(2,1)S(1)}, bf16[256,1024]{1,0:T(8,128)(2,1)S(1)}, u32[]{:S(2)}, u32[]{:S(2)}) collective-permute-start(bf16[256,1024]{1,0:T(8,128)(2,1)S(1)} %convolution_convert_fusion.9), channel_id=1, source_target_pairs={{0,1},{1,0},{2,3},{3,2},{4,5},{5,4},{6,7},{7,6},{8,9},{9,8},{10,11... | collective-permute-start | bytes 1572872 | tf_op jit(solution)/shard_map/ppermute | solution.py:63
  260.5 167.8 %reduce-scatter.5.cloned.1.call-start = ((), (), s32[]{:S(2)}) async-start(), calls=%async_computation.6 | async-start | bytes 2621440 | tf_op jit(solution)/shard_map/reduce_scatter | solution.py:359
  269.7 14.4 %collective-permute-start.36 = (bf16[256,1024]{1,0:T(8,128)(2,1)S(1)}, bf16[256,1024]{1,0:T(8,128)(2,1)S(1)}, u32[]{:S(2)}, u32[]{:S(2)}) collective-permute-start(bf16[256,1024]{1,0:T(8,128)(2,1)S(1)} %convolution_convert_fusion.7), channel_id=1, source_target_pairs={{0,1},{1,0},{2,3},{3,2},{4,5},{5,4},{6,7},{7,6},{8,9},{9,8},{10,11... | collective-permute-start | bytes 1572872 | tf_op jit(solution)/shard_map/ppermute | solution.py:63
  284.3 16.2 %collective-permute-start.39 = (bf16[128,1024]{1,0:T(8,128)(2,1)S(1)}, bf16[128,1024]{1,0:T(8,128)(2,1)S(1)}, u32[]{:S(2)}, u32[]{:S(2)}) collective-permute-start(bf16[128,1024]{1,0:T(8,128)(2,1)S(1)} %slice.1047), channel_id=1, source_target_pairs={{0,8},{1,17},{2,10},{3,19},{4,12},{5,21},{6,14},{7,23},{8,0},{9,25... | collective-permute-start | bytes 786440 | tf_op jit(solution)/shard_map/ppermute | solution.py:63
  311.4 38.7 %collective-permute-start.40 = (bf16[128,1024]{1,0:T(8,128)(2,1)S(1)}, bf16[128,1024]{1,0:T(8,128)(2,1)S(1)}, u32[]{:S(2)}, u32[]{:S(2)}) collective-permute-start(bf16[128,1024]{1,0:T(8,128)(2,1)S(1)} %copy-done.69), channel_id=1, source_target_pairs={{0,0},{1,1},{2,10},{3,11},{4,20},{5,21},{6,30},{7,31},{8,2},{9,3},... | collective-permute-start | bytes 786440 | tf_op jit(solution)/shard_map/ppermute | solution.py:63
  334.4 15.0 %collective-permute-start.55 = (bf16[128,1024]{1,0:T(8,128)(2,1)S(1)}, bf16[128,1024]{1,0:T(8,128)(2,1)S(1)}, u32[]{:S(2)}, u32[]{:S(2)}) collective-permute-start(bf16[128,1024]{1,0:T(8,128)(2,1)S(1)} %slice.1045), channel_id=1, source_target_pairs={{0,8},{1,17},{2,10},{3,19},{4,12},{5,21},{6,14},{7,23},{8,0},{9,25... | collective-permute-start | bytes 786440 | tf_op jit(solution)/shard_map/ppermute | solution.py:63
  352.7 16.1 %collective-permute-start.56 = (bf16[256,1024]{1,0:T(8,128)(2,1)}, bf16[256,1024]{1,0:T(8,128)(2,1)}, u32[]{:S(2)}, u32[]{:S(2)}) collective-permute-start(bf16[256,1024]{1,0:T(8,128)(2,1)} %convolution_convert_fusion.3), channel_id=1, source_target_pairs={{0,1},{1,0},{2,3},{3,2},{4,5},{5,4},{6,7},{7,6},{8,9},{9,8},{10,11... | collective-permute-start | bytes 1572872 | tf_op jit(solution)/shard_map/ppermute | solution.py:63
  386.7 14.1 %collective-permute-start.63 = (bf16[128,2048]{1,0:T(8,128)(2,1)S(1)}, bf16[128,2048]{1,0:T(8,128)(2,1)S(1)}, u32[]{:S(2)}, u32[]{:S(2)}) collective-permute-start(bf16[128,2048]{1,0:T(8,128)(2,1)S(1)} %pad_maximum_fusion.18.refs_0_), channel_id=1, source_target_pairs={{0,8},{1,17},{2,10},{3,19},{4,12},{5,21},{6,14},{7,23},{8,0},{9,25... | collective-permute-start | bytes 1572872 | tf_op jit(solution)/shard_map/ppermute | solution.py:63
  386.7 28.8 %collective-permute-start.64 = (bf16[128,2048]{1,0:T(8,128)(2,1)S(1)}, bf16[128,2048]{1,0:T(8,128)(2,1)S(1)}, u32[]{:S(2)}, u32[]{:S(2)}) collective-permute-start(bf16[128,2048]{1,0:T(8,128)(2,1)S(1)} %pad_maximum_fusion.18.refs_0_), channel_id=1, source_target_pairs={{0,16},{1,9},{2,18},{3,11},{4,20},{5,13},{6,22},{7,15},{8,24},{9,1... | collective-permute-start | bytes 1572872 | tf_op jit(solution)/shard_map/ppermute | solution.py:63
  400.8 14.7 %collective-permute-start.65 = (bf16[128,2048]{1,0:T(8,128)(2,1)S(1)}, bf16[128,2048]{1,0:T(8,128)(2,1)S(1)}, u32[]{:S(2)}, u32[]{:S(2)}) collective-permute-start(bf16[128,2048]{1,0:T(8,128)(2,1)S(1)} %collective-permute-done.63.refs_1_), channel_id=1, source_target_pairs={{0,16},{1,9},{2,18},{3,11},{4,20},{5,13},{6,22},{7,15},{8,24},{9,1... | collective-permute-start | bytes 1572872 | tf_op jit(solution)/shard_map/ppermute | solution.py:63
  421.6 33.4 %collective-permute-start.61 = (bf16[128,1024]{1,0:T(8,128)(2,1)}, bf16[128,1024]{1,0:T(8,128)(2,1)S(1)}, u32[]{:S(2)}, u32[]{:S(2)}) collective-permute-start(bf16[128,1024]{1,0:T(8,128)(2,1)} %fusion.103), channel_id=1, source_target_pairs={{0,0},{1,1},{2,10},{3,11},{4,20},{5,21},{6,30},{7,31},{8,2},{9,3},... | collective-permute-start | bytes 786440 | tf_op jit(solution)/shard_map/ppermute | solution.py:63
  430.9 22.1 %collective-permute-start.74 = (bf16[128,2048]{1,0:T(8,128)(2,1)S(1)}, bf16[128,2048]{1,0:T(8,128)(2,1)S(1)}, u32[]{:S(2)}, u32[]{:S(2)}) collective-permute-start(bf16[128,2048]{1,0:T(8,128)(2,1)S(1)} %pad_maximum_fusion.20.refs_0_), channel_id=1, source_target_pairs={{0,8},{1,17},{2,10},{3,19},{4,12},{5,21},{6,14},{7,23},{8,0},{9,25... | collective-permute-start | bytes 1572872 | tf_op jit(solution)/shard_map/ppermute | solution.py:63
  442.1 16.6 %collective-permute-start.70 = (f32[17,128]{1,0:T(8,128)S(1)}, f32[17,128]{1,0:T(8,128)S(1)}, u32[]{:S(2)}, u32[]{:S(2)}) collective-permute-start(f32[17,128]{1,0:T(8,128)S(1)} %fusion.241), channel_id=1, source_target_pairs={{0,16},{1,17},{2,18},{3,19},{4,20},{5,21},{6,22},{7,23},{8,24},{9,... | collective-permute-start | bytes 26120 | tf_op jit(solution)/shard_map/ppermute | solution.py:63
  453.0 14.8 %collective-permute-start.76 = (bf16[128,2048]{1,0:T(8,128)(2,1)S(1)}, bf16[128,2048]{1,0:T(8,128)(2,1)S(1)}, u32[]{:S(2)}, u32[]{:S(2)}) collective-permute-start(bf16[128,2048]{1,0:T(8,128)(2,1)S(1)} %collective-permute-done.74.refs_1_), channel_id=1, source_target_pairs={{0,16},{1,9},{2,18},{3,11},{4,20},{5,13},{6,22},{7,15},{8,24},{9,1... | collective-permute-start | bytes 1572872 | tf_op jit(solution)/shard_map/ppermute | solution.py:63
  (178 other events, 1391.3 us)
Sparse Core Ops, SparseCore 0:
  27.8 41.6 all-gather.3
  71.6 42.7 all-gather.5
  116.6 57.8 all-gather.7
  260.6 46.7 reduce-scatter.2
  365.4 43.9 reduce-scatter.4
